TPU v7x, 32 devices: a whole 2x2x4 slice. The times are simulated.
32 devices in a mesh: stream: 2 (over core), dp: 16 (over z, y, x).
Axes of the slice: x: 2, y: 2, z: 4, core: 2. Of those that a mesh axis runs over, the one named last changes fastest.
Arguments:
- layer_input: bfloat16 [2, 16384, 768], P('stream', 'dp'), may hold values from -6 to 6
- pair_group: int32 [256], P('dp'), may hold values from 0 to 108, as said below
- query_weight: bfloat16 [768, 768], replicated, may hold values from -0.21875 to 0.21875
- query_bias: float32 [768], replicated, may hold values from -4 to 4
- key_weight: bfloat16 [768, 768], replicated, may hold values from -0.21875 to 0.21875
- value_weight: bfloat16 [768, 768], replicated, may hold values from -0.21875 to 0.21875
- value_bias: float32 [768], replicated, may hold values from -4 to 4
- out_weight: bfloat16 [768, 768], replicated, may hold values from -1 to 1
- out_bias: float32 [768], replicated, may hold values from -4 to 4
- mixer_gain: float32 [768], replicated, may hold values from 0.1 to 1.9
- mixer_shift: float32 [768], replicated, may hold values from -4 to 4
- up_weight: bfloat16 [768, 3072], replicated, may hold values from -0.21875 to 0.21875
- up_bias: float32 [3072], replicated, may hold values from -4 to 4
- down_weight: bfloat16 [3072, 768], replicated, may hold values from -0.109375 to 0.109375
- down_bias: float32 [768], replicated, may hold values from -4 to 4
- final_gain: float32 [768], replicated, may hold values from 0.1 to 1.9
- final_shift: float32 [768], replicated, may hold values from -4 to 4
- upstream: bfloat16 [2, 16384, 768], P('stream', 'dp'), may hold values from -0.75 to 0.75
Outputs:
- layer_output: bfloat16 [2, 16384, 768], P('stream', 'dp')
- input_grad: float32 [2, 16384, 768], P('stream', 'dp')
- total_loss: float32 [2, 256], P('stream', 'dp')
- query_weight_grad: float32 [768, 768], replicated
- query_bias_grad: float32 [768], replicated
- key_weight_grad: float32 [768, 768], replicated
- value_weight_grad: float32 [768, 768], replicated
- value_bias_grad: float32 [768], replicated
- out_weight_grad: float32 [768, 768], replicated
- out_bias_grad: float32 [768], replicated
- mixer_gain_grad: float32 [768], replicated
- mixer_shift_grad: float32 [768], replicated
- up_weight_grad: float32 [768, 3072], replicated
- up_bias_grad: float32 [3072], replicated
- down_weight_grad: float32 [3072, 768], replicated
- down_bias_grad: float32 [768], replicated
- final_gain_grad: float32 [768], replicated
- final_shift_grad: float32 [768], replicated
Inputs may be any that keep to these rules, and one draw needn't show every extreme that they name: `pair_group`: every one of the 109 ids names 2 or more pairs; the first and the last pair have the same id.
All inputs are finite; a program needn't handle non-finite values.
Results may differ from a plain program's by a relative error of at most 0.014.
Values may be sent and summed in bfloat16 or wider, within the bound.
No kernel may reach another device: no remote copies, remote signals or barrier semaphores. Data moves between devices by JAX's collectives and lax.ppermute only.
A program may use at most 256 MiB of HBM per device.

v0:
```python
import functools
import math

import jax
import jax.numpy as jnp
from jax import lax
from jax.experimental import pallas as pl
from jax.experimental.pallas import tpu as pltpu
from jax.sharding import PartitionSpec as P

D = 768
HEADS = 12
HD = 64
GROUPS = 109
LANES = 128

MARGIN = 0.3
LOGIT_SCALE = 30.0
NORM_EPS = 1e-12
UNIT_EPS = 1e-06
highest = lax.Precision.HIGHEST
low = jnp.bfloat16
full = jnp.float32


def dot(left, right):
    return lax.dot_general(left, right, (((1,), (0,)), ((), ())), preferred_element_type=full)


def dot_t(left, right):
    return lax.dot_general(left, right, (((1,), (1,)), ((), ())), preferred_element_type=full)


def t_dot(left, right):
    return lax.dot_general(left, right, (((0,), (0,)), ((), ())), preferred_element_type=full)


def mean_of(values):
    return jnp.sum(values, axis=-1, keepdims=True) * (1.0 / D)


def norm_stats(values):
    centred = values - mean_of(values)
    inv_std = lax.rsqrt(mean_of(centred * centred) + NORM_EPS)
    return centred * inv_std, inv_std


def norm_back(grad_hat, normed_hat, inv_std):
    return inv_std * (grad_hat - mean_of(grad_hat) - normed_hat * mean_of(grad_hat * normed_hat))


def normal_cdf(values):
    bell = jnp.exp(-0.5 * values * values)
    step = 1.0 / (1.0 + (0.3275911 / math.sqrt(2.0)) * jnp.abs(values))
    tail = 0.5 * 1.061405429
    for factor in (-1.453152027, 1.421413741, -0.284496736, 0.254829592):
        tail = tail * step + 0.5 * factor
    tail = tail * step * bell
    return jnp.where(values >= 0.0, 1.0 - tail, tail), bell


def gelu_and_slope(values):
    cdf, bell = normal_cdf(values)
    return values * cdf, cdf + values * bell * (1.0 / math.sqrt(2.0 * math.pi))


def columns_sum(values):
    return jnp.sum(values, axis=0, keepdims=True)


def line(ref, first=0):
    return jnp.concatenate([ref[pl.ds(first + k, 1), :] for k in range(D // LANES)], axis=1)


def fixed_spec(*shape):
    return pl.BlockSpec(shape, lambda *_: (0,) * len(shape))


def vector_spec(count=D):
    return fixed_spec(count // LANES, LANES)


def shape_of(*shape, dtype=low):
    return jax.ShapeDtypeStruct(shape, dtype)


def far(*shape, dtype=low):
    return pltpu.HBM(shape, dtype)


def params(grid_dims, mib=20):
    return pltpu.CompilerParams(dimension_semantics=("arbitrary",) * grid_dims, vmem_limit_bytes=mib << 20)


def cost(micros):
    return pl.CostEstimate(flops=int(micros * 3.0 * 1.15e9), bytes_accessed=1000, transcendentals=0)


def two_heads(block):
    lane = lax.broadcasted_iota(jnp.int32, block.shape, 1)
    zero = jnp.zeros_like(block)
    return jnp.concatenate([jnp.where(lane < HD, block, zero), jnp.where(lane < HD, zero, block)], axis=0)


def own_head(both):
    count = both.shape[0] // 2
    lane = lax.broadcasted_iota(jnp.int32, (count, both.shape[1]), 1)
    return jnp.where(lane < HD, both[:count], both[count:])


def cells_of(count, seq_len):
    return [
        (slice(start, start + seq_len), slice(first, first + 2 * HD))
        for first in range(0, D, 2 * HD)
        for start in range(0, count, seq_len)
    ]


def joined(pieces, count, seq_len):
    tall = count // seq_len
    columns = [jnp.concatenate(pieces[k : k + tall], axis=0) for k in range(0, len(pieces), tall)]
    return jnp.concatenate(columns, axis=1)


def attention_kernel(seq_len, x_ref, wq, wk, wv, wo, bq, bv, bo, gain, shift,
                     q_ref, k_ref, v_ref, p_ref, c_ref, nl_ref, hat_ref, inv_ref, nll_ref, hatl_ref):
    x = x_ref[...]
    count = x.shape[0]
    q = (dot(x, wq[...]) + line(bq)).astype(low)
    k = dot(x, wk[...]).astype(low)
    v = (dot(x, wv[...]) + line(bv)).astype(low)
    q_ref[...], k_ref[...], v_ref[...] = q, k, v
    cells = cells_of(count, seq_len)
    factor = 1.0 / math.sqrt(HD)
    scores = [dot_t(k[cell], two_heads(q[cell])) * factor for cell in cells]
    probs = []
    for cell, score in zip(cells, scores, strict=True):
        terms = jnp.exp(score - jnp.max(score, axis=0, keepdims=True))
        probs.append((terms * (1.0 / columns_sum(terms))).astype(low))
        p_ref[cell] = probs[-1]
    pieces = [own_head(t_dot(prob, v[cell])).astype(low) for cell, prob in zip(cells, probs, strict=True)]
    context = joined(pieces, count, seq_len)
    c_ref[...] = context
    hat, inv_std = norm_stats(x.astype(full) + dot(context, wo[...]) + line(bo))
    normed_low = (hat * line(gain) + line(shift)).astype(low)
    hat_ref[...] = hat
    inv_ref[...] = jnp.broadcast_to(inv_std, inv_ref.shape)
    nl_ref[...] = normed_low
    for s in range(count // seq_len):
        nll_ref[0, s : s + 1, :] = normed_low[s * seq_len : s * seq_len + 1, :].astype(full)
        hatl_ref[0, s : s + 1, :] = hat[s * seq_len : s * seq_len + 1, :]


def attention_forward(tokens, seq_len, wq, wk, wv, wo, *vectors):
    count = tokens.shape[0]
    rows = 256
    steps, leads = count // rows, rows // seq_len
    row, mat = pl.BlockSpec((rows, D), lambda i: (i, 0)), fixed_spec(D, D)
    lead = pl.BlockSpec((1, leads, D), lambda i: (i, 0, 0))
    return pl.pallas_call(
        functools.partial(attention_kernel, seq_len),
        grid=(steps,),
        in_specs=[row, mat, mat, mat, mat] + [vector_spec()] * 5,
        out_specs=[row] * 7 + [pl.BlockSpec((rows, LANES), lambda i: (i, 0)), lead, lead],
        out_shape=[far(count, D)] * 5
        + [far(count, D), far(count, D, dtype=full), far(count, LANES, dtype=full)]
        + [shape_of(steps, leads, D, dtype=full)] * 2,
        compiler_params=params(1, 20),
        name="attention_forward",
        cost_estimate=cost(10),
    )(tokens, wq, wk, wv, wo, *vectors)


def lead_kernel(nl_ref, hat_ref, uw, ub, dw, gain1, shift1, db, gain2, shift2,
                lead_ref, hat2_ref, inv2_ref, linv_ref, unit_ref, nl, acc):
    step = pl.program_id(0)

    @pl.when(step == 0)
    def _():
        hat = jnp.concatenate([hat_ref[k] for k in range(hat_ref.shape[0])], axis=0)
        nl[...] = jnp.concatenate([nl_ref[k] for k in range(nl_ref.shape[0])], axis=0).astype(low)
        acc[...] = hat * line(gain1) + line(shift1) + line(db)

    pre = dot(nl[...], uw[...]) + line(ub, step * (D // LANES))
    acc[...] += dot(gelu_and_slope(pre)[0].astype(low), dw[...])

    @pl.when(step == pl.num_programs(0) - 1)
    def _():
        hat, inv_std = norm_stats(acc[...])
        lead = hat * line(gain2) + line(shift2)
        lead_inv = lax.rsqrt(jnp.sum(lead * lead, axis=-1, keepdims=True) + UNIT_EPS)
        lead_ref[...] = lead
        hat2_ref[...] = hat
        inv2_ref[...] = jnp.broadcast_to(inv_std, inv2_ref.shape)
        linv_ref[...] = jnp.broadcast_to(lead_inv, linv_ref.shape)
        unit_ref[...] = (lead * lead_inv).astype(low)


def lead_forward(nl, hat, uw, ub, dw, *vectors):
    count = nl.shape[0] * nl.shape[1]
    hidden = uw.shape[1]
    row, lane = fixed_spec(count, D), fixed_spec(count, LANES)
    return pl.pallas_call(
        lead_kernel,
        grid=(hidden // D,),
        in_specs=[
            fixed_spec(*nl.shape), fixed_spec(*hat.shape),
            pl.BlockSpec((D, D), lambda j: (0, j)), vector_spec(hidden), pl.BlockSpec((D, D), lambda j: (j, 0)),
        ] + [vector_spec()] * 5,
        out_specs=[row, row, lane, lane, row],
        out_shape=[shape_of(count, D, dtype=full)] * 2
        + [shape_of(count, LANES, dtype=full)] * 2 + [shape_of(count, D)],
        scratch_shapes=[pltpu.VMEM((count, D), low), pltpu.VMEM((count, D), full)],
        compiler_params=params(1),
        name="lead_forward",
        cost_estimate=cost(3),
    )(nl, hat, uw, ub, dw, *vectors)


def ff_kernel(part, seq_len, nl_ref, uw, ub, dw, gain1, shift1, db, gain2, shift2, hat_far, up_far, *rest):
    out_ref, act_ref, slope_ref, dr2_ref, low_ref, sums_ref, leads_ref, acc, hat_ref, up_ref, sems = rest[-11:]
    step = pl.program_id(0)
    rows = acc.shape[0]
    span = pl.ds(part * rows, rows)
    copies = [
        pltpu.make_async_copy(source.at[span, :], target, sems.at[k])
        for k, (source, target) in enumerate(((hat_far, hat_ref), (up_far, up_ref)))
    ]

    @pl.when(step == 0)
    def _():
        for copy in copies:
            copy.start()
        acc[...] = jnp.zeros_like(acc)

    value, slope = gelu_and_slope(dot(nl_ref[...], uw[...]) + line(ub, step * (D // LANES)))
    act = value.astype(low)
    slope_ref[...] = slope.astype(low)
    act_ref[...] = act
    acc[...] += dot(act, dw[...])

    @pl.when(step == pl.num_programs(0) - 1)
    def _():
        for copy in copies:
            copy.wait()
        normed = hat_ref[...] * line(gain1) + line(shift1)
        hat, inv_std = norm_stats(acc[...] + (normed + line(db)))
        gain = line(gain2)
        out_ref[...] = (hat * gain + line(shift2)).astype(low)
        grad = up_ref[...].astype(full)
        dr2 = norm_back(grad * gain, hat, inv_std)
        dr2_ref[...] = dr2
        branch = dr2.astype(low)
        low_ref[...] = branch
        sums_ref[0, 0:1, :] = columns_sum(grad * hat)
        sums_ref[0, 1:2, :] = columns_sum(grad)
        sums_ref[0, 2:3, :] = columns_sum(branch.astype(full))
        for s in range(rows // seq_len):
            leads_ref[0, s : s + 1, :] = dr2[s * seq_len : s * seq_len + 1, :]


def ff_forward(part, parts, carried, seq_len, nl, hat, upstream, uw, ub, dw, *vectors):
    count = nl.shape[0]
    rows = count // parts
    hidden = uw.shape[1]
    row = pl.BlockSpec((rows, D), lambda j: (part, 0))
    wide = pl.BlockSpec((rows, D), lambda j: (part, j))
    anywhere = pl.BlockSpec(memory_space=pl.ANY)
    operands = [in_far(nl), uw, ub, dw, *vectors, in_far(hat), upstream]
    in_specs = [row, pl.BlockSpec((D, D), lambda j: (0, j)), vector_spec(hidden), pl.BlockSpec((D, D), lambda j: (j, 0))]
    in_specs += [vector_spec()] * 5 + [anywhere] * 2
    aliases = {}
    if carried is not None:
        aliases = {len(operands) + k: k for k in range(len(carried))}
        operands += list(carried)
        in_specs += [anywhere] * len(carried)
    sums = lambda tall: pl.BlockSpec((1, tall, D), lambda j: (part, 0, 0))
    return pl.pallas_call(
        functools.partial(ff_kernel, part, seq_len),
        grid=(hidden // D,),
        in_specs=in_specs,
        out_specs=[row, wide, wide, row, row, sums(8), sums(rows // seq_len)],
        scratch_shapes=[
            pltpu.VMEM((rows, D), full), pltpu.VMEM((rows, D), full), pltpu.VMEM((rows, D), low),
            pltpu.SemaphoreType.DMA((2,)),
        ],
        out_shape=[
            far(count, D), far(count, hidden), far(count, hidden),
            far(count, D, dtype=full), far(count, D), shape_of(parts, 8, D, dtype=full),
            shape_of(parts, rows // seq_len, D, dtype=full),
        ],
        input_output_aliases=aliases,
        compiler_params=params(1, 20),
        name=f"ff_forward_{part}",
        cost_estimate=cost(13),
    )(*operands)


def loss_kernel(seq_count, own_ref, other_ref, lead_ref, hat_ref, inv_ref, linv_ref, gain2, loss_ref, fix_ref, sums_ref):
    count = own_ref.shape[0]
    own, other = own_ref[:, :D], other_ref[:, :D]
    columns = own_ref[:, D : D + 1].astype(full)
    rows = dot_t(jnp.ones((8, LANES), low), own_ref[:, D:])[0:1] * (1.0 / LANES)
    same = columns == rows
    place = [lax.broadcasted_iota(jnp.int32, (count, count), axis) for axis in range(2)]
    diagonal = (place[0] == place[1]).astype(full)
    logits = LOGIT_SCALE * dot_t(own, other) - LOGIT_SCALE * MARGIN * diagonal
    masked = jnp.where(same, logits, -jnp.inf)
    col_top = jnp.max(masked, axis=0, keepdims=True)
    col_lse = col_top + jnp.log(columns_sum(jnp.exp(masked - col_top)))
    mine = masked[:seq_count]
    row_top = jnp.max(mine, axis=1, keepdims=True)
    row_lse = row_top + jnp.log(jnp.sum(jnp.exp(mine - row_top), axis=1, keepdims=True))
    mine_diag = diagonal[:seq_count]
    own_logit = jnp.sum(logits[:seq_count] * mine_diag, axis=1, keepdims=True)
    found = same.astype(full)
    row_weight = (count / GROUPS) / jnp.sum(found[:seq_count], axis=1, keepdims=True)
    col_weight = (count / GROUPS) / columns_sum(found)
    loss_ref[...] = jnp.broadcast_to(row_weight * (row_lse - own_logit), loss_ref.shape)
    dsims = row_weight * (jnp.exp(mine - row_lse) - mine_diag) + col_weight * (jnp.exp(mine - col_lse) - mine_diag)
    high = dsims.astype(low)
    rest = (dsims - high.astype(full)).astype(low)
    unit_grad = LOGIT_SCALE * (dot(high, other) + dot(rest, other))
    lead, lead_inv, hat = lead_ref[...], linv_ref[:, 0:1], hat_ref[...]
    cross = jnp.sum(lead * unit_grad, axis=-1, keepdims=True)
    lead_grad = lead_inv * unit_grad - lead_inv * lead_inv * lead_inv * cross * lead
    fix_ref[...] = norm_back(lead_grad * line(gain2), hat, inv_ref[:, 0:1])
    sums_ref[0:1, :] = columns_sum(lead_grad * hat)
    sums_ref[1:2, :] = columns_sum(lead_grad)


def pair_loss(own_side, other_side, lead, lead_hat, inv2, lead_inv, gain):
    seq_count = lead.shape[0]
    if own_side.shape[0] <= 512:
        loss, fix, sums = pl.pallas_call(
            functools.partial(loss_kernel, seq_count),
            out_shape=[
                shape_of(seq_count, LANES, dtype=full), shape_of(seq_count, D, dtype=full), shape_of(8, D, dtype=full)
            ],
            compiler_params=params(0),
            name="pair_loss",
            cost_estimate=cost(4),
        )(own_side, other_side, lead, lead_hat, inv2, lead_inv, in_far(gain.reshape(-1, LANES)))
        return loss[:, 0][None], fix, sums
    pairs_all = own_side.shape[0]
    groups = own_side[:, D].astype(full)
    same_group = groups[:, None] == groups[None, :]
    row_weight = pairs_all / GROUPS / jnp.sum(same_group.astype(full), axis=1)
    sim_scores = LOGIT_SCALE * jnp.einsum("id,jd->ij", own_side[:, :D], other_side[:, :D], preferred_element_type=full)
    place = jnp.arange(pairs_all, dtype=jnp.int32)
    diagonal = (place[:, None] == place[None, :]).astype(full)
    logits = sim_scores - LOGIT_SCALE * MARGIN * diagonal
    masked = jnp.where(same_group, logits, -jnp.inf)
    col_top = jnp.max(masked, axis=0, keepdims=True)
    col_lse = col_top + jnp.log(jnp.sum(jnp.exp(masked - col_top), axis=0, keepdims=True))
    own = masked[:seq_count]
    row_top = jnp.max(own, axis=1, keepdims=True)
    row_lse = row_top + jnp.log(jnp.sum(jnp.exp(own - row_top), axis=1, keepdims=True))
    own_diag = diagonal[:seq_count]
    own_logit = jnp.sum(logits[:seq_count] * own_diag, axis=1)
    loss_rows = (row_weight[:seq_count] * (row_lse[:, 0] - own_logit))[None]
    dsims = row_weight[:seq_count, None] * (jnp.exp(own - row_lse) - own_diag)
    dsims += row_weight[None, :] * (jnp.exp(own - col_lse) - own_diag)
    unit_grad = LOGIT_SCALE * jnp.dot(dsims, other_side[:, :D].astype(full), precision=highest)
    lead_inv = lead_inv[:, :1]
    cross = jnp.sum(lead * unit_grad, axis=-1, keepdims=True)
    lead_grad = lead_inv * unit_grad - lead_inv * lead_inv * lead_inv * cross * lead
    sums = jnp.stack([jnp.sum(lead_grad * lead_hat, axis=0), jnp.sum(lead_grad, axis=0)])
    return loss_rows, norm_back(lead_grad * gain[None], lead_hat, inv2[:, :1]), sums


def down_grad_kernel(seq_len, fresh, place, *refs):
    step = pl.program_id(0)
    if fresh:
        old_ref, leads_ref, fix_ref, act_ref, *outs, db_ref, sum_ref = refs

        @pl.when(step == 0)
        def _():
            db_ref[...] = old_ref[...]
            fixed = (leads_ref[...] + fix_ref[...]).astype(low)
            sum_ref[...] = columns_sum(fixed.astype(full) - leads_ref[...].astype(low).astype(full))
            for s in range(fix_ref.shape[0]):
                block = old_ref[s * seq_len : s * seq_len + 16, :]
                first = lax.broadcasted_iota(jnp.int32, block.shape, 0) == 0
                block = jnp.where(first, fixed[s : s + 1, :].astype(full), block.astype(full))
                db_ref[s * seq_len : s * seq_len + 16, :] = block.astype(low)
    else:
        db_ref, act_ref, *outs = refs
    grad = t_dot(act_ref[...], db_ref[...]).astype(low)
    tall = grad.shape[0]
    for rank in range(4):

        @pl.when(step == rank)
        def _(rank=rank):
            outs[rank // 2][rank % 2 * tall : (rank % 2 + 1) * tall, :] = grad


def down_gradient(place, first, act, dbranch, leads=None, fix=None, seq_len=None):
    count, hidden = act.shape
    tall = hidden // 8
    fresh = fix is not None
    operands = [dbranch] + ([leads, fix] if fresh else []) + [in_far(act)]
    moving = pl.BlockSpec((count, tall), lambda p, place: (0, place[first + p]))
    in_specs = [fixed_spec(*operand.shape) for operand in operands[:-1]] + [moving]
    out_specs = [fixed_spec(2 * tall, D)] * 2
    out_shape = [shape_of(2 * tall, D)] * 2
    if fresh:
        out_specs += [fixed_spec(count, D), fixed_spec(1, D)]
        out_shape += [shape_of(count, D), shape_of(1, D, dtype=full)]
    return pl.pallas_call(
        functools.partial(down_grad_kernel, seq_len, fresh),
        grid_spec=pltpu.PrefetchScalarGridSpec(
            num_scalar_prefetch=1, grid=(4,), in_specs=in_specs, out_specs=out_specs
        ),
        out_shape=out_shape,
        compiler_params=params(1),
        name=f"down_grad_{first}",
        cost_estimate=cost(4),
    )(place, *operands)


def put_rows(place, grad_ref, outs, columns):
    tall = grad_ref.shape[0] // 8
    for rank in range(8):
        at = pl.multiple_of(place[rank] * tall, 16)
        outs[rank // 2][rank % 2 * tall : (rank % 2 + 1) * tall, columns] = grad_ref[pl.ds(at, tall), :]


def hidden_kernel(place, db_ref, slope_ref, dw, nl_ref, *rest):
    dpre_ref, sum_ref, *outs, scratch = rest[-7:]
    dpre = (dot_t(db_ref[...], dw[...]) * slope_ref[...].astype(full)).astype(low)
    dpre_ref[...] = dpre
    sum_ref[0:1, :] = columns_sum(dpre.astype(full))
    scratch[...] = t_dot(nl_ref[...], dpre).astype(low)
    put_rows(place, scratch, outs, slice(None))


def hidden_gradient(place, part, parts, carried, dbranch, slope, dw, nl):
    count, hidden = slope.shape
    steps = hidden // D // parts
    wide = pl.BlockSpec((count, D), lambda j, *_: (0, part * steps + j))
    pair = D // 4
    operands = [dbranch, in_far(slope), dw, in_far(nl)]
    in_specs = [
        fixed_spec(count, D), wide, pl.BlockSpec((D, D), lambda j, *_: (part * steps + j, 0)), fixed_spec(count, D)
    ]
    aliases = {2: 0}
    if carried is not None:
        operands[1] = in_far(carried[0])
        aliases |= {5 + k: 1 + k for k in range(5)}
        operands += list(carried[1:])
        in_specs += [pl.BlockSpec(memory_space=pl.ANY)] * 5
    out_specs = [wide] + [
        pl.BlockSpec((rows, D), lambda j, *_: (0, part * steps + j)) for rows in (8, pair, pair, pair, pair)
    ]
    return pl.pallas_call(
        hidden_kernel,
        grid_spec=pltpu.PrefetchScalarGridSpec(
            num_scalar_prefetch=1,
            grid=(steps,),
            in_specs=in_specs,
            out_specs=out_specs,
            scratch_shapes=[pltpu.VMEM((D, D), low)],
        ),
        out_shape=[far(count, hidden), shape_of(8, hidden, dtype=full)] + [shape_of(pair, hidden)] * 4,
        input_output_aliases=aliases,
        compiler_params=params(1, 18),
        name=f"hidden_gradient_{part}",
        cost_estimate=cost(8),
    )(place, *operands)


def norm_one_kernel(seq_len, dpre_ref, fix_ref, uw, wo, gain1, dr2_far, hat_far, inv_ref,
                    dr1_ref, datt_ref, dctx_ref, sums_ref, acc, dr2_ref, hat_ref, sems):
    step = pl.program_id(0)
    copies = [
        pltpu.make_async_copy(source, target, sems.at[k])
        for k, (source, target) in enumerate(((dr2_far, dr2_ref), (hat_far, hat_ref)))
    ]

    @pl.when(step == 0)
    def _():
        for copy in copies:
            copy.start()
        acc[...] = jnp.zeros_like(acc)

    acc[...] += dot_t(dpre_ref[...], uw[...])

    @pl.when(step == pl.num_programs(0) - 1)
    def _():
        for copy in copies:
            copy.wait()
        gain = line(gain1)
        totals = [jnp.zeros((1, D), full)] * 3
        for start in range(0, acc.shape[0], 256):
            rows = slice(start, start + 256)
            pieces = []
            for s in range(start // seq_len, (start + 256) // seq_len):
                block = dr2_ref[s * seq_len : (s + 1) * seq_len, :]
                first = lax.broadcasted_iota(jnp.int32, block.shape, 0) == 0
                pieces.append(block + jnp.where(first, fix_ref[s : s + 1, :], 0.0))
            grad, hat = acc[rows, :] + jnp.concatenate(pieces, axis=0), hat_ref[rows, :]
            dr1 = norm_back(grad * gain, hat, inv_ref[rows, 0:1])
            dr1_ref[rows, :] = dr1
            datt = dr1.astype(low)
            datt_ref[0, rows, :] = datt
            dctx_ref[rows, :] = dot_t(datt, wo[...]).astype(low)
            totals = [
                total + columns_sum(part) for total, part in zip(totals, (grad * hat, grad, datt.astype(full)), strict=True)
            ]
        for rank, total in enumerate(totals):
            sums_ref[rank : rank + 1, :] = total


def norm_one_backward(dpre, dr2, fix, seq_len, hat, inv, uw, wo, gain1):
    count, hidden = dpre.shape
    anywhere = pl.BlockSpec(memory_space=pl.ANY)
    return pl.pallas_call(
        functools.partial(norm_one_kernel, seq_len),
        grid=(hidden // D,),
        in_specs=[
            pl.BlockSpec((count, D), lambda j: (0, j)), fixed_spec(*fix.shape), pl.BlockSpec((D, D), lambda j: (0, j)),
            fixed_spec(D, D), vector_spec(), anywhere, anywhere, fixed_spec(count, LANES),
        ],
        out_specs=[fixed_spec(count, D), pl.BlockSpec((1, count, D), lambda j: (3, 0, 0)), fixed_spec(count, D), fixed_spec(8, D)],
        out_shape=[far(count, D, dtype=full), far(4, count, D), far(count, D), shape_of(8, D, dtype=full)],
        scratch_shapes=[pltpu.VMEM((count, D), full)] * 3 + [pltpu.SemaphoreType.DMA((2,))],
        compiler_params=params(1, 30),
        name="norm_one_backward",
        cost_estimate=cost(13),
    )(in_far(dpre), fix, uw, wo, gain1, in_far(dr2), in_far(hat), in_far(inv))


def attention_back_kernel(seq_len, q_ref, k_ref, v_ref, p_ref, dc_ref, stack_ref, d_ref, sums):
    q, k, v, probs, dctx = (ref[...] for ref in (q_ref, k_ref, v_ref, p_ref, dc_ref))
    count = q.shape[0]
    cells = cells_of(count, seq_len)
    factor = 1.0 / math.sqrt(HD)
    spread_dctx = [two_heads(dctx[cell]) for cell in cells]
    dprobs = [dot_t(v[cell], wide) for cell, wide in zip(cells, spread_dctx, strict=True)]
    dvals = [dot(probs[cell], wide).astype(low) for cell, wide in zip(cells, spread_dctx, strict=True)]
    dscores = []
    for cell, dprob in zip(cells, dprobs, strict=True):
        prob = probs[cell].astype(full)
        dscores.append((prob * (dprob - columns_sum(prob * dprob))).astype(low))
    dkeys = [(dot(ds, two_heads(q[cell])) * factor).astype(low) for cell, ds in zip(cells, dscores, strict=True)]
    dqueries = [(own_head(t_dot(ds, k[cell])) * factor).astype(low) for cell, ds in zip(cells, dscores, strict=True)]

    @pl.when(pl.program_id(0) == 0)
    def _():
        sums[...] = jnp.zeros_like(sums)

    for rank, pieces in enumerate((dqueries, dkeys, dvals)):
        grad = joined(pieces, count, seq_len)
        d_ref[rank] = grad
        sums[rank : rank + 1, :] += columns_sum(grad.astype(full))


def attention_backward(seq_len, q, k, v, probs, dctx, stack):
    count = q.shape[0]
    rows = 256
    row = pl.BlockSpec((rows, D), lambda i: (i, 0))
    return pl.pallas_call(
        functools.partial(attention_back_kernel, seq_len),
        grid=(count // rows,),
        in_specs=[row] * 5 + [pl.BlockSpec(memory_space=pl.ANY)],
        out_specs=[pl.BlockSpec((3, rows, D), lambda i: (0, i, 0)), fixed_spec(8, D)],
        out_shape=[far(4, count, D), shape_of(8, D, dtype=full)],
        input_output_aliases={5: 0},
        compiler_params=params(1, 14),
        name="attention_backward",
        cost_estimate=cost(8),
    )(*map(in_far, (q, k, v, probs, dctx, stack)))


def square_grad_kernel(place, c_ref, d_ref, x_far, small_ref, *rest):
    outs, x_ref, scratch, sem = rest[:4], rest[4], rest[5], rest[6]
    step = pl.program_id(0)
    copy = pltpu.make_async_copy(x_far, x_ref, sem)

    @pl.when(step == 0)
    def _():
        copy.start()
        scratch[...] = t_dot(c_ref[...], d_ref[0]).astype(low)
        tall = D // 8
        for rank in range(8):
            out_ref, first = outs[rank // 2], rank % 2 * tall
            out_ref[first : first + tall, 4 * D :] = jnp.zeros((tall, LANES), low)

            @pl.when(place[rank] == 0)
            def _(out_ref=out_ref, first=first):
                out_ref[first : first + small_ref.shape[0], 4 * D :] = small_ref[...].astype(low)

    @pl.when(step == 1)
    def _():
        copy.wait()

    @pl.when(step > 0)
    def _():
        scratch[...] = t_dot(x_ref[...], d_ref[0]).astype(low)

    put_rows(place, scratch, outs, pl.ds(pl.multiple_of((3 - step) * D, LANES), D))


def square_gradient(place, tokens, context, stack, small):
    count = tokens.shape[0]
    pair, columns = D // 4, 4 * D + LANES
    return pl.pallas_call(
        square_grad_kernel,
        grid_spec=pltpu.PrefetchScalarGridSpec(
            num_scalar_prefetch=1,
            grid=(4,),
            in_specs=[
                fixed_spec(count, D), pl.BlockSpec((1, count, D), lambda j, *_: (3 - j, 0, 0)),
                pl.BlockSpec(memory_space=pl.ANY), fixed_spec(*small.shape),
            ],
            out_specs=[fixed_spec(pair, columns)] * 4,
            scratch_shapes=[pltpu.VMEM((count, D), low), pltpu.VMEM((D, D), low), pltpu.SemaphoreType.DMA],
        ),
        out_shape=[shape_of(pair, columns)] * 4,
        compiler_params=params(1, 18),
        name="square_gradient",
        cost_estimate=cost(12),
    )(place, *map(in_far, (context, stack, tokens)), small)


def input_grad_kernel(dr1_ref, d_ref, wq, wk, wv, out_ref):
    out_ref[...] = dr1_ref[...] + dot_t(d_ref[0], wq[...]) + dot_t(d_ref[1], wk[...]) + dot_t(d_ref[2], wv[...])


def input_gradient(dr1, stack, wq, wk, wv):
    count = dr1.shape[0]
    rows = 256
    row, mat = pl.BlockSpec((rows, D), lambda i: (i, 0)), fixed_spec(D, D)
    return pl.pallas_call(
        input_grad_kernel,
        grid=(count // rows,),
        in_specs=[row, pl.BlockSpec((3, rows, D), lambda i: (0, i, 0))] + [mat] * 3,
        out_specs=row,
        out_shape=far(count, D, dtype=full),
        compiler_params=params(1),
        name="input_gradient",
        cost_estimate=cost(6),
    )(in_far(dr1), in_far(stack), wq, wk, wv)


def spread_kernel(widths, talls, first, place, *refs):
    smalls = refs[len(refs) - len(talls) :]
    outs = refs[len(refs) - len(talls) - len(widths) : len(refs) - len(talls)]
    tall = outs[0].shape[0]
    held = refs[0].shape[0] // tall
    if first and talls:

        @pl.when(pl.program_id(0) == 0)
        def _():
            for ref, old in zip(smalls, refs[4 // held : 4 // held + len(talls)], strict=True):
                ref[...] = old[...]

    for rank in range(4):

        @pl.when(pl.program_id(0) == rank)
        def _(rank=rank):
            source, rows = refs[rank // held], rank % held * tall
            at = 0
            for ref, width in zip(outs, widths, strict=True):
                ref[...] = source[rows : rows + tall, at : at + width].astype(full)
                at += width
            if talls:

                @pl.when(place[first + rank] == 0)
                def _():
                    top = rows
                    for ref in smalls:
                        ref[...] = source[top : top + ref.shape[0], at:].astype(full)
                        top += ref.shape[0]


def spread(place, first, pairs, widths, talls, carried, name):
    tall = sum(pair.shape[0] for pair in pairs) // 4
    carried = list(carried or [])
    small = [fixed_spec(rows, LANES) for rows in talls]
    in_specs = [fixed_spec(*pair.shape) for pair in pairs]
    operands = list(pairs)
    if carried:
        operands += carried[len(widths) :] + carried[: len(widths)]
        in_specs += small + [pl.BlockSpec(memory_space=pl.ANY)] * len(widths)
    return pl.pallas_call(
        functools.partial(spread_kernel, widths, talls, first),
        grid_spec=pltpu.PrefetchScalarGridSpec(
            num_scalar_prefetch=1,
            grid=(4,),
            in_specs=in_specs,
            out_specs=[pl.BlockSpec((tall, width), lambda p, place: (place[first + p], 0)) for width in widths] + small,
        ),
        out_shape=[far(8 * tall, width, dtype=full) for width in widths]
        + [shape_of(rows, LANES, dtype=full) for rows in talls],
        input_output_aliases={1 + len(operands) - len(widths) + k: k for k in range(len(widths))} if carried else {},
        compiler_params=params(1),
        name=f"{name}_spread_{first}",
        cost_estimate=cost(3),
    )(place, *operands)


def places():
    half = lax.axis_index("stream")
    chip = lax.axis_index("dp")
    bits = (chip & 1, (chip >> 1) & 1)
    table = []
    for side in (half, 1 - half):
        first = jnp.where(side == 0, bits[0], bits[1])
        second = jnp.where(side == 0, bits[1], bits[0])
        table += [4 * side + 2 * (first ^ (k >> 1)) + (second ^ (k & 1)) for k in range(4)]
    return jnp.stack(table).astype(jnp.int32)


def chip_partner(bit_zero, bit_one):
    chips = lax.axis_size("dp")
    return [
        (half * chips + chip, half * chips + (chip ^ (bit_zero if half == 0 else bit_one)))
        for half in range(2)
        for chip in range(chips)
    ]


def core_partner():
    chips = lax.axis_size("dp")
    return [(half * chips + chip, (1 - half) * chips + chip) for half in range(2) for chip in range(chips)]


def swap(piece, pairs):
    return lax.ppermute(piece, ("stream", "dp"), pairs)


def add_low(left, right):
    return (left.astype(full) + right.astype(full)).astype(low)


def tie(value, after):
    return value if after is None else lax.optimization_barrier((value, after))[0]


def all_sum(sent):
    others = [swap(pair, core_partner()) for pair in sent]
    kept = yield sent
    pair = add_low(kept[1], others[1])
    other = swap(pair, chip_partner(1, 2))
    mine = add_low(kept[0], others[0])
    after = yield pair
    tall = mine.shape[0] // 2
    mine = tie(mine, after)
    block = add_low(mine[tall:], other[tall:])
    mine = add_low(mine[:tall], other[:tall])
    other = swap(block, chip_partner(2, 1))
    after = yield block
    bits = [1 << k for k in range(2, lax.axis_size("dp").bit_length() - 1)]
    for rank, pair in enumerate(zip(bits, bits[::-1], strict=True)):
        mine = add_low(tie(mine, after), other)
        other = swap(mine, chip_partner(*pair))
        after = (yield mine) if rank in (0, len(bits) - 1) else None
    mine = add_low(tie(mine, after), other)
    other = swap(mine, chip_partner(2, 1))
    after = yield mine
    pair = jnp.concatenate([tie(mine, after), other])
    other = swap(pair, chip_partner(1, 2))
    after = yield pair
    pairs = [tie(pair, after), other]
    others = [swap(each, core_partner()) for each in pairs]
    yield pairs
    yield others


def gather_rows(rows):
    chips = lax.axis_size("dp")
    bit = 1
    after = None
    while bit < chips:
        others = [swap(rows, chip_partner(k * bit, k * bit)) for k in range(1, 4) if k * bit < chips]
        after = yield rows
        rows = jnp.concatenate([tie(rows, after)] + others)
        bit *= 4
    other = swap(rows, core_partner())
    yield rows
    yield rows, other


def in_far(array):
    return pltpu.with_memory_space_constraint(array, pltpu.HBM)


def shards(
    layer_input, pair_group, query_weight, query_bias, key_weight, value_weight, value_bias,
    out_weight, out_bias, mixer_gain, mixer_shift, up_weight, up_bias, down_weight, down_bias,
    final_gain, final_shift, upstream,
):
    count = layer_input.shape[1]
    seq_count = pair_group.shape[0]
    seq_len = count // seq_count
    hidden = up_bias.shape[0]
    tokens, upstream = in_far(layer_input[0]), in_far(upstream[0])
    wq, wk, wv, wo = map(in_far, (query_weight, key_weight, value_weight, out_weight))
    uw, dw = in_far(up_weight), in_far(down_weight)
    fold = lambda vector: in_far(vector.reshape(-1, LANES))
    bq, bv, bo, g1, s1 = map(fold, (query_bias, value_bias, out_bias, mixer_gain, mixer_shift))
    ub, db, g2, s2 = map(fold, (up_bias, down_bias, final_gain, final_shift))
    place = places()

    q, k, v, probs, context, nl, hat, inv, lead_nl, lead_hat = attention_forward(
        tokens, seq_len, wq, wk, wv, wo, bq, bv, bo, g1, s1
    )
    lead, lead_hat, lead_inv2, lead_inv, units = lead_forward(lead_nl, lead_hat, uw, ub, dw, g1, s1, db, g2, s2)
    ids = jnp.broadcast_to(pair_group.astype(low)[:, None], (seq_count, LANES))
    hops = gather_rows(jnp.concatenate([units, ids], axis=1))
    sent = next(hops)
    parts = 2
    carried = None
    for part in range(parts):
        carried = ff_forward(
            part, parts, carried, seq_len, tie(nl, sent), hat, upstream, uw, ub, dw, g1, s1, db, g2, s2
        )
        sent = hops.send(carried[5])
    while not isinstance(sent, tuple):
        sent = hops.send(None)
    layer_output, act, slope, dr2, dbranch, final_sums, dr2_leads = carried
    loss_rows, fix, lead_sums = pair_loss(*sent, lead, lead_hat, lead_inv2, lead_inv, final_gain)

    *down_sent, dbranch, down_sum = down_gradient(place, 4, act, dbranch, dr2_leads.reshape(-1, D), fix, seq_len)
    sent = down_sent
    talls = [hidden // LANES] + [D // LANES] * 8
    down = all_sum(down_sent)
    next(down)
    down_kept = down_gradient(place, 0, act, tie(dbranch, sent))
    sent = down_kept
    sent = down.send(tie(down_kept, sent))
    dpre, up_sums, *up_blocks = hidden_gradient(place, 0, 1, None, tie(dbranch, sent), slope, dw, nl)
    sent = dpre
    sent = down.send(sent)
    up = all_sum(up_blocks[2:])
    next(up)
    sent = (sent, up_blocks[2:])
    dr1, stack, dctx, mixer = norm_one_backward(tie(dpre, sent), dr2, fix, seq_len, hat, inv, uw, wo, g1)
    sent = dctx
    sent = up.send(tie(up_blocks[:2], sent))
    sent = down.send(sent)
    stack, qkv = attention_backward(seq_len, q, k, v, probs, tie(dctx, sent), stack)
    sent = stack
    final = jnp.sum(final_sums, axis=0)
    small = jnp.concatenate(
        [
            up_sums[0], mixer[2], mixer[0], mixer[1], final[2] + down_sum[0], final[0] + lead_sums[0],
            final[1] + lead_sums[1], qkv[0], qkv[2],
        ]
    ).reshape(-1, LANES)
    square_blocks = square_gradient(place, tokens, context, tie(stack, sent), small)
    sent = square_blocks[2]
    sent = down.send(sent)
    sent = up.send(sent)
    square = all_sum(square_blocks[2:])
    next(square)
    sent = (sent, square_blocks[2:])
    sent = square.send(tie(square_blocks[:2], sent))
    sent = up.send(sent)
    input_grad = input_gradient(tie(dr1, sent), stack, wq, wk, wv)
    sent = input_grad
    sent = down.send(sent)
    sent = square.send(sent)
    sent = up.send(sent)
    sent = down.send(sent)
    sent = square.send(sent)
    sent = up.send(sent)
    down_own = down.send(sent)
    sent = down_own
    sent = square.send(sent)
    sent = up.send(sent)
    down_out = spread(place, 0, tie(down_own, sent), [D], [], None, "down")
    sent = down_out
    sent = square.send(sent)
    up_own = up.send(sent)
    sent = up_own
    sent = square.send(sent)
    up_out = spread(place, 0, tie(up_own, sent), [hidden], [], None, "up")
    sent = up_out
    up_out = spread(place, 4, up.send(sent), [hidden], [], up_out, "up")
    sent = up_out
    down_out = spread(place, 4, down.send(sent), [D], [], down_out, "down")
    sent = down_out
    square_own = square.send(sent)
    sent = square_own
    squares = spread(place, 0, tie(square_own, sent), [D] * 4, talls, None, "square")
    sent = squares
    squares = spread(place, 4, square.send(sent), [D] * 4, talls, squares, "square")
    wq_grad, wk_grad, wv_grad, wo_grad, *smalls = squares
    up_b, out_b, gain_one, shift_one, down_b, gain_two, shift_two, query_b, value_b = (each.reshape(-1) for each in smalls)
    return (
        layer_output[None], input_grad[None], loss_rows,
        wq_grad, query_b, wk_grad, wv_grad, value_b, wo_grad, out_b,
        gain_one, shift_one, up_out[0], up_b, down_out[0], down_b, gain_two, shift_two,
    )


def solution(mesh):
    split = P("stream", "dp", None)
    return jax.shard_map(
        shards,
        mesh=mesh,
        in_specs=(split, P("dp")) + (P(),) * 15 + (split,),
        out_specs=(split, split, P("stream", "dp")) + (P(),) * 15,
        check_vma=False,
    )
```

profile of v0, /device:TPU:0, one launch (start us, length us, event | category | flops | bytes accessed | tf_op | source)
XLA Modules:
  0.0 263.7 jit_solution(4320878204315635532)
XLA Ops:
  1.3 14.1 %attention_forward.1 = (bf16[1024,768]{1,0:T(8,128)(2,1)}, bf16[1024,768]{1,0:T(8,128)(2,1)}, bf16[1024,768]{1,0:T(8,128)(2,1)}, bf16[1024,768]{1,0:T(8,128)(2,1...) custom-call(bf16[1024,768]{1,0:T(8,128)(2,1)} %bitcast.40, ...), custom_call_target="tpu_custom_call" | custom-call | flops 34500001792 | bytes 1000 | tf_op jit(solution)/shard_map/attention_forward/pallas_call | solution.py:160
  15.5 5.7 %lead_forward.1 = (f32[16,768]{1,0:T(8,128)S(1)}, f32[16,768]{1,0:T(8,128)S(1)}, f32[16,128]{1,0:T(8,128)S(1)}, f32[16,128]{1,0:T(8,128)S(1)}, bf16[16,768]{1,0:T(8,128)(2,1)S(1)}) custom-call(f32[4,4,768]{2,1,0:T(4,128)S(1)} %get-tuple-element.137.nl_ref, f32[4,4,768]{2,1,0:T(4,128)S(1)} %get-tuple-element.138.hat_ref, bf16[768,3072]{1,0:T(8,128)(2,1)} %uw.7, ...), custom_call_target="tpu_custom_call" | custom-call | flops 10350000128 | bytes 1000 | tf_op jit(solution)/shard_map/lead_forward/pallas_call | solution.py:203
  21.3 2.9 %collective-permute-start = (bf16[16,896]{1,0:T(8,128)(2,1)S(1)}, bf16[16,896]{1,0:T(8,128)(2,1)S(1)}, u32[]{:S(2)}, u32[]{:S(2)}) collective-permute-start(bf16[16,896]{1,0:T(8,128)(2,1)S(1)} %pad_maximum_fusion), channel_id=1, source_target_pairs={{0,1},{1,0},{2,3},{3,2},{4,5},{5,4},{6,7},{7,6},{8,9},{9,8},{10,11... | collective-permute-start | bytes 86024 | tf_op jit(solution)/shard_map/ppermute | solution.py:731
  24.2 1.5 collective-permute-start.1
  25.7 15.8 %ff_forward_0.1 = (bf16[1024,768]{1,0:T(8,128)(2,1)}, bf16[1024,3072]{1,0:T(8,128)(2,1)}, bf16[1024,3072]{1,0:T(8,128)(2,1)}, f32[1024,768]{1,0:T(8,128)}, bf16[...) custom-call(bf16[1024,768]{1,0:T(8,128)(2,1)} %get-tuple-element.144.nl_ref, ...), custom_call_target="tpu_custom_call" | custom-call | flops 44849999872 | bytes 1000 | tf_op jit(solution)/shard_map/ff_forward_0/pallas_call | solution.py:278
  41.7 2.1 collective-permute-start.3
  43.7 2.6 collective-permute-start.4
  46.3 15.8 %ff_forward_1.1 = (bf16[1024,768]{1,0:T(8,128)(2,1)}, bf16[1024,3072]{1,0:T(8,128)(2,1)}, bf16[1024,3072]{1,0:T(8,128)(2,1)}, f32[1024,768]{1,0:T(8,128)}, bf16[...) custom-call(bf16[1024,768]{1,0:T(8,128)(2,1)} %get-tuple-element.144, ...), custom_call_target="tpu_custom_call", output_to_operand_aliasing={{0}: (11, {}), {1}: (12, {}), {2}: (13, {}), {3}: (14, {}),... | custom-call | flops 44849999872 | bytes 1000 | tf_op jit(solution)/shard_map/ff_forward_1/pallas_call | solution.py:278
  62.4 1.7 collective-permute-done.6.other_ref
  64.1 1.9 pair_loss.1
  66.0 5.9 %down_grad_4.1 = (bf16[768,768]{1,0:T(8,128)(2,1)S(1)}, bf16[768,768]{1,0:T(8,128)(2,1)S(1)}, bf16[1024,768]{1,0:T(8,128)(2,1)S(1)}, f32[1,768]{1,0:T(1,128)S(1)}) custom-call(s32[8]{0:T(128)S(1)} %stack.35.place, bf16[1024,768]{1,0:T(8,128)(2,1)S(1)} %copy-done, f32[16,768]{1,0:T(8,128)S(1)} %bitcast.35, f32[16,768]{1,0:T(8,128)S(1)} %get-tuple-element.160.refs_2_.fix_ref, ...), custom_call_target="tpu_custom_call" | custom-call | flops 13799999488 | bytes 1000 | tf_op jit(solution)/shard_map/down_grad_4/pallas_call | solution.py:410
  72.5 5.6 %down_grad_0.1 = (bf16[768,768]{1,0:T(8,128)(2,1)S(1)}, bf16[768,768]{1,0:T(8,128)(2,1)S(1)}) custom-call(s32[8]{0:T(128)S(1)} %stack.35.place, bf16[1024,768]{1,0:T(8,128)(2,1)S(1)} %get-tuple-element.167.refs_0_.db_ref, bf16[1024,3072]{1,0:T(8,128)(2,1)} %get-tuple-element.161.refs_3_.refs_1_), custom_call_target="tpu_custom_call" | custom-call | flops 13799999488 | bytes 1000 | tf_op jit(solution)/shard_map/down_grad_0/pallas_call | solution.py:410
  78.5 1.8 collective-permute-start.9
  80.2 14.9 %hidden_gradient_0.1 = (bf16[1024,3072]{1,0:T(8,128)(2,1)}, f32[8,3072]{1,0:T(8,128)S(1)}, bf16[192,3072]{1,0:T(8,128)(2,1)S(1)}, bf16[192,3072]{1,0:T(8,128)(2,...) custom-call(s32[8]{0:T(128)S(1)} %stack.35.place, ...), custom_call_target="tpu_custom_call", output_to_operand_aliasing={{0}: (2, {})} | custom-call | flops 27599998976 | bytes 1000 | tf_op jit(solution)/shard_map/hidden_gradient_0/pallas_call | solution.py:456
  96.3 1.6 collective-permute-start.12
  97.9 14.4 %norm_one_backward.1 = (f32[1024,768]{1,0:T(8,128)}, bf16[4,1024,768]{2,1,0:T(8,128)(2,1)}, bf16[1024,768]{1,0:T(8,128)(2,1)}, f32[8,768]{1,0:T(8,128)S(1)}) custom-call(bf16[1024,3072]{1,0:T(8,128)(2,1)} %get-tuple-element.174.dpre_ref, f32[16,768]{1,0:T(8,128)S(1)} %get-tuple-element.160.refs_2_.fix_ref, bf16[768,3072]{1,0:T(8,128)(2,1)} %uw.7, ...), custom_call_target="tpu_custom_call" | custom-call | flops 44849999872 | bytes 1000 | tf_op jit(solution)/shard_map/norm_one_backward/pallas_call | solution.py:518
  113.6 0.7 collective-permute-start.13
  114.4 9.2 %attention_backward.1 = (bf16[4,1024,768]{2,1,0:T(8,128)(2,1)}, f32[8,768]{1,0:T(8,128)S(1)}) custom-call(bf16[1024,768]{1,0:T(8,128)(2,1)} %get-tuple-element.185.q_ref, bf16[1024,768]{1,0:T(8,128)(2,1)} %get-tuple-element.186.k_ref, bf16[1024,768]{1,0:T(8,128)(2,1)} %get-tuple-element.187.v_ref, ...), custom_call_target="tpu_custom_call", output_to_operand_aliasing={{0}: (5, {})} | custom-call | flops 27599998976 | bytes 1000 | tf_op jit(solution)/shard_map/attention_backward/pallas_call | solution.py:563
  123.6 8.9 %square_gradient.1 = (bf16[192,3200]{1,0:T(8,128)(2,1)S(1)}, bf16[192,3200]{1,0:T(8,128)(2,1)S(1)}, bf16[192,3200]{1,0:T(8,128)(2,1)S(1)}, bf16[192,3200]{1,0:T(8,128)(2,1)S(1)}) custom-call(s32[8]{0:T(128)S(1)} %stack.35.place, bf16[1024,768]{1,0:T(8,128)(2,1)} %get-tuple-element.184.c_ref, bf16[4,1024,768]{2,1,0:T(8,128)(2,1)} %get-tuple-element.192.d_ref, ...), custom_call_target="tpu_custom_call" | custom-call | flops 41400000512 | bytes 1000 | tf_op jit(solution)/shard_map/square_gradient/pallas_call | solution.py:608
  133.7 3.6 %collective-permute-start.18 = (bf16[384,768]{1,0:T(8,128)(2,1)S(1)}, bf16[384,768]{1,0:T(8,128)(2,1)S(1)}, u32[]{:S(2)}, u32[]{:S(2)}) collective-permute-start(bf16[384,768]{1,0:T(8,128)(2,1)S(1)} %add_convert_fusion.17), channel_id=1, source_target_pairs={{0,8},{1,9},{2,10},{3,11},{4,12},{5,13},{6,14},{7,15},{8,0},{9,1},... | collective-permute-start | bytes 1769480 | tf_op jit(solution)/shard_map/ppermute | solution.py:731
  137.7 1.0 collective-permute-start.16
  139.0 1.2 collective-permute-start.19
  140.2 13.7 %collective-permute-done.16 = bf16[96,3072]{1,0:T(8,128)(2,1)S(1)} collective-permute-done((bf16[96,3072]{1,0:T(8,128)(2,1)S(1)}, bf16[96,3072]{1,0:T(8,128)(2,1)S(1)}, u32[]{:S(2)}, u32[]{:S(2)}) %collective-permute-start.16) | collective-permute-done | bytes 589856 | tf_op jit(solution)/shard_map/ppermute | solution.py:731
  154.2 8.8 %input_gradient.1 = f32[1024,768]{1,0:T(8,128)} custom-call(f32[1024,768]{1,0:T(8,128)} %get-tuple-element.206.dr1_ref, bf16[4,1024,768]{2,1,0:T(8,128)(2,1)} %get-tuple-element.192.d_ref, bf16[768,768]{1,0:T(8,128)(2,1)} %wq.3, bf16[768,768]{1,0:T(8,128)(2,1)} %wk.3, bf16[768,768]{1,0:T(8,128)(2,1)} %wv.3), custom_call_target="tpu_custom_call" | custom-call | flops 20700000256 | bytes 1000 | tf_op jit(solution)/shard_map/input_gradient/pallas_call | solution.py:635
  163.2 0.9 collective-permute-start.21
  164.7 1.2 collective-permute-start.22
  165.9 4.8 %collective-permute-done.20 = bf16[96,3072]{1,0:T(8,128)(2,1)S(1)} collective-permute-done((bf16[96,3072]{1,0:T(8,128)(2,1)S(1)}, bf16[96,3072]{1,0:T(8,128)(2,1)S(1)}, u32[]{:S(2)}, u32[]{:S(2)}) %collective-permute-start.20) | collective-permute-done | bytes 589856 | tf_op jit(solution)/shard_map/ppermute | solution.py:731
  171.1 3.8 %collective-permute-done.21 = bf16[384,768]{1,0:T(8,128)(2,1)S(1)} collective-permute-done((bf16[384,768]{1,0:T(8,128)(2,1)S(1)}, bf16[384,768]{1,0:T(8,128)(2,1)S(1)}, u32[]{:S(2)}, u32[]{:S(2)}) %collective-permute-start.21) | collective-permute-done | bytes 589856 | tf_op jit(solution)/shard_map/ppermute | solution.py:731
  174.9 1.7 collective-permute-start.24
  176.6 11.4 %collective-permute-done.22 = bf16[96,3200]{1,0:T(8,128)(2,1)S(1)} collective-permute-done((bf16[96,3200]{1,0:T(8,128)(2,1)S(1)}, bf16[96,3200]{1,0:T(8,128)(2,1)S(1)}, u32[]{:S(2)}, u32[]{:S(2)}) %collective-permute-start.22) | collective-permute-done | bytes 614432 | tf_op jit(solution)/shard_map/ppermute | solution.py:731
  188.2 1.7 collective-permute-start.25
  189.9 10.4 %collective-permute-done.23 = bf16[96,3072]{1,0:T(8,128)(2,1)S(1)} collective-permute-done((bf16[96,3072]{1,0:T(8,128)(2,1)S(1)}, bf16[96,3072]{1,0:T(8,128)(2,1)S(1)}, u32[]{:S(2)}, u32[]{:S(2)}) %collective-permute-start.23) | collective-permute-done | bytes 589856 | tf_op jit(solution)/shard_map/ppermute | solution.py:731
  200.5 1.6 collective-permute-start.26
  202.6 6.7 %collective-permute-done.25 = bf16[96,3200]{1,0:T(8,128)(2,1)S(1)} collective-permute-done((bf16[96,3200]{1,0:T(8,128)(2,1)S(1)}, bf16[96,3200]{1,0:T(8,128)(2,1)S(1)}, u32[]{:S(2)}, u32[]{:S(2)}) %collective-permute-start.25) | collective-permute-done | bytes 614432 | tf_op jit(solution)/shard_map/ppermute | solution.py:731
  209.6 5.8 %collective-permute-done.26 = bf16[96,3072]{1,0:T(8,128)(2,1)S(1)} collective-permute-done((bf16[96,3072]{1,0:T(8,128)(2,1)S(1)}, bf16[96,3072]{1,0:T(8,128)(2,1)S(1)}, u32[]{:S(2)}, u32[]{:S(2)}) %collective-permute-start.26) | collective-permute-done | bytes 589856 | tf_op jit(solution)/shard_map/ppermute | solution.py:731
  215.4 0.7 collective-permute-start.28
  216.1 3.2 %down_spread_0.1.refs_2_ = f32[3072,768]{1,0:T(8,128)} custom-call(s32[8]{0:T(128)S(1)} %stack.35.place, bf16[768,768]{1,0:T(8,128)(2,1)S(1)} %constant_dynamic-update-slice_fusion.9.refs_0_, bf16[768,768]{1,0:T(8,128)(2,1)S(1)} %collective-permute-done.24.refs_1_), custom_call_target="tpu_custom_call" | custom-call | flops 10350000128 | bytes 1000 | tf_op jit(solution)/shard_map/down_spread_0/pallas_call | solution.py:687
  219.3 6.8 %collective-permute-done.27 = bf16[96,3200]{1,0:T(8,128)(2,1)S(1)} collective-permute-done((bf16[96,3200]{1,0:T(8,128)(2,1)S(1)}, bf16[96,3200]{1,0:T(8,128)(2,1)S(1)}, u32[]{:S(2)}, u32[]{:S(2)}) %collective-permute-start.27) | collective-permute-done | bytes 614432 | tf_op jit(solution)/shard_map/ppermute | solution.py:731
  226.2 2.6 collective-permute-start.29
  229.4 6.7 %collective-permute-done.28.refs_1_ = bf16[192,3072]{1,0:T(8,128)(2,1)S(1)} collective-permute-done((bf16[192,3072]{1,0:T(8,128)(2,1)S(1)}, bf16[192,3072]{1,0:T(8,128)(2,1)S(1)}, u32[]{:S(2)}, u32[]{:S(2)}) %collective-permute-start.28) | collective-permute-done | bytes 1179680 | tf_op jit(solution)/shard_map/ppermute | solution.py:731
  236.1 0.8 collective-permute-done.29
  237.0 1.1 collective-permute-start.33
  238.1 3.2 %down_spread_4.1 = f32[3072,768]{1,0:T(8,128)} custom-call(s32[8]{0:T(128)S(1)} %stack.35.place, bf16[768,768]{1,0:T(8,128)(2,1)S(1)} %collective-permute-done.30.refs_0_, bf16[768,768]{1,0:T(8,128)(2,1)S(1)} %collective-permute-done.31.refs_1_, f32[3072,768]{1,0:T(8,128)} %down_spread_0.1.refs_2_), custom_call_target="tpu_custom_call", output_to_operand_aliasing={{}: (3, {})} | custom-call | flops 10350000128 | bytes 1000 | tf_op jit(solution)/shard_map/down_spread_4/pallas_call | solution.py:687
  241.3 3.2 %up_spread_0.1.refs_2_ = f32[768,3072]{1,0:T(8,128)} custom-call(s32[8]{0:T(128)S(1)} %stack.35.place, bf16[192,3072]{1,0:T(8,128)(2,1)S(1)} %constant_dynamic-update-slice_fusion.11.refs_0_, bf16[192,3072]{1,0:T(8,128)(2,1)S(1)} %collective-permute-done.28.refs_1_), custom_call_target="tpu_custom_call" | custom-call | flops 10350000128 | bytes 1000 | tf_op jit(solution)/shard_map/up_spread_0/pallas_call | solution.py:687
  244.5 9.3 %collective-permute-done.33.refs_1_ = bf16[192,3200]{1,0:T(8,128)(2,1)S(1)} collective-permute-done((bf16[192,3200]{1,0:T(8,128)(2,1)S(1)}, bf16[192,3200]{1,0:T(8,128)(2,1)S(1)}, u32[]{:S(2)}, u32[]{:S(2)}) %collective-permute-start.33) | collective-permute-done | bytes 1228832 | tf_op jit(solution)/shard_map/ppermute | solution.py:731
  253.8 3.2 %up_spread_4.1 = f32[768,3072]{1,0:T(8,128)} custom-call(s32[8]{0:T(128)S(1)} %stack.35.place, bf16[192,3072]{1,0:T(8,128)(2,1)S(1)} %collective-permute-done.35.refs_0_, bf16[192,3072]{1,0:T(8,128)(2,1)S(1)} %collective-permute-done.36.refs_1_, f32[768,3072]{1,0:T(8,128)} %up_spread_0.1.refs_2_), custom_call_target="tpu_custom_call", output_to_operand_aliasing={{}: (3, {})} | custom-call | flops 10350000128 | bytes 1000 | tf_op jit(solution)/shard_map/up_spread_4/pallas_call | solution.py:687
  257.0 3.2 %square_spread_0.1 = (f32[768,768]{1,0:T(8,128)}, f32[768,768]{1,0:T(8,128)}, f32[768,768]{1,0:T(8,128)}, f32[768,768]{1,0:T(8,128)}, f32[24,128]{1,0:T(8,128)S(...) custom-call(s32[8]{0:T(128)S(1)} %stack.35.place, ...), custom_call_target="tpu_custom_call" | custom-call | flops 10350000128 | bytes 1000 | tf_op jit(solution)/shard_map/square_spread_0/pallas_call | solution.py:687
  260.2 3.3 %square_spread_4.1 = (f32[768,768]{1,0:T(8,128)}, f32[768,768]{1,0:T(8,128)}, f32[768,768]{1,0:T(8,128)}, f32[768,768]{1,0:T(8,128)}, f32[24,128]{1,0:T(8,128)},...) custom-call(s32[8]{0:T(128)S(1)} %stack.35.place, ...), custom_call_target="tpu_custom_call", output_to_operand_aliasing={{0}: (12, {}), {1}: (13, {}), {2}: (14, {}), {3}: (15, {})} | custom-call | flops 10350000128 | bytes 1000 | tf_op jit(solution)/shard_map/square_spread_4/pallas_call | solution.py:687
  (97 shorter events, 9.7 us)
Async XLA Ops:
  21.3 20.3 %collective-permute-start = (bf16[16,896]{1,0:T(8,128)(2,1)S(1)}, bf16[16,896]{1,0:T(8,128)(2,1)S(1)}, u32[]{:S(2)}, u32[]{:S(2)}) collective-permute-start(bf16[16,896]{1,0:T(8,128)(2,1)S(1)} %pad_maximum_fusion), channel_id=1, source_target_pairs={{0,1},{1,0},{2,3},{3,2},{4,5},{5,4},{6,7},{7,6},{8,9},{9,8},{10,11... | collective-permute-start | bytes 86024 | tf_op jit(solution)/shard_map/ppermute | solution.py:731
  24.2 17.4 %collective-permute-start.1 = (bf16[16,896]{1,0:T(8,128)(2,1)S(1)}, bf16[16,896]{1,0:T(8,128)(2,1)S(1)}, u32[]{:S(2)}, u32[]{:S(2)}) collective-permute-start(bf16[16,896]{1,0:T(8,128)(2,1)S(1)} %pad_maximum_fusion), channel_id=1, source_target_pairs={{0,2},{1,3},{2,0},{3,1},{4,6},{5,7},{6,4},{7,5},{8,10},{9,11},{10,... | collective-permute-start | bytes 86024 | tf_op jit(solution)/shard_map/ppermute | solution.py:731
  25.7 15.9 %collective-permute-start.2 = (bf16[16,896]{1,0:T(8,128)(2,1)S(1)}, bf16[16,896]{1,0:T(8,128)(2,1)S(1)}, u32[]{:S(2)}, u32[]{:S(2)}) collective-permute-start(bf16[16,896]{1,0:T(8,128)(2,1)S(1)} %pad_maximum_fusion), channel_id=1, source_target_pairs={{0,3},{1,2},{2,1},{3,0},{4,7},{5,6},{6,5},{7,4},{8,11},{9,10},{10,... | collective-permute-start | bytes 86024 | tf_op jit(solution)/shard_map/ppermute | solution.py:731
  41.7 20.5 %collective-permute-start.3 = (bf16[64,896]{1,0:T(8,128)(2,1)S(1)}, bf16[64,896]{1,0:T(8,128)(2,1)S(1)}, u32[]{:S(2)}, u32[]{:S(2)}) collective-permute-start(bf16[64,896]{1,0:T(8,128)(2,1)S(1)} %constant_dynamic-update-slice_fusion), channel_id=1, source_target_pairs={{0,4},{1,5},{2,6},{3,7},{4,0},{5,1},{6,2},{7,3},{8,12},{9,13},{10,... | collective-permute-start | bytes 344072 | tf_op jit(solution)/shard_map/ppermute | solution.py:731
  43.7 18.4 %collective-permute-start.4 = (bf16[64,896]{1,0:T(8,128)(2,1)S(1)}, bf16[64,896]{1,0:T(8,128)(2,1)S(1)}, u32[]{:S(2)}, u32[]{:S(2)}) collective-permute-start(bf16[64,896]{1,0:T(8,128)(2,1)S(1)} %constant_dynamic-update-slice_fusion), channel_id=1, source_target_pairs={{0,8},{1,9},{2,10},{3,11},{4,12},{5,13},{6,14},{7,15},{8,0},{9,1},... | collective-permute-start | bytes 344072 | tf_op jit(solution)/shard_map/ppermute | solution.py:731
  46.3 15.9 %collective-permute-start.5 = (bf16[64,896]{1,0:T(8,128)(2,1)S(1)}, bf16[64,896]{1,0:T(8,128)(2,1)S(1)}, u32[]{:S(2)}, u32[]{:S(2)}) collective-permute-start(bf16[64,896]{1,0:T(8,128)(2,1)S(1)} %constant_dynamic-update-slice_fusion), channel_id=1, source_target_pairs={{0,12},{1,13},{2,14},{3,15},{4,8},{5,9},{6,10},{7,11},{8,4},{9,5},... | collective-permute-start | bytes 344072 | tf_op jit(solution)/shard_map/ppermute | solution.py:731
  62.2 1.9 collective-permute-start.6
  64.1 1.9 copy-start
  71.9 23.2 %collective-permute-start.8 = (bf16[768,768]{1,0:T(8,128)(2,1)S(1)}, bf16[768,768]{1,0:T(8,128)(2,1)S(1)}, u32[]{:S(2)}, u32[]{:S(2)}) collective-permute-start(bf16[768,768]{1,0:T(8,128)(2,1)S(1)} %get-tuple-element.163), channel_id=1, source_target_pairs={{0,16},{1,17},{2,18},{3,19},{4,20},{5,21},{6,22},{7,23},{8,24},{9,... | collective-permute-start | bytes 3538952 | tf_op jit(solution)/shard_map/ppermute | solution.py:731
  72.1 6.0 %collective-permute-start.7 = (bf16[768,768]{1,0:T(8,128)(2,1)S(1)}, bf16[768,768]{1,0:T(8,128)(2,1)S(1)}, u32[]{:S(2)}, u32[]{:S(2)}) collective-permute-start(bf16[768,768]{1,0:T(8,128)(2,1)S(1)} %get-tuple-element.164), channel_id=1, source_target_pairs={{0,16},{1,17},{2,18},{3,19},{4,20},{5,21},{6,22},{7,23},{8,24},{9,... | collective-permute-start | bytes 3538952 | tf_op jit(solution)/shard_map/ppermute | solution.py:731
  78.5 17.5 %collective-permute-start.9 = (bf16[768,768]{1,0:T(8,128)(2,1)S(1)}, bf16[768,768]{1,0:T(8,128)(2,1)S(1)}, u32[]{:S(2)}, u32[]{:S(2)}) collective-permute-start(bf16[768,768]{1,0:T(8,128)(2,1)S(1)} %add_convert_fusion.5), channel_id=1, source_target_pairs={{0,1},{1,0},{2,3},{3,2},{4,5},{5,4},{6,7},{7,6},{8,9},{9,8},{10,11... | collective-permute-start | bytes 3538952 | tf_op jit(solution)/shard_map/ppermute | solution.py:731
  95.4 17.0 %collective-permute-start.11 = (bf16[192,3072]{1,0:T(8,128)(2,1)S(1)}, bf16[192,3072]{1,0:T(8,128)(2,1)S(1)}, u32[]{:S(2)}, u32[]{:S(2)}) collective-permute-start(bf16[192,3072]{1,0:T(8,128)(2,1)S(1)} %get-tuple-element.173), channel_id=1, source_target_pairs={{0,16},{1,17},{2,18},{3,19},{4,20},{5,21},{6,22},{7,23},{8,24},{9,... | collective-permute-start | bytes 3538952 | tf_op jit(solution)/shard_map/ppermute | solution.py:731
  95.5 37.3 %collective-permute-start.10 = (bf16[192,3072]{1,0:T(8,128)(2,1)S(1)}, bf16[192,3072]{1,0:T(8,128)(2,1)S(1)}, u32[]{:S(2)}, u32[]{:S(2)}) collective-permute-start(bf16[192,3072]{1,0:T(8,128)(2,1)S(1)} %get-tuple-element.172), channel_id=1, source_target_pairs={{0,16},{1,17},{2,18},{3,19},{4,20},{5,21},{6,22},{7,23},{8,24},{9,... | collective-permute-start | bytes 3538952 | tf_op jit(solution)/shard_map/ppermute | solution.py:731
  96.3 17.2 %collective-permute-start.12 = (bf16[384,768]{1,0:T(8,128)(2,1)S(1)}, bf16[384,768]{1,0:T(8,128)(2,1)S(1)}, u32[]{:S(2)}, u32[]{:S(2)}) collective-permute-start(bf16[384,768]{1,0:T(8,128)(2,1)S(1)} %get-tuple-element.267), channel_id=1, source_target_pairs={{0,2},{1,3},{2,0},{3,1},{4,6},{5,7},{6,4},{7,5},{8,10},{9,11},{10,... | collective-permute-start | bytes 1769480 | tf_op jit(solution)/shard_map/ppermute | solution.py:731
  112.8 24.5 %collective-permute-start.14 = (bf16[192,3072]{1,0:T(8,128)(2,1)S(1)}, bf16[192,3072]{1,0:T(8,128)(2,1)S(1)}, u32[]{:S(2)}, u32[]{:S(2)}) collective-permute-start(bf16[192,3072]{1,0:T(8,128)(2,1)S(1)} %add_convert_fusion.2), channel_id=1, source_target_pairs={{0,1},{1,0},{2,3},{3,2},{4,5},{5,4},{6,7},{7,6},{8,9},{9,8},{10,11... | collective-permute-start | bytes 3538952 | tf_op jit(solution)/shard_map/ppermute | solution.py:731
  113.6 20.0 %collective-permute-start.13 = (bf16[384,768]{1,0:T(8,128)(2,1)S(1)}, bf16[384,768]{1,0:T(8,128)(2,1)S(1)}, u32[]{:S(2)}, u32[]{:S(2)}) collective-permute-start(bf16[384,768]{1,0:T(8,128)(2,1)S(1)} %add_convert_fusion.18), channel_id=1, source_target_pairs={{0,4},{1,5},{2,6},{3,7},{4,0},{5,1},{6,2},{7,3},{8,12},{9,13},{10,... | collective-permute-start | bytes 1769480 | tf_op jit(solution)/shard_map/ppermute | solution.py:731
  132.5 6.2 %collective-permute-start.15 = (bf16[192,3200]{1,0:T(8,128)(2,1)S(1)}, bf16[192,3200]{1,0:T(8,128)(2,1)S(1)}, u32[]{:S(2)}, u32[]{:S(2)}) collective-permute-start(bf16[192,3200]{1,0:T(8,128)(2,1)S(1)} %get-tuple-element.203), channel_id=1, source_target_pairs={{0,16},{1,17},{2,18},{3,19},{4,20},{5,21},{6,22},{7,23},{8,24},{9,... | collective-permute-start | bytes 3686408 | tf_op jit(solution)/shard_map/ppermute | solution.py:731
  133.3 30.9 %collective-permute-start.17 = (bf16[192,3200]{1,0:T(8,128)(2,1)S(1)}, bf16[192,3200]{1,0:T(8,128)(2,1)S(1)}, u32[]{:S(2)}, u32[]{:S(2)}) collective-permute-start(bf16[192,3200]{1,0:T(8,128)(2,1)S(1)} %get-tuple-element.198), channel_id=1, source_target_pairs={{0,16},{1,17},{2,18},{3,19},{4,20},{5,21},{6,22},{7,23},{8,24},{9,... | collective-permute-start | bytes 3686408 | tf_op jit(solution)/shard_map/ppermute | solution.py:731
  133.7 29.3 %collective-permute-start.18 = (bf16[384,768]{1,0:T(8,128)(2,1)S(1)}, bf16[384,768]{1,0:T(8,128)(2,1)S(1)}, u32[]{:S(2)}, u32[]{:S(2)}) collective-permute-start(bf16[384,768]{1,0:T(8,128)(2,1)S(1)} %add_convert_fusion.17), channel_id=1, source_target_pairs={{0,8},{1,9},{2,10},{3,11},{4,12},{5,13},{6,14},{7,15},{8,0},{9,1},... | collective-permute-start | bytes 1769480 | tf_op jit(solution)/shard_map/ppermute | solution.py:731
  137.7 16.2 %collective-permute-start.16 = (bf16[96,3072]{1,0:T(8,128)(2,1)S(1)}, bf16[96,3072]{1,0:T(8,128)(2,1)S(1)}, u32[]{:S(2)}, u32[]{:S(2)}) collective-permute-start(bf16[96,3072]{1,0:T(8,128)(2,1)S(1)} %get-tuple-element.265), channel_id=1, source_target_pairs={{0,2},{1,3},{2,0},{3,1},{4,6},{5,7},{6,4},{7,5},{8,10},{9,11},{10,... | collective-permute-start | bytes 1769480 | tf_op jit(solution)/shard_map/ppermute | solution.py:731
  139.0 25.4 %collective-permute-start.19 = (bf16[192,3200]{1,0:T(8,128)(2,1)S(1)}, bf16[192,3200]{1,0:T(8,128)(2,1)S(1)}, u32[]{:S(2)}, u32[]{:S(2)}) collective-permute-start(bf16[192,3200]{1,0:T(8,128)(2,1)S(1)} %add_convert_fusion.1), channel_id=1, source_target_pairs={{0,1},{1,0},{2,3},{3,2},{4,5},{5,4},{6,7},{7,6},{8,9},{9,8},{10,11... | collective-permute-start | bytes 3686408 | tf_op jit(solution)/shard_map/ppermute | solution.py:731
  154.1 16.7 %collective-permute-start.20 = (bf16[96,3072]{1,0:T(8,128)(2,1)S(1)}, bf16[96,3072]{1,0:T(8,128)(2,1)S(1)}, u32[]{:S(2)}, u32[]{:S(2)}) collective-permute-start(bf16[96,3072]{1,0:T(8,128)(2,1)S(1)} %add_convert_fusion.14), channel_id=1, source_target_pairs={{0,4},{1,5},{2,6},{3,7},{4,0},{5,1},{6,2},{7,3},{8,12},{9,13},{10,... | collective-permute-start | bytes 1769480 | tf_op jit(solution)/shard_map/ppermute | solution.py:731
  163.2 11.7 %collective-permute-start.21 = (bf16[384,768]{1,0:T(8,128)(2,1)S(1)}, bf16[384,768]{1,0:T(8,128)(2,1)S(1)}, u32[]{:S(2)}, u32[]{:S(2)}) collective-permute-start(bf16[384,768]{1,0:T(8,128)(2,1)S(1)} %add_convert_fusion.13), channel_id=1, source_target_pairs={{0,2},{1,3},{2,0},{3,1},{4,6},{5,7},{6,4},{7,5},{8,10},{9,11},{10,... | collective-permute-start | bytes 1769480 | tf_op jit(solution)/shard_map/ppermute | solution.py:731
  164.7 23.3 %collective-permute-start.22 = (bf16[96,3200]{1,0:T(8,128)(2,1)S(1)}, bf16[96,3200]{1,0:T(8,128)(2,1)S(1)}, u32[]{:S(2)}, u32[]{:S(2)}) collective-permute-start(bf16[96,3200]{1,0:T(8,128)(2,1)S(1)} %get-tuple-element.263), channel_id=1, source_target_pairs={{0,2},{1,3},{2,0},{3,1},{4,6},{5,7},{6,4},{7,5},{8,10},{9,11},{10,... | collective-permute-start | bytes 1843208 | tf_op jit(solution)/shard_map/ppermute | solution.py:731
  170.9 29.4 %collective-permute-start.23 = (bf16[96,3072]{1,0:T(8,128)(2,1)S(1)}, bf16[96,3072]{1,0:T(8,128)(2,1)S(1)}, u32[]{:S(2)}, u32[]{:S(2)}) collective-permute-start(bf16[96,3072]{1,0:T(8,128)(2,1)S(1)} %add_convert_fusion.12), channel_id=1, source_target_pairs={{0,8},{1,9},{2,10},{3,11},{4,12},{5,13},{6,14},{7,15},{8,0},{9,1},... | collective-permute-start | bytes 1769480 | tf_op jit(solution)/shard_map/ppermute | solution.py:731
  174.9 27.1 %collective-permute-start.24 = (bf16[768,768]{1,0:T(8,128)(2,1)S(1)}, bf16[768,768]{1,0:T(8,128)(2,1)S(1)}, u32[]{:S(2)}, u32[]{:S(2)}) collective-permute-start(bf16[768,768]{1,0:T(8,128)(2,1)S(1)} %constant_dynamic-update-slice_fusion.9.refs_0_), channel_id=1, source_target_pairs={{0,1},{1,0},{2,3},{3,2},{4,5},{5,4},{6,7},{7,6},{8,9},{9,8},{10,11... | collective-permute-start | bytes 3538952 | tf_op jit(solution)/shard_map/ppermute | solution.py:731
  188.2 21.1 %collective-permute-start.25 = (bf16[96,3200]{1,0:T(8,128)(2,1)S(1)}, bf16[96,3200]{1,0:T(8,128)(2,1)S(1)}, u32[]{:S(2)}, u32[]{:S(2)}) collective-permute-start(bf16[96,3200]{1,0:T(8,128)(2,1)S(1)} %add_convert_fusion.8), channel_id=1, source_target_pairs={{0,4},{1,5},{2,6},{3,7},{4,0},{5,1},{6,2},{7,3},{8,12},{9,13},{10,... | collective-permute-start | bytes 1843208 | tf_op jit(solution)/shard_map/ppermute | solution.py:731
  200.5 14.9 %collective-permute-start.26 = (bf16[96,3072]{1,0:T(8,128)(2,1)S(1)}, bf16[96,3072]{1,0:T(8,128)(2,1)S(1)}, u32[]{:S(2)}, u32[]{:S(2)}) collective-permute-start(bf16[96,3072]{1,0:T(8,128)(2,1)S(1)} %add_convert_fusion.11), channel_id=1, source_target_pairs={{0,2},{1,3},{2,0},{3,1},{4,6},{5,7},{6,4},{7,5},{8,10},{9,11},{10,... | collective-permute-start | bytes 1769480 | tf_op jit(solution)/shard_map/ppermute | solution.py:731
  202.1 36.1 %collective-permute-start.30 = (bf16[768,768]{1,0:T(8,128)(2,1)S(1)}, bf16[768,768]{1,0:T(8,128)(2,1)S(1)}, u32[]{:S(2)}, u32[]{:S(2)}) collective-permute-start(bf16[768,768]{1,0:T(8,128)(2,1)S(1)} %constant_dynamic-update-slice_fusion.9.refs_0_), channel_id=1, source_target_pairs={{0,16},{1,17},{2,18},{3,19},{4,20},{5,21},{6,22},{7,23},{8,24},{9,... | collective-permute-start | bytes 3538952 | tf_op jit(solution)/shard_map/ppermute | solution.py:731
  202.1 36.1 %collective-permute-start.31 = (bf16[768,768]{1,0:T(8,128)(2,1)S(1)}, bf16[768,768]{1,0:T(8,128)(2,1)S(1)}, u32[]{:S(2)}, u32[]{:S(2)}) collective-permute-start(bf16[768,768]{1,0:T(8,128)(2,1)S(1)} %collective-permute-done.24.refs_1_), channel_id=1, source_target_pairs={{0,16},{1,17},{2,18},{3,19},{4,20},{5,21},{6,22},{7,23},{8,24},{9,... | collective-permute-start | bytes 3538952 | tf_op jit(solution)/shard_map/ppermute | solution.py:731
  209.4 16.7 %collective-permute-start.27 = (bf16[96,3200]{1,0:T(8,128)(2,1)S(1)}, bf16[96,3200]{1,0:T(8,128)(2,1)S(1)}, u32[]{:S(2)}, u32[]{:S(2)}) collective-permute-start(bf16[96,3200]{1,0:T(8,128)(2,1)S(1)} %add_convert_fusion.7), channel_id=1, source_target_pairs={{0,8},{1,9},{2,10},{3,11},{4,12},{5,13},{6,14},{7,15},{8,0},{9,1},... | collective-permute-start | bytes 1843208 | tf_op jit(solution)/shard_map/ppermute | solution.py:731
  215.4 20.7 %collective-permute-start.28 = (bf16[192,3072]{1,0:T(8,128)(2,1)S(1)}, bf16[192,3072]{1,0:T(8,128)(2,1)S(1)}, u32[]{:S(2)}, u32[]{:S(2)}) collective-permute-start(bf16[192,3072]{1,0:T(8,128)(2,1)S(1)} %constant_dynamic-update-slice_fusion.11.refs_0_), channel_id=1, source_target_pairs={{0,1},{1,0},{2,3},{3,2},{4,5},{5,4},{6,7},{7,6},{8,9},{9,8},{10,11... | collective-permute-start | bytes 3538952 | tf_op jit(solution)/shard_map/ppermute | solution.py:731
  226.2 10.7 %collective-permute-start.29 = (bf16[96,3200]{1,0:T(8,128)(2,1)S(1)}, bf16[96,3200]{1,0:T(8,128)(2,1)S(1)}, u32[]{:S(2)}, u32[]{:S(2)}) collective-permute-start(bf16[96,3200]{1,0:T(8,128)(2,1)S(1)} %add_convert_fusion.6), channel_id=1, source_target_pairs={{0,2},{1,3},{2,0},{3,1},{4,6},{5,7},{6,4},{7,5},{8,10},{9,11},{10,... | collective-permute-start | bytes 1843208 | tf_op jit(solution)/shard_map/ppermute | solution.py:731
  229.4 24.4 %collective-permute-start.35 = (bf16[192,3072]{1,0:T(8,128)(2,1)S(1)}, bf16[192,3072]{1,0:T(8,128)(2,1)S(1)}, u32[]{:S(2)}, u32[]{:S(2)}) collective-permute-start(bf16[192,3072]{1,0:T(8,128)(2,1)S(1)} %constant_dynamic-update-slice_fusion.11.refs_0_), channel_id=1, source_target_pairs={{0,16},{1,17},{2,18},{3,19},{4,20},{5,21},{6,22},{7,23},{8,24},{9,... | collective-permute-start | bytes 3538952 | tf_op jit(solution)/shard_map/ppermute | solution.py:731
  236.1 17.7 %collective-permute-start.36 = (bf16[192,3072]{1,0:T(8,128)(2,1)S(1)}, bf16[192,3072]{1,0:T(8,128)(2,1)S(1)}, u32[]{:S(2)}, u32[]{:S(2)}) collective-permute-start(bf16[192,3072]{1,0:T(8,128)(2,1)S(1)} %collective-permute-done.28.refs_1_), channel_id=1, source_target_pairs={{0,16},{1,17},{2,18},{3,19},{4,20},{5,21},{6,22},{7,23},{8,24},{9,... | collective-permute-start | bytes 3538952 | tf_op jit(solution)/shard_map/ppermute | solution.py:731
  237.0 16.8 %collective-permute-start.33 = (bf16[192,3200]{1,0:T(8,128)(2,1)S(1)}, bf16[192,3200]{1,0:T(8,128)(2,1)S(1)}, u32[]{:S(2)}, u32[]{:S(2)}) collective-permute-start(bf16[192,3200]{1,0:T(8,128)(2,1)S(1)} %constant_dynamic-update-slice_fusion.13.refs_0_), channel_id=1, source_target_pairs={{0,1},{1,0},{2,3},{3,2},{4,5},{5,4},{6,7},{7,6},{8,9},{9,8},{10,11... | collective-permute-start | bytes 3686408 | tf_op jit(solution)/shard_map/ppermute | solution.py:731
  241.3 18.9 %collective-permute-start.32 = (bf16[192,3200]{1,0:T(8,128)(2,1)S(1)}, bf16[192,3200]{1,0:T(8,128)(2,1)S(1)}, u32[]{:S(2)}, u32[]{:S(2)}) collective-permute-start(bf16[192,3200]{1,0:T(8,128)(2,1)S(1)} %constant_dynamic-update-slice_fusion.13.refs_0_), channel_id=1, source_target_pairs={{0,16},{1,17},{2,18},{3,19},{4,20},{5,21},{6,22},{7,23},{8,24},{9,... | collective-permute-start | bytes 3686408 | tf_op jit(solution)/shard_map/ppermute | solution.py:731
  253.8 6.4 %collective-permute-start.34 = (bf16[192,3200]{1,0:T(8,128)(2,1)S(1)}, bf16[192,3200]{1,0:T(8,128)(2,1)S(1)}, u32[]{:S(2)}, u32[]{:S(2)}) collective-permute-start(bf16[192,3200]{1,0:T(8,128)(2,1)S(1)} %collective-permute-done.33.refs_1_), channel_id=1, source_target_pairs={{0,16},{1,17},{2,18},{3,19},{4,20},{5,21},{6,22},{7,23},{8,24},{9,... | collective-permute-start | bytes 3686408 | tf_op jit(solution)/shard_map/ppermute | solution.py:731
where the time goes:
time: 264 us
  Pallas kernels  140 us (53%)
  waiting for transfers between devices  82.1 us (31%)
  starting transfers between devices  33.8 us (13%)
  other arithmetic  5.09 us (2%)
    ppermute x37, waiting for transfers between devices, swap(): return lax.ppermute(piece, ('stream', 'dp'), pairs)  82.1 us
    ppermute x37, starting transfers between devices, swap(): return lax.ppermute(piece, ('stream', 'dp'), pairs)  33.8 us
    pallas_call x2, Pallas kernels, ff_forward(): pl.pallas_call(functools.partial(ff_kernel, part, seq_len), grid=(hidden...  31.6 us
    pallas_call x6, Pallas kernels, spread(): pl.pallas_call(functools.partial(spread_kernel, widths, talls, first), gr...  19.1 us
    pallas_call x1, Pallas kernels, hidden_gradient(): pl.pallas_call(hidden_kernel, grid_spec=pltpu.PrefetchScalarGridSpec(num_...  14.9 us
    pallas_call x1, Pallas kernels, norm_one_backward(): pl.pallas_call(functools.partial(norm_one_kernel, seq_len), grid=(hidden...  14.4 us
    pallas_call x1, Pallas kernels, attention_forward(): pl.pallas_call(functools.partial(attention_kernel, seq_len), grid=(steps,...  14.1 us
    pallas_call x2, Pallas kernels, down_gradient(): pl.pallas_call(functools.partial(down_grad_kernel, seq_len, fresh), grid_...  11.5 us
  transfers between devices with their start and end apart: 37, of which 12 were waited for; matrix products, arithmetic and copies ran while one was open for 2% of the time, Pallas kernels for 41%

commit v1 on v0

--- a/solution.py
+++ b/solution.py
@@ -93,7 +93,7 @@
 
 
 def cost(micros):
-    return pl.CostEstimate(flops=int(micros * 3.0 * 1.15e9), bytes_accessed=1000, transcendentals=0)
+    return pl.CostEstimate(flops=int(micros * 0.02 * 1.15e9), bytes_accessed=1000, transcendentals=0)
 
 
 def two_heads(block):
@@ -218,7 +218,7 @@
 
 
 def ff_kernel(part, seq_len, nl_ref, uw, ub, dw, gain1, shift1, db, gain2, shift2, hat_far, up_far, *rest):
-    out_ref, act_ref, slope_ref, dr2_ref, low_ref, sums_ref, leads_ref, acc, hat_ref, up_ref, sems = rest[-11:]
+    out_ref, act_ref, slope_ref, low_ref, sums_ref, leads_ref, acc, hat_ref, up_ref, sems = rest[-10:]
     step = pl.program_id(0)
     rows = acc.shape[0]
     span = pl.ds(part * rows, rows)
@@ -249,7 +249,6 @@
         out_ref[...] = (hat * gain + line(shift2)).astype(low)
         grad = up_ref[...].astype(full)
         dr2 = norm_back(grad * gain, hat, inv_std)
-        dr2_ref[...] = dr2
         branch = dr2.astype(low)
         low_ref[...] = branch
         sums_ref[0, 0:1, :] = columns_sum(grad * hat)
@@ -279,14 +278,14 @@
         functools.partial(ff_kernel, part, seq_len),
         grid=(hidden // D,),
         in_specs=in_specs,
-        out_specs=[row, wide, wide, row, row, sums(8), sums(rows // seq_len)],
+        out_specs=[row, wide, wide, row, sums(8), sums(rows // seq_len)],
         scratch_shapes=[
             pltpu.VMEM((rows, D), full), pltpu.VMEM((rows, D), full), pltpu.VMEM((rows, D), low),
             pltpu.SemaphoreType.DMA((2,)),
         ],
         out_shape=[
             far(count, D), far(count, hidden), far(count, hidden),
-            far(count, D, dtype=full), far(count, D), shape_of(parts, 8, D, dtype=full),
+            far(count, D), shape_of(parts, 8, D, dtype=full),
             shape_of(parts, rows // seq_len, D, dtype=full),
         ],
         input_output_aliases=aliases,
@@ -399,14 +398,14 @@
     count, hidden = act.shape
     tall = hidden // 8
     fresh = fix is not None
-    operands = [dbranch] + ([leads, fix] if fresh else []) + [in_far(act)]
+    operands = [in_far(dbranch)] + ([leads, fix] if fresh else []) + [in_far(act)]
     moving = pl.BlockSpec((count, tall), lambda p, place: (0, place[first + p]))
     in_specs = [fixed_spec(*operand.shape) for operand in operands[:-1]] + [moving]
     out_specs = [fixed_spec(2 * tall, D)] * 2
     out_shape = [shape_of(2 * tall, D)] * 2
     if fresh:
         out_specs += [fixed_spec(count, D), fixed_spec(1, D)]
-        out_shape += [shape_of(count, D), shape_of(1, D, dtype=full)]
+        out_shape += [far(count, D), shape_of(1, D, dtype=full)]
     return pl.pallas_call(
         functools.partial(down_grad_kernel, seq_len, fresh),
         grid_spec=pltpu.PrefetchScalarGridSpec(
@@ -426,8 +425,8 @@
         outs[rank // 2][rank % 2 * tall : (rank % 2 + 1) * tall, columns] = grad_ref[pl.ds(at, tall), :]
 
 
-def hidden_kernel(place, db_ref, slope_ref, dw, nl_ref, *rest):
-    dpre_ref, sum_ref, *outs, scratch = rest[-7:]
+def hidden_kernel(place, db_ref, slope_ref, dw, nl_ref, dpre_ref, sum_ref, *rest):
+    *outs, scratch = rest
     dpre = (dot_t(db_ref[...], dw[...]) * slope_ref[...].astype(full)).astype(low)
     dpre_ref[...] = dpre
     sum_ref[0:1, :] = columns_sum(dpre.astype(full))
@@ -435,47 +434,33 @@
     put_rows(place, scratch, outs, slice(None))
 
 
-def hidden_gradient(place, part, parts, carried, dbranch, slope, dw, nl):
+def hidden_gradient(place, dbranch, slope, dw, nl):
     count, hidden = slope.shape
-    steps = hidden // D // parts
-    wide = pl.BlockSpec((count, D), lambda j, *_: (0, part * steps + j))
+    wide = pl.BlockSpec((count, D), lambda j, *_: (0, j))
     pair = D // 4
-    operands = [dbranch, in_far(slope), dw, in_far(nl)]
-    in_specs = [
-        fixed_spec(count, D), wide, pl.BlockSpec((D, D), lambda j, *_: (part * steps + j, 0)), fixed_spec(count, D)
-    ]
-    aliases = {2: 0}
-    if carried is not None:
-        operands[1] = in_far(carried[0])
-        aliases |= {5 + k: 1 + k for k in range(5)}
-        operands += list(carried[1:])
-        in_specs += [pl.BlockSpec(memory_space=pl.ANY)] * 5
-    out_specs = [wide] + [
-        pl.BlockSpec((rows, D), lambda j, *_: (0, part * steps + j)) for rows in (8, pair, pair, pair, pair)
-    ]
     return pl.pallas_call(
         hidden_kernel,
         grid_spec=pltpu.PrefetchScalarGridSpec(
             num_scalar_prefetch=1,
-            grid=(steps,),
-            in_specs=in_specs,
-            out_specs=out_specs,
+            grid=(hidden // D,),
+            in_specs=[fixed_spec(count, D), wide, pl.BlockSpec((D, D), lambda j, *_: (j, 0)), fixed_spec(count, D)],
+            out_specs=[wide] + [pl.BlockSpec((rows, D), lambda j, *_: (0, j)) for rows in (8, pair, pair, pair, pair)],
             scratch_shapes=[pltpu.VMEM((D, D), low)],
         ),
         out_shape=[far(count, hidden), shape_of(8, hidden, dtype=full)] + [shape_of(pair, hidden)] * 4,
-        input_output_aliases=aliases,
+        input_output_aliases={2: 0},
         compiler_params=params(1, 18),
-        name=f"hidden_gradient_{part}",
-        cost_estimate=cost(8),
-    )(place, *operands)
-
-
-def norm_one_kernel(seq_len, dpre_ref, fix_ref, uw, wo, gain1, dr2_far, hat_far, inv_ref,
-                    dr1_ref, datt_ref, dctx_ref, sums_ref, acc, dr2_ref, hat_ref, sems):
+        name="hidden_gradient",
+        cost_estimate=cost(15),
+    )(place, in_far(dbranch), in_far(slope), dw, in_far(nl))
+
+
+def norm_one_kernel(dpre_ref, uw, gain1, wo_far, branch_far, hat_far, inv_far,
+                    datt_ref, dctx_ref, sums_ref, acc, wo, branch_ref, hat_ref, inv_ref, sems):
     step = pl.program_id(0)
     copies = [
         pltpu.make_async_copy(source, target, sems.at[k])
-        for k, (source, target) in enumerate(((dr2_far, dr2_ref), (hat_far, hat_ref)))
+        for k, (source, target) in enumerate(((wo_far, wo), (branch_far, branch_ref), (hat_far, hat_ref), (inv_far, inv_ref)))
     ]
 
     @pl.when(step == 0)
@@ -494,14 +479,8 @@
         totals = [jnp.zeros((1, D), full)] * 3
         for start in range(0, acc.shape[0], 256):
             rows = slice(start, start + 256)
-            pieces = []
-            for s in range(start // seq_len, (start + 256) // seq_len):
-                block = dr2_ref[s * seq_len : (s + 1) * seq_len, :]
-                first = lax.broadcasted_iota(jnp.int32, block.shape, 0) == 0
-                pieces.append(block + jnp.where(first, fix_ref[s : s + 1, :], 0.0))
-            grad, hat = acc[rows, :] + jnp.concatenate(pieces, axis=0), hat_ref[rows, :]
+            grad, hat = acc[rows, :] + branch_ref[rows, :].astype(full), hat_ref[rows, :]
             dr1 = norm_back(grad * gain, hat, inv_ref[rows, 0:1])
-            dr1_ref[rows, :] = dr1
             datt = dr1.astype(low)
             datt_ref[0, rows, :] = datt
             dctx_ref[rows, :] = dot_t(datt, wo[...]).astype(low)
@@ -512,23 +491,25 @@
             sums_ref[rank : rank + 1, :] = total
 
 
-def norm_one_backward(dpre, dr2, fix, seq_len, hat, inv, uw, wo, gain1):
+def norm_one_backward(dpre, dbranch, hat, inv, uw, wo, gain1):
     count, hidden = dpre.shape
     anywhere = pl.BlockSpec(memory_space=pl.ANY)
     return pl.pallas_call(
-        functools.partial(norm_one_kernel, seq_len),
+        norm_one_kernel,
         grid=(hidden // D,),
         in_specs=[
-            pl.BlockSpec((count, D), lambda j: (0, j)), fixed_spec(*fix.shape), pl.BlockSpec((D, D), lambda j: (0, j)),
-            fixed_spec(D, D), vector_spec(), anywhere, anywhere, fixed_spec(count, LANES),
+            pl.BlockSpec((count, D), lambda j: (0, j)), pl.BlockSpec((D, D), lambda j: (0, j)), vector_spec(), anywhere, anywhere, anywhere, anywhere,
         ],
-        out_specs=[fixed_spec(count, D), pl.BlockSpec((1, count, D), lambda j: (3, 0, 0)), fixed_spec(count, D), fixed_spec(8, D)],
-        out_shape=[far(count, D, dtype=full), far(4, count, D), far(count, D), shape_of(8, D, dtype=full)],
-        scratch_shapes=[pltpu.VMEM((count, D), full)] * 3 + [pltpu.SemaphoreType.DMA((2,))],
-        compiler_params=params(1, 30),
+        out_specs=[pl.BlockSpec((1, count, D), lambda j: (3, 0, 0)), fixed_spec(count, D), fixed_spec(8, D)],
+        out_shape=[far(4, count, D), far(count, D), shape_of(8, D, dtype=full)],
+        scratch_shapes=[
+            pltpu.VMEM((count, D), full), pltpu.VMEM((D, D), low), pltpu.VMEM((count, D), low),
+            pltpu.VMEM((count, D), full), pltpu.VMEM((count, LANES), full), pltpu.SemaphoreType.DMA((4,)),
+        ],
+        compiler_params=params(1, 24),
         name="norm_one_backward",
         cost_estimate=cost(13),
-    )(in_far(dpre), fix, uw, wo, gain1, in_far(dr2), in_far(hat), in_far(inv))
+    )(in_far(dpre), uw, gain1, wo, in_far(dbranch), in_far(hat), in_far(inv))
 
 
 def attention_back_kernel(seq_len, q_ref, k_ref, v_ref, p_ref, dc_ref, stack_ref, d_ref, sums):
@@ -573,75 +554,86 @@
     )(*map(in_far, (q, k, v, probs, dctx, stack)))
 
 
-def square_grad_kernel(place, c_ref, d_ref, x_far, small_ref, *rest):
-    outs, x_ref, scratch, sem = rest[:4], rest[4], rest[5], rest[6]
+def square_grad_kernel(late, place, left_ref, d_ref, *rest):
     step = pl.program_id(0)
-    copy = pltpu.make_async_copy(x_far, x_ref, sem)
-
-    @pl.when(step == 0)
-    def _():
-        copy.start()
-        scratch[...] = t_dot(c_ref[...], d_ref[0]).astype(low)
-        tall = D // 8
-        for rank in range(8):
-            out_ref, first = outs[rank // 2], rank % 2 * tall
-            out_ref[first : first + tall, 4 * D :] = jnp.zeros((tall, LANES), low)
-
-            @pl.when(place[rank] == 0)
-            def _(out_ref=out_ref, first=first):
-                out_ref[first : first + small_ref.shape[0], 4 * D :] = small_ref[...].astype(low)
-
-    @pl.when(step == 1)
-    def _():
-        copy.wait()
-
-    @pl.when(step > 0)
-    def _():
-        scratch[...] = t_dot(x_ref[...], d_ref[0]).astype(low)
-
-    put_rows(place, scratch, outs, pl.ds(pl.multiple_of((3 - step) * D, LANES), D))
-
-
-def square_gradient(place, tokens, context, stack, small):
-    count = tokens.shape[0]
-    pair, columns = D // 4, 4 * D + LANES
+    if late:
+        far_ref, *outs, scratch, late_ref, sem = rest
+        copy = pltpu.make_async_copy(far_ref, late_ref, sem)
+
+        @pl.when(step == 0)
+        def _():
+            copy.start()
+            scratch[...] = t_dot(left_ref[...], d_ref[0]).astype(low)
+
+        @pl.when(step == 1)
+        def _():
+            copy.wait()
+            scratch[...] = t_dot(late_ref[...], d_ref[0]).astype(low)
+    else:
+        small_ref, *outs, scratch = rest
+        scratch[...] = t_dot(left_ref[...], d_ref[0]).astype(low)
+
+        @pl.when(step == 0)
+        def _():
+            tall = D // 8
+            for rank in range(8):
+                out_ref, first = outs[rank // 2], rank % 2 * tall
+                out_ref[first : first + tall, 2 * D :] = jnp.zeros((tall, LANES), low)
+
+                @pl.when(place[rank] == 0)
+                def _(out_ref=out_ref, first=first):
+                    out_ref[first : first + small_ref.shape[0], 2 * D :] = small_ref[...].astype(low)
+
+    put_rows(place, scratch, outs, pl.ds(pl.multiple_of(step * D, LANES), D))
+
+
+def square_gradient(place, lefts, stack, slots, small, name):
+    count = lefts[0].shape[0]
+    late = len(lefts) == 2
+    pair, columns = D // 4, 2 * D + (0 if late else LANES)
+    scratch = [pltpu.VMEM((D, D), low)]
+    if late:
+        scratch += [pltpu.VMEM((count, D), low), pltpu.SemaphoreType.DMA]
     return pl.pallas_call(
-        square_grad_kernel,
+        functools.partial(square_grad_kernel, late),
         grid_spec=pltpu.PrefetchScalarGridSpec(
             num_scalar_prefetch=1,
-            grid=(4,),
+            grid=(2,),
             in_specs=[
-                fixed_spec(count, D), pl.BlockSpec((1, count, D), lambda j, *_: (3 - j, 0, 0)),
-                pl.BlockSpec(memory_space=pl.ANY), fixed_spec(*small.shape),
+                fixed_spec(count, D),
+                pl.BlockSpec((1, count, D), lambda j, *_: (slots[0] + j * (slots[1] - slots[0]), 0, 0)),
+                pl.BlockSpec(memory_space=pl.ANY) if late else fixed_spec(*small.shape),
             ],
             out_specs=[fixed_spec(pair, columns)] * 4,
-            scratch_shapes=[pltpu.VMEM((count, D), low), pltpu.VMEM((D, D), low), pltpu.SemaphoreType.DMA],
+            scratch_shapes=scratch,
         ),
         out_shape=[shape_of(pair, columns)] * 4,
         compiler_params=params(1, 18),
-        name="square_gradient",
-        cost_estimate=cost(12),
-    )(place, *map(in_far, (context, stack, tokens)), small)
-
-
-def input_grad_kernel(dr1_ref, d_ref, wq, wk, wv, out_ref):
-    out_ref[...] = dr1_ref[...] + dot_t(d_ref[0], wq[...]) + dot_t(d_ref[1], wk[...]) + dot_t(d_ref[2], wv[...])
-
-
-def input_gradient(dr1, stack, wq, wk, wv):
-    count = dr1.shape[0]
+        name=name,
+        cost_estimate=cost(6),
+    )(place, in_far(lefts[0]), in_far(stack), in_far(lefts[1]) if late else small)
+
+
+def input_grad_kernel(d_ref, wq, wk, wv, out_ref):
+    out_ref[...] = (
+        d_ref[3].astype(full) + dot_t(d_ref[0], wq[...]) + dot_t(d_ref[1], wk[...]) + dot_t(d_ref[2], wv[...])
+    )
+
+
+def input_gradient(stack, wq, wk, wv):
+    count = stack.shape[1]
     rows = 256
-    row, mat = pl.BlockSpec((rows, D), lambda i: (i, 0)), fixed_spec(D, D)
+    mat = fixed_spec(D, D)
     return pl.pallas_call(
         input_grad_kernel,
         grid=(count // rows,),
-        in_specs=[row, pl.BlockSpec((3, rows, D), lambda i: (0, i, 0))] + [mat] * 3,
-        out_specs=row,
+        in_specs=[pl.BlockSpec((4, rows, D), lambda i: (0, i, 0))] + [mat] * 3,
+        out_specs=pl.BlockSpec((rows, D), lambda i: (i, 0)),
         out_shape=far(count, D, dtype=full),
         compiler_params=params(1),
         name="input_gradient",
         cost_estimate=cost(6),
-    )(in_far(dr1), in_far(stack), wq, wk, wv)
+    )(in_far(stack), wq, wk, wv)
 
 
 def spread_kernel(widths, talls, first, place, *refs):
@@ -817,32 +809,40 @@
         carried = ff_forward(
             part, parts, carried, seq_len, tie(nl, sent), hat, upstream, uw, ub, dw, g1, s1, db, g2, s2
         )
-        sent = hops.send(carried[5])
+        sent = hops.send(carried[4])
     while not isinstance(sent, tuple):
         sent = hops.send(None)
-    layer_output, act, slope, dr2, dbranch, final_sums, dr2_leads = carried
+    layer_output, act, slope, dbranch, final_sums, dr2_leads = carried
     loss_rows, fix, lead_sums = pair_loss(*sent, lead, lead_hat, lead_inv2, lead_inv, final_gain)
 
-    *down_sent, dbranch, down_sum = down_gradient(place, 4, act, dbranch, dr2_leads.reshape(-1, D), fix, seq_len)
-    sent = down_sent
+    *down_blocks, dbranch, down_sum = down_gradient(place, 4, act, dbranch, dr2_leads.reshape(-1, D), fix, seq_len)
+    sent = down_blocks
     talls = [hidden // LANES] + [D // LANES] * 8
-    down = all_sum(down_sent)
+    down = all_sum(down_blocks)
     next(down)
+    sent = (sent, down_blocks)
     down_kept = down_gradient(place, 0, act, tie(dbranch, sent))
     sent = down_kept
     sent = down.send(tie(down_kept, sent))
-    dpre, up_sums, *up_blocks = hidden_gradient(place, 0, 1, None, tie(dbranch, sent), slope, dw, nl)
+    dpre, up_sums, *up_blocks = hidden_gradient(place, tie(dbranch, sent), slope, dw, nl)
     sent = dpre
     sent = down.send(sent)
     up = all_sum(up_blocks[2:])
     next(up)
     sent = (sent, up_blocks[2:])
-    dr1, stack, dctx, mixer = norm_one_backward(tie(dpre, sent), dr2, fix, seq_len, hat, inv, uw, wo, g1)
+    stack, dctx, mixer = norm_one_backward(tie(dpre, sent), dbranch, hat, inv, uw, wo, g1)
     sent = dctx
+    sent = down.send(sent)
     sent = up.send(tie(up_blocks[:2], sent))
-    sent = down.send(sent)
     stack, qkv = attention_backward(seq_len, q, k, v, probs, tie(dctx, sent), stack)
     sent = stack
+    value_blocks = square_gradient(place, [context, tokens], tie(stack, sent), (3, 2), None, "value_gradient")
+    sent = value_blocks[2]
+    sent = down.send(sent)
+    value = all_sum(value_blocks[2:])
+    next(value)
+    sent = (sent, value_blocks[2:])
+    sent = up.send(sent)
     final = jnp.sum(final_sums, axis=0)
     small = jnp.concatenate(
         [
@@ -850,49 +850,60 @@
             final[1] + lead_sums[1], qkv[0], qkv[2],
         ]
     ).reshape(-1, LANES)
-    square_blocks = square_gradient(place, tokens, context, tie(stack, sent), small)
-    sent = square_blocks[2]
+    query_blocks = square_gradient(place, [tokens], tie(stack, sent), (0, 1), small, "query_gradient")
+    sent = query_blocks[2]
+    sent = value.send(tie(value_blocks[:2], sent))
+    sent = up.send(sent)
+    query = all_sum(query_blocks[2:])
+    next(query)
+    sent = (sent, query_blocks[2:])
     sent = down.send(sent)
-    sent = up.send(sent)
-    square = all_sum(square_blocks[2:])
-    next(square)
-    sent = (sent, square_blocks[2:])
-    sent = square.send(tie(square_blocks[:2], sent))
-    sent = up.send(sent)
-    input_grad = input_gradient(tie(dr1, sent), stack, wq, wk, wv)
-    sent = input_grad
-    sent = down.send(sent)
-    sent = square.send(sent)
+    sent = query.send(tie(query_blocks[:2], sent))
+    sent = value.send(sent)
     sent = up.send(sent)
     sent = down.send(sent)
-    sent = square.send(sent)
+    input_grad = input_gradient(tie(stack, sent), wq, wk, wv)
+    sent = input_grad
+    sent = value.send(sent)
+    sent = query.send(sent)
     sent = up.send(sent)
     down_own = down.send(sent)
     sent = down_own
-    sent = square.send(sent)
-    sent = up.send(sent)
+    sent = value.send(sent)
     down_out = spread(place, 0, tie(down_own, sent), [D], [], None, "down")
     sent = down_out
-    sent = square.send(sent)
+    sent = query.send(sent)
+    sent = up.send(sent)
+    sent = query.send(sent)
+    sent = value.send(sent)
+    sent = query.send(sent)
+    down_out = spread(place, 4, down.send(sent), [D], [], down_out, "down")
+    sent = down_out
     up_own = up.send(sent)
     sent = up_own
-    sent = square.send(sent)
+    sent = value.send(sent)
     up_out = spread(place, 0, tie(up_own, sent), [hidden], [], None, "up")
     sent = up_out
+    sent = query.send(sent)
     up_out = spread(place, 4, up.send(sent), [hidden], [], up_out, "up")
     sent = up_out
-    down_out = spread(place, 4, down.send(sent), [D], [], down_out, "down")
-    sent = down_out
-    square_own = square.send(sent)
-    sent = square_own
-    squares = spread(place, 0, tie(square_own, sent), [D] * 4, talls, None, "square")
-    sent = squares
-    squares = spread(place, 4, square.send(sent), [D] * 4, talls, squares, "square")
-    wq_grad, wk_grad, wv_grad, wo_grad, *smalls = squares
+    value_own = value.send(sent)
+    sent = value_own
+    value_out = spread(place, 0, tie(value_own, sent), [D] * 2, [], None, "value")
+    sent = value_out
+    value_out = spread(place, 4, value.send(sent), [D] * 2, [], value_out, "value")
+    sent = value_out
+    query_own = query.send(sent)
+    sent = query_own
+    query_out = spread(place, 0, tie(query_own, sent), [D] * 2, talls, None, "query")
+    sent = query_out
+    query_out = spread(place, 4, query.send(sent), [D] * 2, talls, query_out, "query")
+    sent = query_out
+    wq_grad, wk_grad, *smalls = query_out
     up_b, out_b, gain_one, shift_one, down_b, gain_two, shift_two, query_b, value_b = (each.reshape(-1) for each in smalls)
     return (
         layer_output[None], input_grad[None], loss_rows,
-        wq_grad, query_b, wk_grad, wv_grad, value_b, wo_grad, out_b,
+        wq_grad, query_b, wk_grad, value_out[1], value_b, value_out[0], out_b,
         gain_one, shift_one, up_out[0], up_b, down_out[0], down_b, gain_two, shift_two,
     )
 

time: 264 us -> 267 us (1.011); the launches traced: 264 us -> 263 us
  waiting for transfers between devices: 82.1 us -> 34.9 us
  starting transfers between devices: 33.8 us -> 62.2 us
  Pallas kernels: 140 us -> 154 us
  other arithmetic: 5.09 us -> 8.61 us
    ppermute x37 -> x47, waiting for transfers between devices: 82.1 us -> 34.9 us  [swap(): return lax.ppermute(piece, ('stream', 'dp'), pairs)]
    ppermute x37 -> x47, starting transfers between devices: 33.8 us -> 62.2 us  [swap(): return lax.ppermute(piece, ('stream', 'dp'), pairs)]
    pallas_call x3 -> x4, Pallas kernels: 32.1 us -> 41.6 us  [the longest x2 20.3 us: square_gradient(): pl.pallas_call(functools.partial(square_grad_kernel, late), grid_spec=plt...]
    pallas_call x6 -> x8, Pallas kernels: 19.1 us -> 22.7 us  [spread(): pl.pallas_call(functools.partial(spread_kernel, widths, talls, first), gr...]
    convert_element_type x18 -> x24, other arithmetic: 4.38 us -> 7.9 us  [add_low(): return (left.astype(full) + right.astype(full)).astype(low)]
  transfers between devices with their start and end apart: 37 -> 47, of which waited for: 12 -> 10; matrix products, arithmetic and copies ran while one was open for 2% -> 3% of each run, Pallas kernels for 41% -> 47%
where the time goes in v1:
time: 267 us; the launch traced here: 263 us
  Pallas kernels  154 us (58%)
  starting transfers between devices  62.2 us (23%)
  waiting for transfers between devices  34.9 us (13%)
  other arithmetic  8.61 us (3%)
    ppermute x47, starting transfers between devices, swap(): return lax.ppermute(piece, ('stream', 'dp'), pairs)  62.2 us
    ppermute x47, waiting for transfers between devices, swap(): return lax.ppermute(piece, ('stream', 'dp'), pairs)  34.9 us
    pallas_call x2, Pallas kernels, ff_forward(): pl.pallas_call(functools.partial(ff_kernel, part, seq_len), grid=(hidden...  30.5 us
    pallas_call x8, Pallas kernels, spread(): pl.pallas_call(functools.partial(spread_kernel, widths, talls, first), gr...  22.7 us
    pallas_call x2, Pallas kernels, square_gradient(): pl.pallas_call(functools.partial(square_grad_kernel, late), grid_spec=plt...  20.3 us
    pallas_call x1, Pallas kernels, hidden_gradient(): pl.pallas_call(hidden_kernel, grid_spec=pltpu.PrefetchScalarGridSpec(num_...  14.8 us
    pallas_call x1, Pallas kernels, attention_forward(): pl.pallas_call(functools.partial(attention_kernel, seq_len), grid=(steps,...  14.1 us
    pallas_call x2, Pallas kernels, down_gradient(): pl.pallas_call(functools.partial(down_grad_kernel, seq_len, fresh), grid_...  13.8 us
  transfers between devices with their start and end apart: 47, of which 10 were waited for; matrix products, arithmetic and copies ran while one was open for 3% of the time, Pallas kernels for 47%

profile of v1, /device:TPU:0, one launch (start us, length us, event | category | flops | bytes accessed | tf_op | source)
XLA Modules:
  0.0 262.7 jit_solution(1524692774607764721)
XLA Ops:
  1.3 14.1 %attention_forward.1 = (bf16[1024,768]{1,0:T(8,128)(2,1)}, bf16[1024,768]{1,0:T(8,128)(2,1)}, bf16[1024,768]{1,0:T(8,128)(2,1)}, bf16[1024,768]{1,0:T(8,128)(2,1...) custom-call(bf16[1024,768]{1,0:T(8,128)(2,1)} %bitcast.36, ...), custom_call_target="tpu_custom_call" | custom-call | flops 230000000 | bytes 1000 | tf_op jit(solution)/shard_map/attention_forward/pallas_call | solution.py:160
  15.5 5.7 %lead_forward.1 = (f32[16,768]{1,0:T(8,128)S(1)}, f32[16,768]{1,0:T(8,128)S(1)}, f32[16,128]{1,0:T(8,128)S(1)}, f32[16,128]{1,0:T(8,128)S(1)}, bf16[16,768]{1,0:T(8,128)(2,1)S(1)}) custom-call(f32[4,4,768]{2,1,0:T(4,128)S(1)} %get-tuple-element.149.nl_ref, f32[4,4,768]{2,1,0:T(4,128)S(1)} %get-tuple-element.150.hat_ref, bf16[768,3072]{1,0:T(8,128)(2,1)} %uw.7, ...), custom_call_target="tpu_custom_call" | custom-call | flops 69000000 | bytes 1000 | tf_op jit(solution)/shard_map/lead_forward/pallas_call | solution.py:203
  21.3 2.9 %collective-permute-start = (bf16[16,896]{1,0:T(8,128)(2,1)S(1)}, bf16[16,896]{1,0:T(8,128)(2,1)S(1)}, u32[]{:S(2)}, u32[]{:S(2)}) collective-permute-start(bf16[16,896]{1,0:T(8,128)(2,1)S(1)} %pad_maximum_fusion), channel_id=1, source_target_pairs={{0,1},{1,0},{2,3},{3,2},{4,5},{5,4},{6,7},{7,6},{8,9},{9,8},{10,11... | collective-permute-start | bytes 86024 | tf_op jit(solution)/shard_map/ppermute | solution.py:723
  25.8 15.3 %ff_forward_0.1 = (bf16[1024,768]{1,0:T(8,128)(2,1)}, bf16[1024,3072]{1,0:T(8,128)(2,1)}, bf16[1024,3072]{1,0:T(8,128)(2,1)}, bf16[1024,768]{1,0:T(8,128)(2,1)},...) custom-call(bf16[1024,768]{1,0:T(8,128)(2,1)} %get-tuple-element.156.nl_ref, bf16[768,3072]{1,0:T(8,128)(2,1)} %uw.7, ...), custom_call_target="tpu_custom_call" | custom-call | flops 299000000 | bytes 1000 | tf_op jit(solution)/shard_map/ff_forward_0/pallas_call | solution.py:277
  41.2 2.1 collective-permute-start.3
  43.2 2.6 collective-permute-start.4
  45.8 15.2 %ff_forward_1.1 = (bf16[1024,768]{1,0:T(8,128)(2,1)}, bf16[1024,3072]{1,0:T(8,128)(2,1)}, bf16[1024,3072]{1,0:T(8,128)(2,1)}, bf16[1024,768]{1,0:T(8,128)(2,1)},...) custom-call(bf16[1024,768]{1,0:T(8,128)(2,1)} %get-tuple-element.156, ...), custom_call_target="tpu_custom_call", output_to_operand_aliasing={{0}: (11, {}), {1}: (12, {}), {2}: (13, {}), {3}: (14, {}),... | custom-call | flops 299000000 | bytes 1000 | tf_op jit(solution)/shard_map/ff_forward_1/pallas_call | solution.py:277
  61.4 1.7 collective-permute-done.6.other_ref
  63.1 1.8 pair_loss.1
  64.8 7.6 %down_grad_4.1 = (bf16[768,768]{1,0:T(8,128)(2,1)S(1)}, bf16[768,768]{1,0:T(8,128)(2,1)S(1)}, bf16[1024,768]{1,0:T(8,128)(2,1)}, f32[1,768]{1,0:T(1,128)S(1)}) custom-call(s32[8]{0:T(128)S(1)} %stack.35.place, bf16[1024,768]{1,0:T(8,128)(2,1)} %get-tuple-element.167.refs_0_, f32[16,768]{1,0:T(8,128)S(1)} %bitcast.34, ...), custom_call_target="tpu_custom_call" | custom-call | flops 92000000 | bytes 1000 | tf_op jit(solution)/shard_map/down_grad_4/pallas_call | solution.py:409
  73.0 6.1 %down_grad_0.1 = (bf16[768,768]{1,0:T(8,128)(2,1)S(1)}, bf16[768,768]{1,0:T(8,128)(2,1)S(1)}) custom-call(s32[8]{0:T(128)S(1)} %stack.35.place, bf16[1024,768]{1,0:T(8,128)(2,1)} %get-tuple-element.182.refs_0_.db_ref.branch_far, bf16[1024,3072]{1,0:T(8,128)(2,1)} %get-tuple-element.176.refs_3_.refs_1_), custom_call_target="tpu_custom_call" | custom-call | flops 92000000 | bytes 1000 | tf_op jit(solution)/shard_map/down_grad_0/pallas_call | solution.py:409
  80.4 1.7 collective-permute-start.9
  82.1 14.8 %hidden_gradient.1 = (bf16[1024,3072]{1,0:T(8,128)(2,1)}, f32[8,3072]{1,0:T(8,128)S(1)}, bf16[192,3072]{1,0:T(8,128)(2,1)S(1)}, bf16[192,3072]{1,0:T(8,128)(2,1)...) custom-call(s32[8]{0:T(128)S(1)} %stack.35.place, ...), custom_call_target="tpu_custom_call", output_to_operand_aliasing={{0}: (2, {})} | custom-call | flops 345000000 | bytes 1000 | tf_op jit(solution)/shard_map/hidden_gradient/pallas_call | solution.py:441
  97.0 1.6 add_convert_fusion.2
  99.1 1.6 add_convert_fusion.16
  100.7 1.6 collective-permute-start.10
  102.3 12.8 %norm_one_backward.1 = (bf16[4,1024,768]{2,1,0:T(8,128)(2,1)}, bf16[1024,768]{1,0:T(8,128)(2,1)}, f32[8,768]{1,0:T(8,128)S(1)}) custom-call(bf16[1024,3072]{1,0:T(8,128)(2,1)} %get-tuple-element.189.dpre_ref, bf16[768,3072]{1,0:T(8,128)(2,1)} %uw.7, f32[6,128]{1,0:T(8,128)} %bitcast.50, bf16[768,768]{1,0:T(8,128)(2,1)} %wo_far.1, ...), custom_call_target="tpu_custom_call" | custom-call | flops 299000000 | bytes 1000 | tf_op jit(solution)/shard_map/norm_one_backward/pallas_call | solution.py:497
  117.1 9.2 %attention_backward.1 = (bf16[4,1024,768]{2,1,0:T(8,128)(2,1)}, f32[8,768]{1,0:T(8,128)S(1)}) custom-call(bf16[1024,768]{1,0:T(8,128)(2,1)} %get-tuple-element.163.q_ref, bf16[1024,768]{1,0:T(8,128)(2,1)} %get-tuple-element.164.k_ref, bf16[1024,768]{1,0:T(8,128)(2,1)} %get-tuple-element.165.v_ref, ...), custom_call_target="tpu_custom_call", output_to_operand_aliasing={{0}: (5, {})} | custom-call | flops 184000000 | bytes 1000 | tf_op jit(solution)/shard_map/attention_backward/pallas_call | solution.py:544
  126.3 14.7 %value_gradient.1 = (bf16[192,1536]{1,0:T(8,128)(2,1)S(1)}, bf16[192,1536]{1,0:T(8,128)(2,1)S(1)}, bf16[192,1536]{1,0:T(8,128)(2,1)S(1)}, bf16[192,1536]{1,0:T(8,128)(2,1)S(1)}) custom-call(s32[8]{0:T(128)S(1)} %stack.35.place, bf16[1024,768]{1,0:T(8,128)(2,1)} %get-tuple-element.199.left_ref, bf16[4,1024,768]{2,1,0:T(8,128)(2,1)} %get-tuple-element.226.d_ref, ...), custom_call_target="tpu_custom_call" | custom-call | flops 138000000 | bytes 1000 | tf_op jit(solution)/shard_map/value_gradient/pallas_call | solution.py:597
  142.3 3.6 %collective-permute-start.17 = (bf16[384,768]{1,0:T(8,128)(2,1)S(1)}, bf16[384,768]{1,0:T(8,128)(2,1)S(1)}, u32[]{:S(2)}, u32[]{:S(2)}) collective-permute-start(bf16[384,768]{1,0:T(8,128)(2,1)S(1)} %add_convert_fusion.14), channel_id=1, source_target_pairs={{0,8},{1,9},{2,10},{3,11},{4,12},{5,13},{6,14},{7,15},{8,0},{9,1},... | collective-permute-start | bytes 1769480 | tf_op jit(solution)/shard_map/ppermute | solution.py:723
  147.2 5.6 %query_gradient.1 = (bf16[192,1664]{1,0:T(8,128)(2,1)S(1)}, bf16[192,1664]{1,0:T(8,128)(2,1)S(1)}, bf16[192,1664]{1,0:T(8,128)(2,1)S(1)}, bf16[192,1664]{1,0:T(8,128)(2,1)S(1)}) custom-call(s32[8]{0:T(128)S(1)} %stack.35.place, bf16[1024,768]{1,0:T(8,128)(2,1)} %bitcast.38, bf16[4,1024,768]{2,1,0:T(8,128)(2,1)} %get-tuple-element.226.d_ref, ...), custom_call_target="tpu_custom_call" | custom-call | flops 138000000 | bytes 1000 | tf_op jit(solution)/shard_map/query_gradient/pallas_call | solution.py:597
  154.6 1.6 collective-permute-done.16
  156.4 3.2 %collective-permute-done.17 = bf16[384,768]{1,0:T(8,128)(2,1)S(1)} collective-permute-done((bf16[384,768]{1,0:T(8,128)(2,1)S(1)}, bf16[384,768]{1,0:T(8,128)(2,1)S(1)}, u32[]{:S(2)}, u32[]{:S(2)}) %collective-permute-start.17) | collective-permute-done | bytes 589856 | tf_op jit(solution)/shard_map/ppermute | solution.py:723
  160.9 3.9 %collective-permute-done.20 = bf16[192,1536]{1,0:T(8,128)(2,1)S(1)} collective-permute-done((bf16[192,1536]{1,0:T(8,128)(2,1)S(1)}, bf16[192,1536]{1,0:T(8,128)(2,1)S(1)}, u32[]{:S(2)}, u32[]{:S(2)}) %collective-permute-start.20) | collective-permute-done | bytes 589856 | tf_op jit(solution)/shard_map/ppermute | solution.py:723
  165.7 2.5 collective-permute-start.25
  168.4 3.1 %collective-permute-done.21 = bf16[96,3072]{1,0:T(8,128)(2,1)S(1)} collective-permute-done((bf16[96,3072]{1,0:T(8,128)(2,1)S(1)}, bf16[96,3072]{1,0:T(8,128)(2,1)S(1)}, u32[]{:S(2)}, u32[]{:S(2)}) %collective-permute-start.21) | collective-permute-done | bytes 589856 | tf_op jit(solution)/shard_map/ppermute | solution.py:723
  171.7 2.3 collective-permute-start.26
  175.6 8.5 %input_gradient.1 = f32[1024,768]{1,0:T(8,128)} custom-call(bf16[4,1024,768]{2,1,0:T(8,128)(2,1)} %get-tuple-element.226.d_ref, bf16[768,768]{1,0:T(8,128)(2,1)} %wq.3, bf16[768,768]{1,0:T(8,128)(2,1)} %wk.3, bf16[768,768]{1,0:T(8,128)(2,1)} %wv.3), custom_call_target="tpu_custom_call" | custom-call | flops 138000000 | bytes 1000 | tf_op jit(solution)/shard_map/input_gradient/pallas_call | solution.py:627
  184.2 4.0 %collective-permute-start.28 = (bf16[96,1536]{1,0:T(8,128)(2,1)S(1)}, bf16[96,1536]{1,0:T(8,128)(2,1)S(1)}, u32[]{:S(2)}, u32[]{:S(2)}) collective-permute-start(bf16[96,1536]{1,0:T(8,128)(2,1)S(1)} %add_convert_fusion.25), channel_id=1, source_target_pairs={{0,4},{1,5},{2,6},{3,7},{4,0},{5,1},{6,2},{7,3},{8,12},{9,13},{10,... | collective-permute-start | bytes 884744 | tf_op jit(solution)/shard_map/ppermute | solution.py:723
  188.5 4.6 %collective-permute-done.26 = bf16[96,3072]{1,0:T(8,128)(2,1)S(1)} collective-permute-done((bf16[96,3072]{1,0:T(8,128)(2,1)S(1)}, bf16[96,3072]{1,0:T(8,128)(2,1)S(1)}, u32[]{:S(2)}, u32[]{:S(2)}) %collective-permute-start.26) | collective-permute-done | bytes 589856 | tf_op jit(solution)/shard_map/ppermute | solution.py:723
  193.4 3.0 %collective-permute-done.27.refs_1_ = bf16[768,768]{1,0:T(8,128)(2,1)S(1)} collective-permute-done((bf16[768,768]{1,0:T(8,128)(2,1)S(1)}, bf16[768,768]{1,0:T(8,128)(2,1)S(1)}, u32[]{:S(2)}, u32[]{:S(2)}) %collective-permute-start.27) | collective-permute-done | bytes 1179680 | tf_op jit(solution)/shard_map/ppermute | solution.py:723
  196.5 3.2 %down_spread_0.1.refs_2_ = f32[3072,768]{1,0:T(8,128)} custom-call(s32[8]{0:T(128)S(1)} %stack.35.place, bf16[768,768]{1,0:T(8,128)(2,1)S(1)} %constant_dynamic-update-slice_fusion.9.refs_0_, bf16[768,768]{1,0:T(8,128)(2,1)S(1)} %collective-permute-done.27.refs_1_), custom_call_target="tpu_custom_call" | custom-call | flops 69000000 | bytes 1000 | tf_op jit(solution)/shard_map/down_spread_0/pallas_call | solution.py:679
  199.7 3.9 %collective-permute-start.31 = (bf16[96,1664]{1,0:T(8,128)(2,1)S(1)}, bf16[96,1664]{1,0:T(8,128)(2,1)S(1)}, u32[]{:S(2)}, u32[]{:S(2)}) collective-permute-start(bf16[96,1664]{1,0:T(8,128)(2,1)S(1)} %add_convert_fusion.20), channel_id=1, source_target_pairs={{0,4},{1,5},{2,6},{3,7},{4,0},{5,1},{6,2},{7,3},{8,12},{9,13},{10,... | collective-permute-start | bytes 958472 | tf_op jit(solution)/shard_map/ppermute | solution.py:723
  203.7 2.5 collective-permute-start.36
  206.2 6.5 %collective-permute-start.32 = (bf16[96,1536]{1,0:T(8,128)(2,1)S(1)}, bf16[96,1536]{1,0:T(8,128)(2,1)S(1)}, u32[]{:S(2)}, u32[]{:S(2)}) collective-permute-start(bf16[96,1536]{1,0:T(8,128)(2,1)S(1)} %add_convert_fusion.24), channel_id=1, source_target_pairs={{0,8},{1,9},{2,10},{3,11},{4,12},{5,13},{6,14},{7,15},{8,0},{9,1},... | collective-permute-start | bytes 884744 | tf_op jit(solution)/shard_map/ppermute | solution.py:723
  212.9 7.8 %collective-permute-start.33 = (bf16[96,1664]{1,0:T(8,128)(2,1)S(1)}, bf16[96,1664]{1,0:T(8,128)(2,1)S(1)}, u32[]{:S(2)}, u32[]{:S(2)}) collective-permute-start(bf16[96,1664]{1,0:T(8,128)(2,1)S(1)} %add_convert_fusion.19), channel_id=1, source_target_pairs={{0,8},{1,9},{2,10},{3,11},{4,12},{5,13},{6,14},{7,15},{8,0},{9,1},... | collective-permute-start | bytes 958472 | tf_op jit(solution)/shard_map/ppermute | solution.py:723
  220.8 3.2 %down_spread_4.1 = f32[3072,768]{1,0:T(8,128)} custom-call(s32[8]{0:T(128)S(1)} %stack.35.place, bf16[768,768]{1,0:T(8,128)(2,1)S(1)} %collective-permute-done.34.refs_0_, bf16[768,768]{1,0:T(8,128)(2,1)S(1)} %collective-permute-done.35.refs_1_, f32[3072,768]{1,0:T(8,128)} %down_spread_0.1.refs_2_), custom_call_target="tpu_custom_call", output_to_operand_aliasing={{}: (3, {})} | custom-call | flops 69000000 | bytes 1000 | tf_op jit(solution)/shard_map/down_spread_4/pallas_call | solution.py:679
  224.5 4.7 %collective-permute-done.33 = bf16[96,1664]{1,0:T(8,128)(2,1)S(1)} collective-permute-done((bf16[96,1664]{1,0:T(8,128)(2,1)S(1)}, bf16[96,1664]{1,0:T(8,128)(2,1)S(1)}, u32[]{:S(2)}, u32[]{:S(2)}) %collective-permute-start.33) | collective-permute-done | bytes 319520 | tf_op jit(solution)/shard_map/ppermute | solution.py:723
  229.5 3.0 %collective-permute-start.42 = (bf16[192,1536]{1,0:T(8,128)(2,1)S(1)}, bf16[192,1536]{1,0:T(8,128)(2,1)S(1)}, u32[]{:S(2)}, u32[]{:S(2)}) collective-permute-start(bf16[192,1536]{1,0:T(8,128)(2,1)S(1)} %constant_dynamic-update-slice_fusion.13.refs_0_), channel_id=1, source_target_pairs={{0,1},{1,0},{2,3},{3,2},{4,5},{5,4},{6,7},{7,6},{8,9},{9,8},{10,11... | collective-permute-start | bytes 1769480 | tf_op jit(solution)/shard_map/ppermute | solution.py:723
  232.4 3.2 %up_spread_0.1.refs_2_ = f32[768,3072]{1,0:T(8,128)} custom-call(s32[8]{0:T(128)S(1)} %stack.35.place, bf16[192,3072]{1,0:T(8,128)(2,1)S(1)} %constant_dynamic-update-slice_fusion.11.refs_0_, bf16[192,3072]{1,0:T(8,128)(2,1)S(1)} %collective-permute-done.36.refs_1_), custom_call_target="tpu_custom_call" | custom-call | flops 69000000 | bytes 1000 | tf_op jit(solution)/shard_map/up_spread_0/pallas_call | solution.py:679
  235.6 4.2 %collective-permute-done.38 = bf16[96,1664]{1,0:T(8,128)(2,1)S(1)} collective-permute-done((bf16[96,1664]{1,0:T(8,128)(2,1)S(1)}, bf16[96,1664]{1,0:T(8,128)(2,1)S(1)}, u32[]{:S(2)}, u32[]{:S(2)}) %collective-permute-start.38) | collective-permute-done | bytes 319520 | tf_op jit(solution)/shard_map/ppermute | solution.py:723
  239.9 3.0 %collective-permute-start.45 = (bf16[192,1664]{1,0:T(8,128)(2,1)S(1)}, bf16[192,1664]{1,0:T(8,128)(2,1)S(1)}, u32[]{:S(2)}, u32[]{:S(2)}) collective-permute-start(bf16[192,1664]{1,0:T(8,128)(2,1)S(1)} %constant_dynamic-update-slice_fusion.15.refs_0_), channel_id=1, source_target_pairs={{0,1},{1,0},{2,3},{3,2},{4,5},{5,4},{6,7},{7,6},{8,9},{9,8},{10,11... | collective-permute-start | bytes 1916936 | tf_op jit(solution)/shard_map/ppermute | solution.py:723
  242.9 3.2 %up_spread_4.1 = f32[768,3072]{1,0:T(8,128)} custom-call(s32[8]{0:T(128)S(1)} %stack.35.place, bf16[192,3072]{1,0:T(8,128)(2,1)S(1)} %collective-permute-done.39.refs_0_, bf16[192,3072]{1,0:T(8,128)(2,1)S(1)} %collective-permute-done.40.refs_1_, f32[768,3072]{1,0:T(8,128)} %up_spread_0.1.refs_2_), custom_call_target="tpu_custom_call", output_to_operand_aliasing={{}: (3, {})} | custom-call | flops 69000000 | bytes 1000 | tf_op jit(solution)/shard_map/up_spread_4/pallas_call | solution.py:679
  246.6 4.7 %collective-permute-done.45.refs_1_ = bf16[192,1664]{1,0:T(8,128)(2,1)S(1)} collective-permute-done((bf16[192,1664]{1,0:T(8,128)(2,1)S(1)}, bf16[192,1664]{1,0:T(8,128)(2,1)S(1)}, u32[]{:S(2)}, u32[]{:S(2)}) %collective-permute-start.45) | collective-permute-done | bytes 639008 | tf_op jit(solution)/shard_map/ppermute | solution.py:723
  251.3 2.5 value_spread_0.1
  253.8 2.5 value_spread_4.1
  257.4 2.5 query_spread_0.1
  259.9 2.6 query_spread_4.1
  (126 shorter events, 19.1 us)
Async XLA Ops:
  21.3 19.8 %collective-permute-start = (bf16[16,896]{1,0:T(8,128)(2,1)S(1)}, bf16[16,896]{1,0:T(8,128)(2,1)S(1)}, u32[]{:S(2)}, u32[]{:S(2)}) collective-permute-start(bf16[16,896]{1,0:T(8,128)(2,1)S(1)} %pad_maximum_fusion), channel_id=1, source_target_pairs={{0,1},{1,0},{2,3},{3,2},{4,5},{5,4},{6,7},{7,6},{8,9},{9,8},{10,11... | collective-permute-start | bytes 86024 | tf_op jit(solution)/shard_map/ppermute | solution.py:723
  24.2 16.9 %collective-permute-start.1 = (bf16[16,896]{1,0:T(8,128)(2,1)S(1)}, bf16[16,896]{1,0:T(8,128)(2,1)S(1)}, u32[]{:S(2)}, u32[]{:S(2)}) collective-permute-start(bf16[16,896]{1,0:T(8,128)(2,1)S(1)} %pad_maximum_fusion), channel_id=1, source_target_pairs={{0,2},{1,3},{2,0},{3,1},{4,6},{5,7},{6,4},{7,5},{8,10},{9,11},{10,... | collective-permute-start | bytes 86024 | tf_op jit(solution)/shard_map/ppermute | solution.py:723
  25.7 15.4 %collective-permute-start.2 = (bf16[16,896]{1,0:T(8,128)(2,1)S(1)}, bf16[16,896]{1,0:T(8,128)(2,1)S(1)}, u32[]{:S(2)}, u32[]{:S(2)}) collective-permute-start(bf16[16,896]{1,0:T(8,128)(2,1)S(1)} %pad_maximum_fusion), channel_id=1, source_target_pairs={{0,3},{1,2},{2,1},{3,0},{4,7},{5,6},{6,5},{7,4},{8,11},{9,10},{10,... | collective-permute-start | bytes 86024 | tf_op jit(solution)/shard_map/ppermute | solution.py:723
  41.2 19.9 %collective-permute-start.3 = (bf16[64,896]{1,0:T(8,128)(2,1)S(1)}, bf16[64,896]{1,0:T(8,128)(2,1)S(1)}, u32[]{:S(2)}, u32[]{:S(2)}) collective-permute-start(bf16[64,896]{1,0:T(8,128)(2,1)S(1)} %constant_dynamic-update-slice_fusion), channel_id=1, source_target_pairs={{0,4},{1,5},{2,6},{3,7},{4,0},{5,1},{6,2},{7,3},{8,12},{9,13},{10,... | collective-permute-start | bytes 344072 | tf_op jit(solution)/shard_map/ppermute | solution.py:723
  43.2 17.9 %collective-permute-start.4 = (bf16[64,896]{1,0:T(8,128)(2,1)S(1)}, bf16[64,896]{1,0:T(8,128)(2,1)S(1)}, u32[]{:S(2)}, u32[]{:S(2)}) collective-permute-start(bf16[64,896]{1,0:T(8,128)(2,1)S(1)} %constant_dynamic-update-slice_fusion), channel_id=1, source_target_pairs={{0,8},{1,9},{2,10},{3,11},{4,12},{5,13},{6,14},{7,15},{8,0},{9,1},... | collective-permute-start | bytes 344072 | tf_op jit(solution)/shard_map/ppermute | solution.py:723
  45.8 15.3 %collective-permute-start.5 = (bf16[64,896]{1,0:T(8,128)(2,1)S(1)}, bf16[64,896]{1,0:T(8,128)(2,1)S(1)}, u32[]{:S(2)}, u32[]{:S(2)}) collective-permute-start(bf16[64,896]{1,0:T(8,128)(2,1)S(1)} %constant_dynamic-update-slice_fusion), channel_id=1, source_target_pairs={{0,12},{1,13},{2,14},{3,15},{4,8},{5,9},{6,10},{7,11},{8,4},{9,5},... | collective-permute-start | bytes 344072 | tf_op jit(solution)/shard_map/ppermute | solution.py:723
  61.2 1.9 collective-permute-start.6
  72.5 6.6 %collective-permute-start.7 = (bf16[768,768]{1,0:T(8,128)(2,1)S(1)}, bf16[768,768]{1,0:T(8,128)(2,1)S(1)}, u32[]{:S(2)}, u32[]{:S(2)}) collective-permute-start(bf16[768,768]{1,0:T(8,128)(2,1)S(1)} %get-tuple-element.179), channel_id=1, source_target_pairs={{0,16},{1,17},{2,18},{3,19},{4,20},{5,21},{6,22},{7,23},{8,24},{9,... | collective-permute-start | bytes 3538952 | tf_op jit(solution)/shard_map/ppermute | solution.py:723
  72.6 24.4 %collective-permute-start.8 = (bf16[768,768]{1,0:T(8,128)(2,1)S(1)}, bf16[768,768]{1,0:T(8,128)(2,1)}, u32[]{:S(2)}, u32[]{:S(2)}) collective-permute-start(bf16[768,768]{1,0:T(8,128)(2,1)S(1)} %get-tuple-element.178), channel_id=1, source_target_pairs={{0,16},{1,17},{2,18},{3,19},{4,20},{5,21},{6,22},{7,23},{8,24},{9,... | collective-permute-start | bytes 3538952 | tf_op jit(solution)/shard_map/ppermute | solution.py:723
  80.4 18.7 %collective-permute-start.9 = (bf16[768,768]{1,0:T(8,128)(2,1)}, bf16[768,768]{1,0:T(8,128)(2,1)}, u32[]{:S(2)}, u32[]{:S(2)}) collective-permute-start(bf16[768,768]{1,0:T(8,128)(2,1)} %add_convert_fusion.3), channel_id=1, source_target_pairs={{0,1},{1,0},{2,3},{3,2},{4,5},{5,4},{6,7},{7,6},{8,9},{9,8},{10,11... | collective-permute-start | bytes 3538952 | tf_op jit(solution)/shard_map/ppermute | solution.py:723
  98.6 17.5 %collective-permute-start.11 = (bf16[192,3072]{1,0:T(8,128)(2,1)S(1)}, bf16[192,3072]{1,0:T(8,128)(2,1)S(1)}, u32[]{:S(2)}, u32[]{:S(2)}) collective-permute-start(bf16[192,3072]{1,0:T(8,128)(2,1)S(1)} %get-tuple-element.188), channel_id=1, source_target_pairs={{0,16},{1,17},{2,18},{3,19},{4,20},{5,21},{6,22},{7,23},{8,24},{9,... | collective-permute-start | bytes 3538952 | tf_op jit(solution)/shard_map/ppermute | solution.py:723
  98.6 43.0 %collective-permute-start.13 = (bf16[192,3072]{1,0:T(8,128)(2,1)S(1)}, bf16[192,3072]{1,0:T(8,128)(2,1)S(1)}, u32[]{:S(2)}, u32[]{:S(2)}) collective-permute-start(bf16[192,3072]{1,0:T(8,128)(2,1)S(1)} %get-tuple-element.187), channel_id=1, source_target_pairs={{0,16},{1,17},{2,18},{3,19},{4,20},{5,21},{6,22},{7,23},{8,24},{9,... | collective-permute-start | bytes 3538952 | tf_op jit(solution)/shard_map/ppermute | solution.py:723
  100.7 14.5 %collective-permute-start.10 = (bf16[384,768]{1,0:T(8,128)(2,1)S(1)}, bf16[384,768]{1,0:T(8,128)(2,1)S(1)}, u32[]{:S(2)}, u32[]{:S(2)}) collective-permute-start(bf16[384,768]{1,0:T(8,128)(2,1)S(1)} %get-tuple-element.289), channel_id=1, source_target_pairs={{0,2},{1,3},{2,0},{3,1},{4,6},{5,7},{6,4},{7,5},{8,10},{9,11},{10,... | collective-permute-start | bytes 1769480 | tf_op jit(solution)/shard_map/ppermute | solution.py:723
  115.3 26.8 %collective-permute-start.12 = (bf16[384,768]{1,0:T(8,128)(2,1)S(1)}, bf16[384,768]{1,0:T(8,128)(2,1)S(1)}, u32[]{:S(2)}, u32[]{:S(2)}) collective-permute-start(bf16[384,768]{1,0:T(8,128)(2,1)S(1)} %add_convert_fusion.15), channel_id=1, source_target_pairs={{0,4},{1,5},{2,6},{3,7},{4,0},{5,1},{6,2},{7,3},{8,12},{9,13},{10,... | collective-permute-start | bytes 1769480 | tf_op jit(solution)/shard_map/ppermute | solution.py:723
  116.5 29.3 %collective-permute-start.14 = (bf16[192,3072]{1,0:T(8,128)(2,1)S(1)}, bf16[192,3072]{1,0:T(8,128)(2,1)S(1)}, u32[]{:S(2)}, u32[]{:S(2)}) collective-permute-start(bf16[192,3072]{1,0:T(8,128)(2,1)S(1)} %add_convert_fusion.1), channel_id=1, source_target_pairs={{0,1},{1,0},{2,3},{3,2},{4,5},{5,4},{6,7},{7,6},{8,9},{9,8},{10,11... | collective-permute-start | bytes 3538952 | tf_op jit(solution)/shard_map/ppermute | solution.py:723
  141.0 13.1 %collective-permute-start.18 = (bf16[192,1536]{1,0:T(8,128)(2,1)S(1)}, bf16[192,1536]{1,0:T(8,128)(2,1)S(1)}, u32[]{:S(2)}, u32[]{:S(2)}) collective-permute-start(bf16[192,1536]{1,0:T(8,128)(2,1)S(1)} %get-tuple-element.201), channel_id=1, source_target_pairs={{0,16},{1,17},{2,18},{3,19},{4,20},{5,21},{6,22},{7,23},{8,24},{9,... | collective-permute-start | bytes 1769480 | tf_op jit(solution)/shard_map/ppermute | solution.py:723
  141.4 11.5 %collective-permute-start.15 = (bf16[192,1536]{1,0:T(8,128)(2,1)S(1)}, bf16[192,1536]{1,0:T(8,128)(2,1)S(1)}, u32[]{:S(2)}, u32[]{:S(2)}) collective-permute-start(bf16[192,1536]{1,0:T(8,128)(2,1)S(1)} %get-tuple-element.204), channel_id=1, source_target_pairs={{0,16},{1,17},{2,18},{3,19},{4,20},{5,21},{6,22},{7,23},{8,24},{9,... | collective-permute-start | bytes 1769480 | tf_op jit(solution)/shard_map/ppermute | solution.py:723
  142.3 17.4 %collective-permute-start.17 = (bf16[384,768]{1,0:T(8,128)(2,1)S(1)}, bf16[384,768]{1,0:T(8,128)(2,1)S(1)}, u32[]{:S(2)}, u32[]{:S(2)}) collective-permute-start(bf16[384,768]{1,0:T(8,128)(2,1)S(1)} %add_convert_fusion.14), channel_id=1, source_target_pairs={{0,8},{1,9},{2,10},{3,11},{4,12},{5,13},{6,14},{7,15},{8,0},{9,1},... | collective-permute-start | bytes 1769480 | tf_op jit(solution)/shard_map/ppermute | solution.py:723
  146.2 9.9 %collective-permute-start.16 = (bf16[96,3072]{1,0:T(8,128)(2,1)S(1)}, bf16[96,3072]{1,0:T(8,128)(2,1)S(1)}, u32[]{:S(2)}, u32[]{:S(2)}) collective-permute-start(bf16[96,3072]{1,0:T(8,128)(2,1)S(1)} %get-tuple-element.287), channel_id=1, source_target_pairs={{0,2},{1,3},{2,0},{3,1},{4,6},{5,7},{6,4},{7,5},{8,10},{9,11},{10,... | collective-permute-start | bytes 1769480 | tf_op jit(solution)/shard_map/ppermute | solution.py:723
  152.8 15.4 %collective-permute-start.23 = (bf16[192,1664]{1,0:T(8,128)(2,1)S(1)}, bf16[192,1664]{1,0:T(8,128)(2,1)S(1)}, u32[]{:S(2)}, u32[]{:S(2)}) collective-permute-start(bf16[192,1664]{1,0:T(8,128)(2,1)S(1)} %get-tuple-element.214), channel_id=1, source_target_pairs={{0,16},{1,17},{2,18},{3,19},{4,20},{5,21},{6,22},{7,23},{8,24},{9,... | collective-permute-start | bytes 1916936 | tf_op jit(solution)/shard_map/ppermute | solution.py:723
  153.0 11.8 %collective-permute-start.20 = (bf16[192,1536]{1,0:T(8,128)(2,1)S(1)}, bf16[192,1536]{1,0:T(8,128)(2,1)S(1)}, u32[]{:S(2)}, u32[]{:S(2)}) collective-permute-start(bf16[192,1536]{1,0:T(8,128)(2,1)S(1)} %add_convert_fusion.11), channel_id=1, source_target_pairs={{0,1},{1,0},{2,3},{3,2},{4,5},{5,4},{6,7},{7,6},{8,9},{9,8},{10,11... | collective-permute-start | bytes 1769480 | tf_op jit(solution)/shard_map/ppermute | solution.py:723
  154.2 6.6 %collective-permute-start.19 = (bf16[192,1664]{1,0:T(8,128)(2,1)S(1)}, bf16[192,1664]{1,0:T(8,128)(2,1)S(1)}, u32[]{:S(2)}, u32[]{:S(2)}) collective-permute-start(bf16[192,1664]{1,0:T(8,128)(2,1)S(1)} %get-tuple-element.217), channel_id=1, source_target_pairs={{0,16},{1,17},{2,18},{3,19},{4,20},{5,21},{6,22},{7,23},{8,24},{9,... | collective-permute-start | bytes 1916936 | tf_op jit(solution)/shard_map/ppermute | solution.py:723
  156.3 15.2 %collective-permute-start.21 = (bf16[96,3072]{1,0:T(8,128)(2,1)S(1)}, bf16[96,3072]{1,0:T(8,128)(2,1)S(1)}, u32[]{:S(2)}, u32[]{:S(2)}) collective-permute-start(bf16[96,3072]{1,0:T(8,128)(2,1)S(1)} %add_convert_fusion.10), channel_id=1, source_target_pairs={{0,4},{1,5},{2,6},{3,7},{4,0},{5,1},{6,2},{7,3},{8,12},{9,13},{10,... | collective-permute-start | bytes 1769480 | tf_op jit(solution)/shard_map/ppermute | solution.py:723
  159.8 14.2 %collective-permute-start.22 = (bf16[384,768]{1,0:T(8,128)(2,1)S(1)}, bf16[384,768]{1,0:T(8,128)(2,1)S(1)}, u32[]{:S(2)}, u32[]{:S(2)}) collective-permute-start(bf16[384,768]{1,0:T(8,128)(2,1)S(1)} %add_convert_fusion.9), channel_id=1, source_target_pairs={{0,2},{1,3},{2,0},{3,1},{4,6},{5,7},{6,4},{7,5},{8,10},{9,11},{10,... | collective-permute-start | bytes 1769480 | tf_op jit(solution)/shard_map/ppermute | solution.py:723
  165.0 19.2 %collective-permute-start.24 = (bf16[96,1536]{1,0:T(8,128)(2,1)S(1)}, bf16[96,1536]{1,0:T(8,128)(2,1)S(1)}, u32[]{:S(2)}, u32[]{:S(2)}) collective-permute-start(bf16[96,1536]{1,0:T(8,128)(2,1)S(1)} %get-tuple-element.293), channel_id=1, source_target_pairs={{0,2},{1,3},{2,0},{3,1},{4,6},{5,7},{6,4},{7,5},{8,10},{9,11},{10,... | collective-permute-start | bytes 884744 | tf_op jit(solution)/shard_map/ppermute | solution.py:723
  165.7 22.5 %collective-permute-start.25 = (bf16[192,1664]{1,0:T(8,128)(2,1)S(1)}, bf16[192,1664]{1,0:T(8,128)(2,1)S(1)}, u32[]{:S(2)}, u32[]{:S(2)}) collective-permute-start(bf16[192,1664]{1,0:T(8,128)(2,1)S(1)} %add_convert_fusion.5), channel_id=1, source_target_pairs={{0,1},{1,0},{2,3},{3,2},{4,5},{5,4},{6,7},{7,6},{8,9},{9,8},{10,11... | collective-permute-start | bytes 1916936 | tf_op jit(solution)/shard_map/ppermute | solution.py:723
  171.7 21.4 %collective-permute-start.26 = (bf16[96,3072]{1,0:T(8,128)(2,1)S(1)}, bf16[96,3072]{1,0:T(8,128)(2,1)S(1)}, u32[]{:S(2)}, u32[]{:S(2)}) collective-permute-start(bf16[96,3072]{1,0:T(8,128)(2,1)S(1)} %add_convert_fusion.7), channel_id=1, source_target_pairs={{0,8},{1,9},{2,10},{3,11},{4,12},{5,13},{6,14},{7,15},{8,0},{9,1},... | collective-permute-start | bytes 1769480 | tf_op jit(solution)/shard_map/ppermute | solution.py:723
  174.1 22.3 %collective-permute-start.27 = (bf16[768,768]{1,0:T(8,128)(2,1)S(1)}, bf16[768,768]{1,0:T(8,128)(2,1)S(1)}, u32[]{:S(2)}, u32[]{:S(2)}) collective-permute-start(bf16[768,768]{1,0:T(8,128)(2,1)S(1)} %constant_dynamic-update-slice_fusion.9.refs_0_), channel_id=1, source_target_pairs={{0,1},{1,0},{2,3},{3,2},{4,5},{5,4},{6,7},{7,6},{8,9},{9,8},{10,11... | collective-permute-start | bytes 3538952 | tf_op jit(solution)/shard_map/ppermute | solution.py:723
  184.2 12.1 %collective-permute-start.28 = (bf16[96,1536]{1,0:T(8,128)(2,1)S(1)}, bf16[96,1536]{1,0:T(8,128)(2,1)S(1)}, u32[]{:S(2)}, u32[]{:S(2)}) collective-permute-start(bf16[96,1536]{1,0:T(8,128)(2,1)S(1)} %add_convert_fusion.25), channel_id=1, source_target_pairs={{0,4},{1,5},{2,6},{3,7},{4,0},{5,1},{6,2},{7,3},{8,12},{9,13},{10,... | collective-permute-start | bytes 884744 | tf_op jit(solution)/shard_map/ppermute | solution.py:723
  188.4 11.2 %collective-permute-start.29 = (bf16[96,1664]{1,0:T(8,128)(2,1)S(1)}, bf16[96,1664]{1,0:T(8,128)(2,1)S(1)}, u32[]{:S(2)}, u32[]{:S(2)}) collective-permute-start(bf16[96,1664]{1,0:T(8,128)(2,1)S(1)} %get-tuple-element.291), channel_id=1, source_target_pairs={{0,2},{1,3},{2,0},{3,1},{4,6},{5,7},{6,4},{7,5},{8,10},{9,11},{10,... | collective-permute-start | bytes 958472 | tf_op jit(solution)/shard_map/ppermute | solution.py:723
  193.2 10.4 %collective-permute-start.30 = (bf16[96,3072]{1,0:T(8,128)(2,1)S(1)}, bf16[96,3072]{1,0:T(8,128)(2,1)S(1)}, u32[]{:S(2)}, u32[]{:S(2)}) collective-permute-start(bf16[96,3072]{1,0:T(8,128)(2,1)S(1)} %add_convert_fusion.6), channel_id=1, source_target_pairs={{0,2},{1,3},{2,0},{3,1},{4,6},{5,7},{6,4},{7,5},{8,10},{9,11},{10,... | collective-permute-start | bytes 1769480 | tf_op jit(solution)/shard_map/ppermute | solution.py:723
  193.3 27.5 %collective-permute-start.34 = (bf16[768,768]{1,0:T(8,128)(2,1)S(1)}, bf16[768,768]{1,0:T(8,128)(2,1)S(1)}, u32[]{:S(2)}, u32[]{:S(2)}) collective-permute-start(bf16[768,768]{1,0:T(8,128)(2,1)S(1)} %constant_dynamic-update-slice_fusion.9.refs_0_), channel_id=1, source_target_pairs={{0,16},{1,17},{2,18},{3,19},{4,20},{5,21},{6,22},{7,23},{8,24},{9,... | collective-permute-start | bytes 3538952 | tf_op jit(solution)/shard_map/ppermute | solution.py:723
  199.7 13.1 %collective-permute-start.31 = (bf16[96,1664]{1,0:T(8,128)(2,1)S(1)}, bf16[96,1664]{1,0:T(8,128)(2,1)S(1)}, u32[]{:S(2)}, u32[]{:S(2)}) collective-permute-start(bf16[96,1664]{1,0:T(8,128)(2,1)S(1)} %add_convert_fusion.20), channel_id=1, source_target_pairs={{0,4},{1,5},{2,6},{3,7},{4,0},{5,1},{6,2},{7,3},{8,12},{9,13},{10,... | collective-permute-start | bytes 958472 | tf_op jit(solution)/shard_map/ppermute | solution.py:723
  203.6 17.2 %collective-permute-start.35 = (bf16[768,768]{1,0:T(8,128)(2,1)S(1)}, bf16[768,768]{1,0:T(8,128)(2,1)S(1)}, u32[]{:S(2)}, u32[]{:S(2)}) collective-permute-start(bf16[768,768]{1,0:T(8,128)(2,1)S(1)} %collective-permute-done.27.refs_1_), channel_id=1, source_target_pairs={{0,16},{1,17},{2,18},{3,19},{4,20},{5,21},{6,22},{7,23},{8,24},{9,... | collective-permute-start | bytes 3538952 | tf_op jit(solution)/shard_map/ppermute | solution.py:723
  203.7 20.3 %collective-permute-start.36 = (bf16[192,3072]{1,0:T(8,128)(2,1)S(1)}, bf16[192,3072]{1,0:T(8,128)(2,1)S(1)}, u32[]{:S(2)}, u32[]{:S(2)}) collective-permute-start(bf16[192,3072]{1,0:T(8,128)(2,1)S(1)} %constant_dynamic-update-slice_fusion.11.refs_0_), channel_id=1, source_target_pairs={{0,1},{1,0},{2,3},{3,2},{4,5},{5,4},{6,7},{7,6},{8,9},{9,8},{10,11... | collective-permute-start | bytes 3538952 | tf_op jit(solution)/shard_map/ppermute | solution.py:723
  206.2 14.4 %collective-permute-start.32 = (bf16[96,1536]{1,0:T(8,128)(2,1)S(1)}, bf16[96,1536]{1,0:T(8,128)(2,1)S(1)}, u32[]{:S(2)}, u32[]{:S(2)}) collective-permute-start(bf16[96,1536]{1,0:T(8,128)(2,1)S(1)} %add_convert_fusion.24), channel_id=1, source_target_pairs={{0,8},{1,9},{2,10},{3,11},{4,12},{5,13},{6,14},{7,15},{8,0},{9,1},... | collective-permute-start | bytes 884744 | tf_op jit(solution)/shard_map/ppermute | solution.py:723
  212.9 16.4 %collective-permute-start.33 = (bf16[96,1664]{1,0:T(8,128)(2,1)S(1)}, bf16[96,1664]{1,0:T(8,128)(2,1)S(1)}, u32[]{:S(2)}, u32[]{:S(2)}) collective-permute-start(bf16[96,1664]{1,0:T(8,128)(2,1)S(1)} %add_convert_fusion.19), channel_id=1, source_target_pairs={{0,8},{1,9},{2,10},{3,11},{4,12},{5,13},{6,14},{7,15},{8,0},{9,1},... | collective-permute-start | bytes 958472 | tf_op jit(solution)/shard_map/ppermute | solution.py:723
  220.7 8.7 %collective-permute-start.37 = (bf16[96,1536]{1,0:T(8,128)(2,1)S(1)}, bf16[96,1536]{1,0:T(8,128)(2,1)S(1)}, u32[]{:S(2)}, u32[]{:S(2)}) collective-permute-start(bf16[96,1536]{1,0:T(8,128)(2,1)S(1)} %add_convert_fusion.23), channel_id=1, source_target_pairs={{0,2},{1,3},{2,0},{3,1},{4,6},{5,7},{6,4},{7,5},{8,10},{9,11},{10,... | collective-permute-start | bytes 884744 | tf_op jit(solution)/shard_map/ppermute | solution.py:723
  224.0 18.9 %collective-permute-start.39 = (bf16[192,3072]{1,0:T(8,128)(2,1)S(1)}, bf16[192,3072]{1,0:T(8,128)(2,1)S(1)}, u32[]{:S(2)}, u32[]{:S(2)}) collective-permute-start(bf16[192,3072]{1,0:T(8,128)(2,1)S(1)} %constant_dynamic-update-slice_fusion.11.refs_0_), channel_id=1, source_target_pairs={{0,16},{1,17},{2,18},{3,19},{4,20},{5,21},{6,22},{7,23},{8,24},{9,... | collective-permute-start | bytes 3538952 | tf_op jit(solution)/shard_map/ppermute | solution.py:723
  224.0 18.9 %collective-permute-start.40 = (bf16[192,3072]{1,0:T(8,128)(2,1)S(1)}, bf16[192,3072]{1,0:T(8,128)(2,1)S(1)}, u32[]{:S(2)}, u32[]{:S(2)}) collective-permute-start(bf16[192,3072]{1,0:T(8,128)(2,1)S(1)} %collective-permute-done.36.refs_1_), channel_id=1, source_target_pairs={{0,16},{1,17},{2,18},{3,19},{4,20},{5,21},{6,22},{7,23},{8,24},{9,... | collective-permute-start | bytes 3538952 | tf_op jit(solution)/shard_map/ppermute | solution.py:723
  229.3 10.5 %collective-permute-start.38 = (bf16[96,1664]{1,0:T(8,128)(2,1)S(1)}, bf16[96,1664]{1,0:T(8,128)(2,1)S(1)}, u32[]{:S(2)}, u32[]{:S(2)}) collective-permute-start(bf16[96,1664]{1,0:T(8,128)(2,1)S(1)} %add_convert_fusion.18), channel_id=1, source_target_pairs={{0,2},{1,3},{2,0},{3,1},{4,6},{5,7},{6,4},{7,5},{8,10},{9,11},{10,... | collective-permute-start | bytes 958472 | tf_op jit(solution)/shard_map/ppermute | solution.py:723
  229.5 13.4 %collective-permute-start.42 = (bf16[192,1536]{1,0:T(8,128)(2,1)S(1)}, bf16[192,1536]{1,0:T(8,128)(2,1)S(1)}, u32[]{:S(2)}, u32[]{:S(2)}) collective-permute-start(bf16[192,1536]{1,0:T(8,128)(2,1)S(1)} %constant_dynamic-update-slice_fusion.13.refs_0_), channel_id=1, source_target_pairs={{0,1},{1,0},{2,3},{3,2},{4,5},{5,4},{6,7},{7,6},{8,9},{9,8},{10,11... | collective-permute-start | bytes 1769480 | tf_op jit(solution)/shard_map/ppermute | solution.py:723
  239.9 11.4 %collective-permute-start.45 = (bf16[192,1664]{1,0:T(8,128)(2,1)S(1)}, bf16[192,1664]{1,0:T(8,128)(2,1)S(1)}, u32[]{:S(2)}, u32[]{:S(2)}) collective-permute-start(bf16[192,1664]{1,0:T(8,128)(2,1)S(1)} %constant_dynamic-update-slice_fusion.15.refs_0_), channel_id=1, source_target_pairs={{0,1},{1,0},{2,3},{3,2},{4,5},{5,4},{6,7},{7,6},{8,9},{9,8},{10,11... | collective-permute-start | bytes 1916936 | tf_op jit(solution)/shard_map/ppermute | solution.py:723
  242.9 10.9 %collective-permute-start.43 = (bf16[192,1536]{1,0:T(8,128)(2,1)S(1)}, bf16[192,1536]{1,0:T(8,128)(2,1)S(1)}, u32[]{:S(2)}, u32[]{:S(2)}) collective-permute-start(bf16[192,1536]{1,0:T(8,128)(2,1)S(1)} %collective-permute-done.42.refs_1_), channel_id=1, source_target_pairs={{0,16},{1,17},{2,18},{3,19},{4,20},{5,21},{6,22},{7,23},{8,24},{9,... | collective-permute-start | bytes 1769480 | tf_op jit(solution)/shard_map/ppermute | solution.py:723
  246.1 7.7 %collective-permute-start.41 = (bf16[192,1536]{1,0:T(8,128)(2,1)S(1)}, bf16[192,1536]{1,0:T(8,128)(2,1)S(1)}, u32[]{:S(2)}, u32[]{:S(2)}) collective-permute-start(bf16[192,1536]{1,0:T(8,128)(2,1)S(1)} %constant_dynamic-update-slice_fusion.13.refs_0_), channel_id=1, source_target_pairs={{0,16},{1,17},{2,18},{3,19},{4,20},{5,21},{6,22},{7,23},{8,24},{9,... | collective-permute-start | bytes 1769480 | tf_op jit(solution)/shard_map/ppermute | solution.py:723
  251.3 8.7 %collective-permute-start.46 = (bf16[192,1664]{1,0:T(8,128)(2,1)S(1)}, bf16[192,1664]{1,0:T(8,128)(2,1)S(1)}, u32[]{:S(2)}, u32[]{:S(2)}) collective-permute-start(bf16[192,1664]{1,0:T(8,128)(2,1)S(1)} %collective-permute-done.45.refs_1_), channel_id=1, source_target_pairs={{0,16},{1,17},{2,18},{3,19},{4,20},{5,21},{6,22},{7,23},{8,24},{9,... | collective-permute-start | bytes 1916936 | tf_op jit(solution)/shard_map/ppermute | solution.py:723
  256.3 3.7 %collective-permute-start.44 = (bf16[192,1664]{1,0:T(8,128)(2,1)S(1)}, bf16[192,1664]{1,0:T(8,128)(2,1)S(1)}, u32[]{:S(2)}, u32[]{:S(2)}) collective-permute-start(bf16[192,1664]{1,0:T(8,128)(2,1)S(1)} %constant_dynamic-update-slice_fusion.15.refs_0_), channel_id=1, source_target_pairs={{0,16},{1,17},{2,18},{3,19},{4,20},{5,21},{6,22},{7,23},{8,24},{9,... | collective-permute-start | bytes 1916936 | tf_op jit(solution)/shard_map/ppermute | solution.py:723

commit v2 on v1

--- a/solution.py
+++ b/solution.py
@@ -86,6 +86,10 @@
 
 def far(*shape, dtype=low):
     return pltpu.HBM(shape, dtype)
+
+
+def near(*shape, dtype=low):
+    return pltpu.VMEM(shape, dtype)
 
 
 def params(grid_dims, mib=20):
@@ -398,14 +402,14 @@
     count, hidden = act.shape
     tall = hidden // 8
     fresh = fix is not None
-    operands = [in_far(dbranch)] + ([leads, fix] if fresh else []) + [in_far(act)]
+    operands = [dbranch] + ([leads, fix] if fresh else []) + [in_far(act)]
     moving = pl.BlockSpec((count, tall), lambda p, place: (0, place[first + p]))
     in_specs = [fixed_spec(*operand.shape) for operand in operands[:-1]] + [moving]
     out_specs = [fixed_spec(2 * tall, D)] * 2
-    out_shape = [shape_of(2 * tall, D)] * 2
+    out_shape = [pltpu.VMEM((2 * tall, D), low)] * 2
     if fresh:
         out_specs += [fixed_spec(count, D), fixed_spec(1, D)]
-        out_shape += [far(count, D), shape_of(1, D, dtype=full)]
+        out_shape += [shape_of(count, D), shape_of(1, D, dtype=full)]
     return pl.pallas_call(
         functools.partial(down_grad_kernel, seq_len, fresh),
         grid_spec=pltpu.PrefetchScalarGridSpec(
@@ -452,7 +456,7 @@
         compiler_params=params(1, 18),
         name="hidden_gradient",
         cost_estimate=cost(15),
-    )(place, in_far(dbranch), in_far(slope), dw, in_far(nl))
+    )(place, dbranch, in_far(slope), dw, in_far(nl))
 
 
 def norm_one_kernel(dpre_ref, uw, gain1, wo_far, branch_far, hat_far, inv_far,
@@ -501,7 +505,7 @@
             pl.BlockSpec((count, D), lambda j: (0, j)), pl.BlockSpec((D, D), lambda j: (0, j)), vector_spec(), anywhere, anywhere, anywhere, anywhere,
         ],
         out_specs=[pl.BlockSpec((1, count, D), lambda j: (3, 0, 0)), fixed_spec(count, D), fixed_spec(8, D)],
-        out_shape=[far(4, count, D), far(count, D), shape_of(8, D, dtype=full)],
+        out_shape=[near(4, count, D), near(count, D), shape_of(8, D, dtype=full)],
         scratch_shapes=[
             pltpu.VMEM((count, D), full), pltpu.VMEM((D, D), low), pltpu.VMEM((count, D), low),
             pltpu.VMEM((count, D), full), pltpu.VMEM((count, LANES), full), pltpu.SemaphoreType.DMA((4,)),
@@ -509,7 +513,7 @@
         compiler_params=params(1, 24),
         name="norm_one_backward",
         cost_estimate=cost(13),
-    )(in_far(dpre), uw, gain1, wo, in_far(dbranch), in_far(hat), in_far(inv))
+    )(in_far(dpre), uw, gain1, wo, dbranch, in_far(hat), in_far(inv))
 
 
 def attention_back_kernel(seq_len, q_ref, k_ref, v_ref, p_ref, dc_ref, stack_ref, d_ref, sums):
@@ -546,12 +550,12 @@
         grid=(count // rows,),
         in_specs=[row] * 5 + [pl.BlockSpec(memory_space=pl.ANY)],
         out_specs=[pl.BlockSpec((3, rows, D), lambda i: (0, i, 0)), fixed_spec(8, D)],
-        out_shape=[far(4, count, D), shape_of(8, D, dtype=full)],
+        out_shape=[near(4, count, D), shape_of(8, D, dtype=full)],
         input_output_aliases={5: 0},
         compiler_params=params(1, 14),
         name="attention_backward",
         cost_estimate=cost(8),
-    )(*map(in_far, (q, k, v, probs, dctx, stack)))
+    )(*map(in_near, (q, k, v, probs, dctx, stack)))
 
 
 def square_grad_kernel(late, place, left_ref, d_ref, *rest):
@@ -611,7 +615,7 @@
         compiler_params=params(1, 18),
         name=name,
         cost_estimate=cost(6),
-    )(place, in_far(lefts[0]), in_far(stack), in_far(lefts[1]) if late else small)
+    )(place, in_far(lefts[0]), in_near(stack), in_far(lefts[1]) if late else small)
 
 
 def input_grad_kernel(d_ref, wq, wk, wv, out_ref):
@@ -633,7 +637,7 @@
         compiler_params=params(1),
         name="input_gradient",
         cost_estimate=cost(6),
-    )(in_far(stack), wq, wk, wv)
+    )(in_near(stack), wq, wk, wv)
 
 
 def spread_kernel(widths, talls, first, place, *refs):
@@ -737,13 +741,13 @@
     pair = add_low(kept[1], others[1])
     other = swap(pair, chip_partner(1, 2))
     mine = add_low(kept[0], others[0])
-    after = yield pair
+    after = yield pair, mine
     tall = mine.shape[0] // 2
     mine = tie(mine, after)
     block = add_low(mine[tall:], other[tall:])
     mine = add_low(mine[:tall], other[:tall])
     other = swap(block, chip_partner(2, 1))
-    after = yield block
+    after = yield block, mine
     bits = [1 << k for k in range(2, lax.axis_size("dp").bit_length() - 1)]
     for rank, pair in enumerate(zip(bits, bits[::-1], strict=True)):
         mine = add_low(tie(mine, after), other)
@@ -777,6 +781,10 @@
 
 def in_far(array):
     return pltpu.with_memory_space_constraint(array, pltpu.HBM)
+
+
+def in_near(array):
+    return pltpu.with_memory_space_constraint(array, pltpu.VMEM)
 
 
 def shards(

time: 267 us -> 260 us (0.974)
  starting transfers between devices: 62.2 us -> 33.8 us
  waiting for transfers between devices: 34.9 us -> 62.2 us
  Pallas kernels: 154 us -> 147 us
    ppermute x47, starting transfers between devices: 62.2 us -> 33.8 us  [swap(): return lax.ppermute(piece, ('stream', 'dp'), pairs)]
    ppermute x47, waiting for transfers between devices: 34.9 us -> 62.2 us  [swap(): return lax.ppermute(piece, ('stream', 'dp'), pairs)]
  transfers between devices with their start and end apart: 47 -> 47, of which waited for: 10 -> 14; matrix products, arithmetic and copies ran while one was open for 3% -> 4% of each run, Pallas kernels for 47% -> 45%
where the time goes in v2:
time: 260 us; the launch traced here: 256 us
  Pallas kernels  147 us (57%)
  waiting for transfers between devices  62.2 us (24%)
  starting transfers between devices  33.8 us (13%)
  other arithmetic  8.58 us (3%)
  local copies, waits for them, and re-layouts  2.74 us (1%)
    ppermute x47, waiting for transfers between devices, swap(): return lax.ppermute(piece, ('stream', 'dp'), pairs)  62.2 us
    ppermute x47, starting transfers between devices, swap(): return lax.ppermute(piece, ('stream', 'dp'), pairs)  33.8 us
    pallas_call x2, Pallas kernels, ff_forward(): pl.pallas_call(functools.partial(ff_kernel, part, seq_len), grid=(hidden...  30.5 us
    pallas_call x8, Pallas kernels, spread(): pl.pallas_call(functools.partial(spread_kernel, widths, talls, first), gr...  22.7 us
    pallas_call x2, Pallas kernels, square_gradient(): pl.pallas_call(functools.partial(square_grad_kernel, late), grid_spec=plt...  19.2 us
    pallas_call x1, Pallas kernels, hidden_gradient(): pl.pallas_call(hidden_kernel, grid_spec=pltpu.PrefetchScalarGridSpec(num_...  14.9 us
    pallas_call x1, Pallas kernels, attention_forward(): pl.pallas_call(functools.partial(attention_kernel, seq_len), grid=(steps,...  14.1 us
    pallas_call x2, Pallas kernels, down_gradient(): pl.pallas_call(functools.partial(down_grad_kernel, seq_len, fresh), grid_...  12.6 us
  transfers between devices with their start and end apart: 47, of which 14 were waited for; matrix products, arithmetic and copies ran while one was open for 4% of the time, Pallas kernels for 45%

profile of v2, /device:TPU:0, one launch (start us, length us, event | category | flops | bytes accessed | tf_op | source)
XLA Modules:
  0.0 255.7 jit_solution(12953197820908049124)
XLA Ops:
  1.3 14.1 %attention_forward.1 = (bf16[1024,768]{1,0:T(8,128)(2,1)}, bf16[1024,768]{1,0:T(8,128)(2,1)}, bf16[1024,768]{1,0:T(8,128)(2,1)}, bf16[1024,768]{1,0:T(8,128)(2,1...) custom-call(bf16[1024,768]{1,0:T(8,128)(2,1)} %bitcast.36, ...), custom_call_target="tpu_custom_call" | custom-call | flops 230000000 | bytes 1000 | tf_op jit(solution)/shard_map/attention_forward/pallas_call | solution.py:164
  15.5 5.7 %lead_forward.1 = (f32[16,768]{1,0:T(8,128)S(1)}, f32[16,768]{1,0:T(8,128)S(1)}, f32[16,128]{1,0:T(8,128)S(1)}, f32[16,128]{1,0:T(8,128)S(1)}, bf16[16,768]{1,0:T(8,128)(2,1)S(1)}) custom-call(f32[4,4,768]{2,1,0:T(4,128)S(1)} %get-tuple-element.149.nl_ref, f32[4,4,768]{2,1,0:T(4,128)S(1)} %get-tuple-element.150.hat_ref, bf16[768,3072]{1,0:T(8,128)(2,1)} %uw.7, ...), custom_call_target="tpu_custom_call" | custom-call | flops 69000000 | bytes 1000 | tf_op jit(solution)/shard_map/lead_forward/pallas_call | solution.py:207
  21.3 2.9 %collective-permute-start = (bf16[16,896]{1,0:T(8,128)(2,1)S(1)}, bf16[16,896]{1,0:T(8,128)(2,1)S(1)}, u32[]{:S(2)}, u32[]{:S(2)}) collective-permute-start(bf16[16,896]{1,0:T(8,128)(2,1)S(1)} %pad_maximum_fusion), channel_id=1, source_target_pairs={{0,1},{1,0},{2,3},{3,2},{4,5},{5,4},{6,7},{7,6},{8,9},{9,8},{10,11... | collective-permute-start | bytes 86024 | tf_op jit(solution)/shard_map/ppermute | solution.py:727
  24.2 1.5 collective-permute-start.1
  25.8 15.3 %ff_forward_0.1 = (bf16[1024,768]{1,0:T(8,128)(2,1)}, bf16[1024,3072]{1,0:T(8,128)(2,1)}, bf16[1024,3072]{1,0:T(8,128)(2,1)}, bf16[1024,768]{1,0:T(8,128)(2,1)},...) custom-call(bf16[1024,768]{1,0:T(8,128)(2,1)} %get-tuple-element.156.nl_ref, bf16[768,3072]{1,0:T(8,128)(2,1)} %uw.7, ...), custom_call_target="tpu_custom_call" | custom-call | flops 299000000 | bytes 1000 | tf_op jit(solution)/shard_map/ff_forward_0/pallas_call | solution.py:281
  41.1 2.1 collective-permute-start.3
  43.2 2.6 %collective-permute-start.4 = (bf16[64,896]{1,0:T(8,128)(2,1)S(1)}, bf16[64,896]{1,0:T(8,128)(2,1)S(1)}, u32[]{:S(2)}, u32[]{:S(2)}) collective-permute-start(bf16[64,896]{1,0:T(8,128)(2,1)S(1)} %constant_dynamic-update-slice_fusion), channel_id=1, source_target_pairs={{0,8},{1,9},{2,10},{3,11},{4,12},{5,13},{6,14},{7,15},{8,0},{9,1},... | collective-permute-start | bytes 344072 | tf_op jit(solution)/shard_map/ppermute | solution.py:727
  45.8 15.2 %ff_forward_1.1 = (bf16[1024,768]{1,0:T(8,128)(2,1)}, bf16[1024,3072]{1,0:T(8,128)(2,1)}, bf16[1024,3072]{1,0:T(8,128)(2,1)}, bf16[1024,768]{1,0:T(8,128)(2,1)},...) custom-call(bf16[1024,768]{1,0:T(8,128)(2,1)} %get-tuple-element.156, ...), custom_call_target="tpu_custom_call", output_to_operand_aliasing={{0}: (11, {}), {1}: (12, {}), {2}: (13, {}), {3}: (14, {}),... | custom-call | flops 299000000 | bytes 1000 | tf_op jit(solution)/shard_map/ff_forward_1/pallas_call | solution.py:281
  61.3 1.7 collective-permute-done.6.other_ref
  63.0 1.8 pair_loss.1
  64.8 7.0 %down_grad_4.1 = (bf16[768,768]{1,0:T(8,128)(2,1)}, bf16[768,768]{1,0:T(8,128)(2,1)S(1)}, bf16[1024,768]{1,0:T(8,128)(2,1)S(1)}, f32[1,768]{1,0:T(1,128)S(1)}) custom-call(s32[8]{0:T(128)S(1)} %stack.35.place, bf16[1024,768]{1,0:T(8,128)(2,1)S(1)} %copy-done, f32[16,768]{1,0:T(8,128)S(1)} %bitcast.34, f32[16,768]{1,0:T(8,128)S(1)} %get-tuple-element.175.refs_2_, ...), custom_call_target="tpu_custom_call" | custom-call | flops 92000000 | bytes 1000 | tf_op jit(solution)/shard_map/down_grad_4/pallas_call | solution.py:413
  72.3 5.6 %down_grad_0.1 = (bf16[768,768]{1,0:T(8,128)(2,1)S(1)}, bf16[768,768]{1,0:T(8,128)(2,1)S(1)}) custom-call(s32[8]{0:T(128)S(1)} %stack.35.place, bf16[1024,768]{1,0:T(8,128)(2,1)S(1)} %get-tuple-element.183.refs_0_.db_ref.branch_far, bf16[1024,3072]{1,0:T(8,128)(2,1)} %get-tuple-element.176.refs_3_.refs_1_), custom_call_target="tpu_custom_call" | custom-call | flops 92000000 | bytes 1000 | tf_op jit(solution)/shard_map/down_grad_0/pallas_call | solution.py:413
  77.9 1.3 add_convert_fusion.3
  79.2 1.7 collective-permute-start.9
  80.9 1.6 add_convert_fusion.2
  82.5 14.9 %hidden_gradient.1 = (bf16[1024,3072]{1,0:T(8,128)(2,1)}, f32[8,3072]{1,0:T(8,128)S(1)}, bf16[192,3072]{1,0:T(8,128)(2,1)S(1)}, bf16[192,3072]{1,0:T(8,128)(2,1)...) custom-call(s32[8]{0:T(128)S(1)} %stack.35.place, ...), custom_call_target="tpu_custom_call", output_to_operand_aliasing={{0}: (2, {})} | custom-call | flops 345000000 | bytes 1000 | tf_op jit(solution)/shard_map/hidden_gradient/pallas_call | solution.py:445
  98.0 1.6 add_convert_fusion.16
  99.5 1.6 collective-permute-start.10
  101.1 11.0 %norm_one_backward.1 = (bf16[4,1024,768]{2,1,0:T(8,128)(2,1)S(1)}, bf16[1024,768]{1,0:T(8,128)(2,1)S(1)}, f32[8,768]{1,0:T(8,128)S(1)}) custom-call(bf16[1024,3072]{1,0:T(8,128)(2,1)} %get-tuple-element.189.dpre_ref, bf16[768,3072]{1,0:T(8,128)(2,1)} %uw.7, f32[6,128]{1,0:T(8,128)} %bitcast.50, bf16[768,768]{1,0:T(8,128)(2,1)} %wo_far.1, ...), custom_call_target="tpu_custom_call" | custom-call | flops 299000000 | bytes 1000 | tf_op jit(solution)/shard_map/norm_one_backward/pallas_call | solution.py:501
  116.1 6.7 %attention_backward.1 = (bf16[4,1024,768]{2,1,0:T(8,128)(2,1)S(1)}, f32[8,768]{1,0:T(8,128)S(1)}) custom-call(bf16[1024,768]{1,0:T(8,128)(2,1)S(1)} %copy-done.1, bf16[1024,768]{1,0:T(8,128)(2,1)S(1)} %copy-done.2, bf16[1024,768]{1,0:T(8,128)(2,1)S(1)} %copy-done.3, bf16[1024,768]{1,0:T(8,128)(2,1)S(1)} %copy-done.4, ...), custom_call_target="tpu_custom_call", output_to_operand_aliasing={{0}: (5, {})} | custom-call | flops 184000000 | bytes 1000 | tf_op jit(solution)/shard_map/attention_backward/pallas_call | solution.py:548
  122.8 14.1 %value_gradient.1 = (bf16[192,1536]{1,0:T(8,128)(2,1)S(1)}, bf16[192,1536]{1,0:T(8,128)(2,1)S(1)}, bf16[192,1536]{1,0:T(8,128)(2,1)S(1)}, bf16[192,1536]{1,0:T(8,128)(2,1)S(1)}) custom-call(s32[8]{0:T(128)S(1)} %stack.35.place, bf16[1024,768]{1,0:T(8,128)(2,1)} %get-tuple-element.200.left_ref, bf16[4,1024,768]{2,1,0:T(8,128)(2,1)S(1)} %get-tuple-element.227.d_ref, ...), custom_call_target="tpu_custom_call" | custom-call | flops 138000000 | bytes 1000 | tf_op jit(solution)/shard_map/value_gradient/pallas_call | solution.py:601
  137.7 3.5 %collective-permute-start.18 = (bf16[384,768]{1,0:T(8,128)(2,1)S(1)}, bf16[384,768]{1,0:T(8,128)(2,1)S(1)}, u32[]{:S(2)}, u32[]{:S(2)}) collective-permute-start(bf16[384,768]{1,0:T(8,128)(2,1)S(1)} %add_convert_fusion.14), channel_id=1, source_target_pairs={{0,8},{1,9},{2,10},{3,11},{4,12},{5,13},{6,14},{7,15},{8,0},{9,1},... | collective-permute-start | bytes 1769480 | tf_op jit(solution)/shard_map/ppermute | solution.py:727
  142.2 5.1 %query_gradient.1 = (bf16[192,1664]{1,0:T(8,128)(2,1)S(1)}, bf16[192,1664]{1,0:T(8,128)(2,1)S(1)}, bf16[192,1664]{1,0:T(8,128)(2,1)S(1)}, bf16[192,1664]{1,0:T(8,128)(2,1)S(1)}) custom-call(s32[8]{0:T(128)S(1)} %stack.35.place, bf16[1024,768]{1,0:T(8,128)(2,1)} %bitcast.38, bf16[4,1024,768]{2,1,0:T(8,128)(2,1)S(1)} %get-tuple-element.227.d_ref, ...), custom_call_target="tpu_custom_call" | custom-call | flops 138000000 | bytes 1000 | tf_op jit(solution)/shard_map/query_gradient/pallas_call | solution.py:601
  149.5 2.8 %collective-permute-done.17 = bf16[96,3072]{1,0:T(8,128)(2,1)S(1)} collective-permute-done((bf16[96,3072]{1,0:T(8,128)(2,1)S(1)}, bf16[96,3072]{1,0:T(8,128)(2,1)S(1)}, u32[]{:S(2)}, u32[]{:S(2)}) %collective-permute-start.17) | collective-permute-done | bytes 589856 | tf_op jit(solution)/shard_map/ppermute | solution.py:727
  152.6 2.5 collective-permute-done.18
  157.0 1.2 collective-permute-done.21
  158.4 1.8 collective-permute-start.24
  160.1 8.1 %collective-permute-done.22 = bf16[96,3072]{1,0:T(8,128)(2,1)S(1)} collective-permute-done((bf16[96,3072]{1,0:T(8,128)(2,1)S(1)}, bf16[96,3072]{1,0:T(8,128)(2,1)S(1)}, u32[]{:S(2)}, u32[]{:S(2)}) %collective-permute-start.22) | collective-permute-done | bytes 589856 | tf_op jit(solution)/shard_map/ppermute | solution.py:727
  169.4 1.6 collective-permute-done.23
  171.9 7.7 %input_gradient.1 = f32[1024,768]{1,0:T(8,128)} custom-call(bf16[4,1024,768]{2,1,0:T(8,128)(2,1)S(1)} %get-tuple-element.227.d_ref, bf16[768,768]{1,0:T(8,128)(2,1)} %wq.3, bf16[768,768]{1,0:T(8,128)(2,1)} %wk.3, bf16[768,768]{1,0:T(8,128)(2,1)} %wv.3), custom_call_target="tpu_custom_call" | custom-call | flops 138000000 | bytes 1000 | tf_op jit(solution)/shard_map/input_gradient/pallas_call | solution.py:631
  180.2 1.5 collective-permute-start.29
  181.7 9.2 %collective-permute-done.26 = bf16[96,3072]{1,0:T(8,128)(2,1)S(1)} collective-permute-done((bf16[96,3072]{1,0:T(8,128)(2,1)S(1)}, bf16[96,3072]{1,0:T(8,128)(2,1)S(1)}, u32[]{:S(2)}, u32[]{:S(2)}) %collective-permute-start.26) | collective-permute-done | bytes 589856 | tf_op jit(solution)/shard_map/ppermute | solution.py:727
  191.3 1.8 collective-permute-done.27.refs_1_
  193.1 3.2 %down_spread_0.1.refs_2_ = f32[3072,768]{1,0:T(8,128)} custom-call(s32[8]{0:T(128)S(1)} %stack.35.place, bf16[768,768]{1,0:T(8,128)(2,1)S(1)} %constant_dynamic-update-slice_fusion.9.refs_0_, bf16[768,768]{1,0:T(8,128)(2,1)S(1)} %collective-permute-done.27.refs_1_), custom_call_target="tpu_custom_call" | custom-call | flops 69000000 | bytes 1000 | tf_op jit(solution)/shard_map/down_spread_0/pallas_call | solution.py:683
  197.1 4.4 %collective-permute-done.30 = bf16[96,3072]{1,0:T(8,128)(2,1)S(1)} collective-permute-done((bf16[96,3072]{1,0:T(8,128)(2,1)S(1)}, bf16[96,3072]{1,0:T(8,128)(2,1)S(1)}, u32[]{:S(2)}, u32[]{:S(2)}) %collective-permute-start.30) | collective-permute-done | bytes 589856 | tf_op jit(solution)/shard_map/ppermute | solution.py:727
  201.7 11.1 %collective-permute-done.31 = bf16[96,1664]{1,0:T(8,128)(2,1)S(1)} collective-permute-done((bf16[96,1664]{1,0:T(8,128)(2,1)S(1)}, bf16[96,1664]{1,0:T(8,128)(2,1)S(1)}, u32[]{:S(2)}, u32[]{:S(2)}) %collective-permute-start.31) | collective-permute-done | bytes 319520 | tf_op jit(solution)/shard_map/ppermute | solution.py:727
  213.5 3.2 %down_spread_4.1 = f32[3072,768]{1,0:T(8,128)} custom-call(s32[8]{0:T(128)S(1)} %stack.35.place, bf16[768,768]{1,0:T(8,128)(2,1)S(1)} %collective-permute-done.34.refs_0_, bf16[768,768]{1,0:T(8,128)(2,1)S(1)} %collective-permute-done.35.refs_1_, f32[3072,768]{1,0:T(8,128)} %down_spread_0.1.refs_2_), custom_call_target="tpu_custom_call", output_to_operand_aliasing={{}: (3, {})} | custom-call | flops 69000000 | bytes 1000 | tf_op jit(solution)/shard_map/down_spread_4/pallas_call | solution.py:683
  216.7 3.6 %collective-permute-done.36.refs_1_ = bf16[192,3072]{1,0:T(8,128)(2,1)S(1)} collective-permute-done((bf16[192,3072]{1,0:T(8,128)(2,1)S(1)}, bf16[192,3072]{1,0:T(8,128)(2,1)S(1)}, u32[]{:S(2)}, u32[]{:S(2)}) %collective-permute-start.36) | collective-permute-done | bytes 1179680 | tf_op jit(solution)/shard_map/ppermute | solution.py:727
  220.2 3.0 %collective-permute-done.33 = bf16[96,1664]{1,0:T(8,128)(2,1)S(1)} collective-permute-done((bf16[96,1664]{1,0:T(8,128)(2,1)S(1)}, bf16[96,1664]{1,0:T(8,128)(2,1)S(1)}, u32[]{:S(2)}, u32[]{:S(2)}) %collective-permute-start.33) | collective-permute-done | bytes 319520 | tf_op jit(solution)/shard_map/ppermute | solution.py:727
  223.8 1.7 collective-permute-start.42
  225.5 3.2 %up_spread_0.1.refs_2_ = f32[768,3072]{1,0:T(8,128)} custom-call(s32[8]{0:T(128)S(1)} %stack.35.place, bf16[192,3072]{1,0:T(8,128)(2,1)S(1)} %constant_dynamic-update-slice_fusion.11.refs_0_, bf16[192,3072]{1,0:T(8,128)(2,1)S(1)} %collective-permute-done.36.refs_1_), custom_call_target="tpu_custom_call" | custom-call | flops 69000000 | bytes 1000 | tf_op jit(solution)/shard_map/up_spread_0/pallas_call | solution.py:683
  228.7 5.1 %collective-permute-done.38 = bf16[96,1664]{1,0:T(8,128)(2,1)S(1)} collective-permute-done((bf16[96,1664]{1,0:T(8,128)(2,1)S(1)}, bf16[96,1664]{1,0:T(8,128)(2,1)S(1)}, u32[]{:S(2)}, u32[]{:S(2)}) %collective-permute-start.38) | collective-permute-done | bytes 319520 | tf_op jit(solution)/shard_map/ppermute | solution.py:727
  234.4 3.2 %up_spread_4.1 = f32[768,3072]{1,0:T(8,128)} custom-call(s32[8]{0:T(128)S(1)} %stack.35.place, bf16[192,3072]{1,0:T(8,128)(2,1)S(1)} %collective-permute-done.39.refs_0_, bf16[192,3072]{1,0:T(8,128)(2,1)S(1)} %collective-permute-done.40.refs_1_, f32[768,3072]{1,0:T(8,128)} %up_spread_0.1.refs_2_), custom_call_target="tpu_custom_call", output_to_operand_aliasing={{}: (3, {})} | custom-call | flops 69000000 | bytes 1000 | tf_op jit(solution)/shard_map/up_spread_4/pallas_call | solution.py:683
  238.1 6.2 %collective-permute-done.45.refs_1_ = bf16[192,1664]{1,0:T(8,128)(2,1)S(1)} collective-permute-done((bf16[192,1664]{1,0:T(8,128)(2,1)S(1)}, bf16[192,1664]{1,0:T(8,128)(2,1)S(1)}, u32[]{:S(2)}, u32[]{:S(2)}) %collective-permute-start.45) | collective-permute-done | bytes 639008 | tf_op jit(solution)/shard_map/ppermute | solution.py:727
  244.3 2.5 value_spread_0.1
  246.8 2.5 value_spread_4.1
  250.5 2.5 query_spread_0.1
  253.0 2.6 %query_spread_4.1 = (f32[768,768]{1,0:T(8,128)}, f32[768,768]{1,0:T(8,128)}, f32[24,128]{1,0:T(8,128)}, f32[6,128]{1,0:T(8,128)}, f32[6,128]{1,0:T(8,128)}, /*in...) custom-call(s32[8]{0:T(128)S(1)} %stack.35.place, ...), custom_call_target="tpu_custom_call", output_to_operand_aliasing={{0}: (12, {}), {1}: (13, {})} | custom-call | flops 69000000 | bytes 1000 | tf_op jit(solution)/shard_map/query_spread_4/pallas_call | solution.py:683
  (136 shorter events, 19.9 us)
Async XLA Ops:
  21.3 19.8 %collective-permute-start = (bf16[16,896]{1,0:T(8,128)(2,1)S(1)}, bf16[16,896]{1,0:T(8,128)(2,1)S(1)}, u32[]{:S(2)}, u32[]{:S(2)}) collective-permute-start(bf16[16,896]{1,0:T(8,128)(2,1)S(1)} %pad_maximum_fusion), channel_id=1, source_target_pairs={{0,1},{1,0},{2,3},{3,2},{4,5},{5,4},{6,7},{7,6},{8,9},{9,8},{10,11... | collective-permute-start | bytes 86024 | tf_op jit(solution)/shard_map/ppermute | solution.py:727
  24.2 16.8 %collective-permute-start.1 = (bf16[16,896]{1,0:T(8,128)(2,1)S(1)}, bf16[16,896]{1,0:T(8,128)(2,1)S(1)}, u32[]{:S(2)}, u32[]{:S(2)}) collective-permute-start(bf16[16,896]{1,0:T(8,128)(2,1)S(1)} %pad_maximum_fusion), channel_id=1, source_target_pairs={{0,2},{1,3},{2,0},{3,1},{4,6},{5,7},{6,4},{7,5},{8,10},{9,11},{10,... | collective-permute-start | bytes 86024 | tf_op jit(solution)/shard_map/ppermute | solution.py:727
  25.7 15.4 %collective-permute-start.2 = (bf16[16,896]{1,0:T(8,128)(2,1)S(1)}, bf16[16,896]{1,0:T(8,128)(2,1)S(1)}, u32[]{:S(2)}, u32[]{:S(2)}) collective-permute-start(bf16[16,896]{1,0:T(8,128)(2,1)S(1)} %pad_maximum_fusion), channel_id=1, source_target_pairs={{0,3},{1,2},{2,1},{3,0},{4,7},{5,6},{6,5},{7,4},{8,11},{9,10},{10,... | collective-permute-start | bytes 86024 | tf_op jit(solution)/shard_map/ppermute | solution.py:727
  41.1 19.9 %collective-permute-start.3 = (bf16[64,896]{1,0:T(8,128)(2,1)S(1)}, bf16[64,896]{1,0:T(8,128)(2,1)S(1)}, u32[]{:S(2)}, u32[]{:S(2)}) collective-permute-start(bf16[64,896]{1,0:T(8,128)(2,1)S(1)} %constant_dynamic-update-slice_fusion), channel_id=1, source_target_pairs={{0,4},{1,5},{2,6},{3,7},{4,0},{5,1},{6,2},{7,3},{8,12},{9,13},{10,... | collective-permute-start | bytes 344072 | tf_op jit(solution)/shard_map/ppermute | solution.py:727
  43.2 17.9 %collective-permute-start.4 = (bf16[64,896]{1,0:T(8,128)(2,1)S(1)}, bf16[64,896]{1,0:T(8,128)(2,1)S(1)}, u32[]{:S(2)}, u32[]{:S(2)}) collective-permute-start(bf16[64,896]{1,0:T(8,128)(2,1)S(1)} %constant_dynamic-update-slice_fusion), channel_id=1, source_target_pairs={{0,8},{1,9},{2,10},{3,11},{4,12},{5,13},{6,14},{7,15},{8,0},{9,1},... | collective-permute-start | bytes 344072 | tf_op jit(solution)/shard_map/ppermute | solution.py:727
  45.8 15.3 %collective-permute-start.5 = (bf16[64,896]{1,0:T(8,128)(2,1)S(1)}, bf16[64,896]{1,0:T(8,128)(2,1)S(1)}, u32[]{:S(2)}, u32[]{:S(2)}) collective-permute-start(bf16[64,896]{1,0:T(8,128)(2,1)S(1)} %constant_dynamic-update-slice_fusion), channel_id=1, source_target_pairs={{0,12},{1,13},{2,14},{3,15},{4,8},{5,9},{6,10},{7,11},{8,4},{9,5},... | collective-permute-start | bytes 344072 | tf_op jit(solution)/shard_map/ppermute | solution.py:727
  61.0 3.8 %copy-start = (bf16[1024,768]{1,0:T(8,128)(2,1)S(1)}, bf16[1024,768]{1,0:T(8,128)(2,1)}, u32[]{:S(2)}) copy-start(bf16[1024,768]{1,0:T(8,128)(2,1)} %get-tuple-element.167.refs_0_) | copy-start | bytes 4718596
  61.1 1.9 collective-permute-start.6
  71.8 6.1 %collective-permute-start.7 = (bf16[768,768]{1,0:T(8,128)(2,1)S(1)}, bf16[768,768]{1,0:T(8,128)(2,1)S(1)}, u32[]{:S(2)}, u32[]{:S(2)}) collective-permute-start(bf16[768,768]{1,0:T(8,128)(2,1)S(1)} %get-tuple-element.179), channel_id=1, source_target_pairs={{0,16},{1,17},{2,18},{3,19},{4,20},{5,21},{6,22},{7,23},{8,24},{9,... | collective-permute-start | bytes 3538952 | tf_op jit(solution)/shard_map/ppermute | solution.py:727
  71.9 9.0 %collective-permute-start.8 = (bf16[768,768]{1,0:T(8,128)(2,1)}, bf16[768,768]{1,0:T(8,128)(2,1)}, u32[]{:S(2)}, u32[]{:S(2)}) collective-permute-start(bf16[768,768]{1,0:T(8,128)(2,1)} %get-tuple-element.178), channel_id=1, source_target_pairs={{0,16},{1,17},{2,18},{3,19},{4,20},{5,21},{6,22},{7,23},{8,24},{9,... | collective-permute-start | bytes 3538952 | tf_op jit(solution)/shard_map/ppermute | solution.py:727
  79.2 18.8 %collective-permute-start.9 = (bf16[768,768]{1,0:T(8,128)(2,1)}, bf16[768,768]{1,0:T(8,128)(2,1)}, u32[]{:S(2)}, u32[]{:S(2)}) collective-permute-start(bf16[768,768]{1,0:T(8,128)(2,1)} %add_convert_fusion.3), channel_id=1, source_target_pairs={{0,1},{1,0},{2,3},{3,2},{4,5},{5,4},{6,7},{7,6},{8,9},{9,8},{10,11... | collective-permute-start | bytes 3538952 | tf_op jit(solution)/shard_map/ppermute | solution.py:727
  97.4 16.8 %collective-permute-start.12 = (bf16[192,3072]{1,0:T(8,128)(2,1)S(1)}, bf16[192,3072]{1,0:T(8,128)(2,1)S(1)}, u32[]{:S(2)}, u32[]{:S(2)}) collective-permute-start(bf16[192,3072]{1,0:T(8,128)(2,1)S(1)} %get-tuple-element.187), channel_id=1, source_target_pairs={{0,16},{1,17},{2,18},{3,19},{4,20},{5,21},{6,22},{7,23},{8,24},{9,... | collective-permute-start | bytes 3538952 | tf_op jit(solution)/shard_map/ppermute | solution.py:727
  97.4 15.7 %collective-permute-start.11 = (bf16[192,3072]{1,0:T(8,128)(2,1)S(1)}, bf16[192,3072]{1,0:T(8,128)(2,1)S(1)}, u32[]{:S(2)}, u32[]{:S(2)}) collective-permute-start(bf16[192,3072]{1,0:T(8,128)(2,1)S(1)} %get-tuple-element.188), channel_id=1, source_target_pairs={{0,16},{1,17},{2,18},{3,19},{4,20},{5,21},{6,22},{7,23},{8,24},{9,... | collective-permute-start | bytes 3538952 | tf_op jit(solution)/shard_map/ppermute | solution.py:727
  99.5 12.7 %collective-permute-start.10 = (bf16[384,768]{1,0:T(8,128)(2,1)S(1)}, bf16[384,768]{1,0:T(8,128)(2,1)S(1)}, u32[]{:S(2)}, u32[]{:S(2)}) collective-permute-start(bf16[384,768]{1,0:T(8,128)(2,1)S(1)} %get-tuple-element.289), channel_id=1, source_target_pairs={{0,2},{1,3},{2,0},{3,1},{4,6},{5,7},{6,4},{7,5},{8,10},{9,11},{10,... | collective-permute-start | bytes 1769480 | tf_op jit(solution)/shard_map/ppermute | solution.py:727
  112.4 25.1 %collective-permute-start.13 = (bf16[384,768]{1,0:T(8,128)(2,1)S(1)}, bf16[384,768]{1,0:T(8,128)(2,1)S(1)}, u32[]{:S(2)}, u32[]{:S(2)}) collective-permute-start(bf16[384,768]{1,0:T(8,128)(2,1)S(1)} %add_convert_fusion.15), channel_id=1, source_target_pairs={{0,4},{1,5},{2,6},{3,7},{4,0},{5,1},{6,2},{7,3},{8,12},{9,13},{10,... | collective-permute-start | bytes 1769480 | tf_op jit(solution)/shard_map/ppermute | solution.py:727
  113.6 27.6 %collective-permute-start.14 = (bf16[192,3072]{1,0:T(8,128)(2,1)S(1)}, bf16[192,3072]{1,0:T(8,128)(2,1)S(1)}, u32[]{:S(2)}, u32[]{:S(2)}) collective-permute-start(bf16[192,3072]{1,0:T(8,128)(2,1)S(1)} %add_convert_fusion.1), channel_id=1, source_target_pairs={{0,1},{1,0},{2,3},{3,2},{4,5},{5,4},{6,7},{7,6},{8,9},{9,8},{10,11... | collective-permute-start | bytes 3538952 | tf_op jit(solution)/shard_map/ppermute | solution.py:727
  136.9 11.6 %collective-permute-start.16 = (bf16[192,1536]{1,0:T(8,128)(2,1)S(1)}, bf16[192,1536]{1,0:T(8,128)(2,1)S(1)}, u32[]{:S(2)}, u32[]{:S(2)}) collective-permute-start(bf16[192,1536]{1,0:T(8,128)(2,1)S(1)} %get-tuple-element.202), channel_id=1, source_target_pairs={{0,16},{1,17},{2,18},{3,19},{4,20},{5,21},{6,22},{7,23},{8,24},{9,... | collective-permute-start | bytes 1769480 | tf_op jit(solution)/shard_map/ppermute | solution.py:727
  137.3 10.1 %collective-permute-start.15 = (bf16[192,1536]{1,0:T(8,128)(2,1)S(1)}, bf16[192,1536]{1,0:T(8,128)(2,1)S(1)}, u32[]{:S(2)}, u32[]{:S(2)}) collective-permute-start(bf16[192,1536]{1,0:T(8,128)(2,1)S(1)} %get-tuple-element.204), channel_id=1, source_target_pairs={{0,16},{1,17},{2,18},{3,19},{4,20},{5,21},{6,22},{7,23},{8,24},{9,... | collective-permute-start | bytes 1769480 | tf_op jit(solution)/shard_map/ppermute | solution.py:727
  137.7 17.4 %collective-permute-start.18 = (bf16[384,768]{1,0:T(8,128)(2,1)S(1)}, bf16[384,768]{1,0:T(8,128)(2,1)S(1)}, u32[]{:S(2)}, u32[]{:S(2)}) collective-permute-start(bf16[384,768]{1,0:T(8,128)(2,1)S(1)} %add_convert_fusion.14), channel_id=1, source_target_pairs={{0,8},{1,9},{2,10},{3,11},{4,12},{5,13},{6,14},{7,15},{8,0},{9,1},... | collective-permute-start | bytes 1769480 | tf_op jit(solution)/shard_map/ppermute | solution.py:727
  141.6 10.8 %collective-permute-start.17 = (bf16[96,3072]{1,0:T(8,128)(2,1)S(1)}, bf16[96,3072]{1,0:T(8,128)(2,1)S(1)}, u32[]{:S(2)}, u32[]{:S(2)}) collective-permute-start(bf16[96,3072]{1,0:T(8,128)(2,1)S(1)} %get-tuple-element.287), channel_id=1, source_target_pairs={{0,2},{1,3},{2,0},{3,1},{4,6},{5,7},{6,4},{7,5},{8,10},{9,11},{10,... | collective-permute-start | bytes 1769480 | tf_op jit(solution)/shard_map/ppermute | solution.py:727
  147.3 9.6 %collective-permute-start.20 = (bf16[192,1664]{1,0:T(8,128)(2,1)S(1)}, bf16[192,1664]{1,0:T(8,128)(2,1)S(1)}, u32[]{:S(2)}, u32[]{:S(2)}) collective-permute-start(bf16[192,1664]{1,0:T(8,128)(2,1)S(1)} %get-tuple-element.214), channel_id=1, source_target_pairs={{0,16},{1,17},{2,18},{3,19},{4,20},{5,21},{6,22},{7,23},{8,24},{9,... | collective-permute-start | bytes 1916936 | tf_op jit(solution)/shard_map/ppermute | solution.py:727
  147.5 10.7 %collective-permute-start.21 = (bf16[192,1536]{1,0:T(8,128)(2,1)S(1)}, bf16[192,1536]{1,0:T(8,128)(2,1)S(1)}, u32[]{:S(2)}, u32[]{:S(2)}) collective-permute-start(bf16[192,1536]{1,0:T(8,128)(2,1)S(1)} %add_convert_fusion.11), channel_id=1, source_target_pairs={{0,1},{1,0},{2,3},{3,2},{4,5},{5,4},{6,7},{7,6},{8,9},{9,8},{10,11... | collective-permute-start | bytes 1769480 | tf_op jit(solution)/shard_map/ppermute | solution.py:727
  148.7 7.1 %collective-permute-start.19 = (bf16[192,1664]{1,0:T(8,128)(2,1)S(1)}, bf16[192,1664]{1,0:T(8,128)(2,1)S(1)}, u32[]{:S(2)}, u32[]{:S(2)}) collective-permute-start(bf16[192,1664]{1,0:T(8,128)(2,1)S(1)} %get-tuple-element.218), channel_id=1, source_target_pairs={{0,16},{1,17},{2,18},{3,19},{4,20},{5,21},{6,22},{7,23},{8,24},{9,... | collective-permute-start | bytes 1916936 | tf_op jit(solution)/shard_map/ppermute | solution.py:727
  152.5 15.7 %collective-permute-start.22 = (bf16[96,3072]{1,0:T(8,128)(2,1)S(1)}, bf16[96,3072]{1,0:T(8,128)(2,1)S(1)}, u32[]{:S(2)}, u32[]{:S(2)}) collective-permute-start(bf16[96,3072]{1,0:T(8,128)(2,1)S(1)} %add_convert_fusion.9), channel_id=1, source_target_pairs={{0,4},{1,5},{2,6},{3,7},{4,0},{5,1},{6,2},{7,3},{8,12},{9,13},{10,... | collective-permute-start | bytes 1769480 | tf_op jit(solution)/shard_map/ppermute | solution.py:727
  155.2 15.8 %collective-permute-start.23 = (bf16[384,768]{1,0:T(8,128)(2,1)S(1)}, bf16[384,768]{1,0:T(8,128)(2,1)S(1)}, u32[]{:S(2)}, u32[]{:S(2)}) collective-permute-start(bf16[384,768]{1,0:T(8,128)(2,1)S(1)} %add_convert_fusion.8), channel_id=1, source_target_pairs={{0,2},{1,3},{2,0},{3,1},{4,6},{5,7},{6,4},{7,5},{8,10},{9,11},{10,... | collective-permute-start | bytes 1769480 | tf_op jit(solution)/shard_map/ppermute | solution.py:727
  156.0 24.1 %collective-permute-start.25 = (bf16[192,1664]{1,0:T(8,128)(2,1)S(1)}, bf16[192,1664]{1,0:T(8,128)(2,1)S(1)}, u32[]{:S(2)}, u32[]{:S(2)}) collective-permute-start(bf16[192,1664]{1,0:T(8,128)(2,1)S(1)} %add_convert_fusion.5), channel_id=1, source_target_pairs={{0,1},{1,0},{2,3},{3,2},{4,5},{5,4},{6,7},{7,6},{8,9},{9,8},{10,11... | collective-permute-start | bytes 1916936 | tf_op jit(solution)/shard_map/ppermute | solution.py:727
  158.4 21.2 %collective-permute-start.24 = (bf16[96,1536]{1,0:T(8,128)(2,1)S(1)}, bf16[96,1536]{1,0:T(8,128)(2,1)S(1)}, u32[]{:S(2)}, u32[]{:S(2)}) collective-permute-start(bf16[96,1536]{1,0:T(8,128)(2,1)S(1)} %get-tuple-element.293), channel_id=1, source_target_pairs={{0,2},{1,3},{2,0},{3,1},{4,6},{5,7},{6,4},{7,5},{8,10},{9,11},{10,... | collective-permute-start | bytes 884744 | tf_op jit(solution)/shard_map/ppermute | solution.py:727
  168.4 22.5 %collective-permute-start.26 = (bf16[96,3072]{1,0:T(8,128)(2,1)S(1)}, bf16[96,3072]{1,0:T(8,128)(2,1)S(1)}, u32[]{:S(2)}, u32[]{:S(2)}) collective-permute-start(bf16[96,3072]{1,0:T(8,128)(2,1)S(1)} %add_convert_fusion.7), channel_id=1, source_target_pairs={{0,8},{1,9},{2,10},{3,11},{4,12},{5,13},{6,14},{7,15},{8,0},{9,1},... | collective-permute-start | bytes 1769480 | tf_op jit(solution)/shard_map/ppermute | solution.py:727
  171.1 22.0 %collective-permute-start.27 = (bf16[768,768]{1,0:T(8,128)(2,1)S(1)}, bf16[768,768]{1,0:T(8,128)(2,1)S(1)}, u32[]{:S(2)}, u32[]{:S(2)}) collective-permute-start(bf16[768,768]{1,0:T(8,128)(2,1)S(1)} %constant_dynamic-update-slice_fusion.9.refs_0_), channel_id=1, source_target_pairs={{0,1},{1,0},{2,3},{3,2},{4,5},{5,4},{6,7},{7,6},{8,9},{9,8},{10,11... | collective-permute-start | bytes 3538952 | tf_op jit(solution)/shard_map/ppermute | solution.py:727
  179.7 13.3 %collective-permute-start.28 = (bf16[96,1536]{1,0:T(8,128)(2,1)S(1)}, bf16[96,1536]{1,0:T(8,128)(2,1)S(1)}, u32[]{:S(2)}, u32[]{:S(2)}) collective-permute-start(bf16[96,1536]{1,0:T(8,128)(2,1)S(1)} %add_convert_fusion.25), channel_id=1, source_target_pairs={{0,4},{1,5},{2,6},{3,7},{4,0},{5,1},{6,2},{7,3},{8,12},{9,13},{10,... | collective-permute-start | bytes 884744 | tf_op jit(solution)/shard_map/ppermute | solution.py:727
  180.2 16.0 %collective-permute-start.29 = (bf16[96,1664]{1,0:T(8,128)(2,1)S(1)}, bf16[96,1664]{1,0:T(8,128)(2,1)S(1)}, u32[]{:S(2)}, u32[]{:S(2)}) collective-permute-start(bf16[96,1664]{1,0:T(8,128)(2,1)S(1)} %get-tuple-element.291), channel_id=1, source_target_pairs={{0,2},{1,3},{2,0},{3,1},{4,6},{5,7},{6,4},{7,5},{8,10},{9,11},{10,... | collective-permute-start | bytes 958472 | tf_op jit(solution)/shard_map/ppermute | solution.py:727
  191.1 10.4 %collective-permute-start.30 = (bf16[96,3072]{1,0:T(8,128)(2,1)S(1)}, bf16[96,3072]{1,0:T(8,128)(2,1)S(1)}, u32[]{:S(2)}, u32[]{:S(2)}) collective-permute-start(bf16[96,3072]{1,0:T(8,128)(2,1)S(1)} %add_convert_fusion.6), channel_id=1, source_target_pairs={{0,2},{1,3},{2,0},{3,1},{4,6},{5,7},{6,4},{7,5},{8,10},{9,11},{10,... | collective-permute-start | bytes 1769480 | tf_op jit(solution)/shard_map/ppermute | solution.py:727
  191.2 22.3 %collective-permute-start.34 = (bf16[768,768]{1,0:T(8,128)(2,1)S(1)}, bf16[768,768]{1,0:T(8,128)(2,1)S(1)}, u32[]{:S(2)}, u32[]{:S(2)}) collective-permute-start(bf16[768,768]{1,0:T(8,128)(2,1)S(1)} %constant_dynamic-update-slice_fusion.9.refs_0_), channel_id=1, source_target_pairs={{0,16},{1,17},{2,18},{3,19},{4,20},{5,21},{6,22},{7,23},{8,24},{9,... | collective-permute-start | bytes 3538952 | tf_op jit(solution)/shard_map/ppermute | solution.py:727
  196.4 16.4 %collective-permute-start.31 = (bf16[96,1664]{1,0:T(8,128)(2,1)S(1)}, bf16[96,1664]{1,0:T(8,128)(2,1)S(1)}, u32[]{:S(2)}, u32[]{:S(2)}) collective-permute-start(bf16[96,1664]{1,0:T(8,128)(2,1)S(1)} %add_convert_fusion.20), channel_id=1, source_target_pairs={{0,4},{1,5},{2,6},{3,7},{4,0},{5,1},{6,2},{7,3},{8,12},{9,13},{10,... | collective-permute-start | bytes 958472 | tf_op jit(solution)/shard_map/ppermute | solution.py:727
  197.0 16.5 %collective-permute-start.35 = (bf16[768,768]{1,0:T(8,128)(2,1)S(1)}, bf16[768,768]{1,0:T(8,128)(2,1)S(1)}, u32[]{:S(2)}, u32[]{:S(2)}) collective-permute-start(bf16[768,768]{1,0:T(8,128)(2,1)S(1)} %collective-permute-done.27.refs_1_), channel_id=1, source_target_pairs={{0,16},{1,17},{2,18},{3,19},{4,20},{5,21},{6,22},{7,23},{8,24},{9,... | collective-permute-start | bytes 3538952 | tf_op jit(solution)/shard_map/ppermute | solution.py:727
  201.5 18.7 %collective-permute-start.36 = (bf16[192,3072]{1,0:T(8,128)(2,1)S(1)}, bf16[192,3072]{1,0:T(8,128)(2,1)S(1)}, u32[]{:S(2)}, u32[]{:S(2)}) collective-permute-start(bf16[192,3072]{1,0:T(8,128)(2,1)S(1)} %constant_dynamic-update-slice_fusion.11.refs_0_), channel_id=1, source_target_pairs={{0,1},{1,0},{2,3},{3,2},{4,5},{5,4},{6,7},{7,6},{8,9},{9,8},{10,11... | collective-permute-start | bytes 3538952 | tf_op jit(solution)/shard_map/ppermute | solution.py:727
  201.6 11.3 %collective-permute-start.32 = (bf16[96,1536]{1,0:T(8,128)(2,1)S(1)}, bf16[96,1536]{1,0:T(8,128)(2,1)S(1)}, u32[]{:S(2)}, u32[]{:S(2)}) collective-permute-start(bf16[96,1536]{1,0:T(8,128)(2,1)S(1)} %add_convert_fusion.24), channel_id=1, source_target_pairs={{0,8},{1,9},{2,10},{3,11},{4,12},{5,13},{6,14},{7,15},{8,0},{9,1},... | collective-permute-start | bytes 884744 | tf_op jit(solution)/shard_map/ppermute | solution.py:727
  212.8 10.4 %collective-permute-start.33 = (bf16[96,1664]{1,0:T(8,128)(2,1)S(1)}, bf16[96,1664]{1,0:T(8,128)(2,1)S(1)}, u32[]{:S(2)}, u32[]{:S(2)}) collective-permute-start(bf16[96,1664]{1,0:T(8,128)(2,1)S(1)} %add_convert_fusion.19), channel_id=1, source_target_pairs={{0,8},{1,9},{2,10},{3,11},{4,12},{5,13},{6,14},{7,15},{8,0},{9,1},... | collective-permute-start | bytes 958472 | tf_op jit(solution)/shard_map/ppermute | solution.py:727
  213.0 10.8 %collective-permute-start.37 = (bf16[96,1536]{1,0:T(8,128)(2,1)S(1)}, bf16[96,1536]{1,0:T(8,128)(2,1)S(1)}, u32[]{:S(2)}, u32[]{:S(2)}) collective-permute-start(bf16[96,1536]{1,0:T(8,128)(2,1)S(1)} %add_convert_fusion.23), channel_id=1, source_target_pairs={{0,2},{1,3},{2,0},{3,1},{4,6},{5,7},{6,4},{7,5},{8,10},{9,11},{10,... | collective-permute-start | bytes 884744 | tf_op jit(solution)/shard_map/ppermute | solution.py:727
  216.7 17.7 %collective-permute-start.39 = (bf16[192,3072]{1,0:T(8,128)(2,1)S(1)}, bf16[192,3072]{1,0:T(8,128)(2,1)S(1)}, u32[]{:S(2)}, u32[]{:S(2)}) collective-permute-start(bf16[192,3072]{1,0:T(8,128)(2,1)S(1)} %constant_dynamic-update-slice_fusion.11.refs_0_), channel_id=1, source_target_pairs={{0,16},{1,17},{2,18},{3,19},{4,20},{5,21},{6,22},{7,23},{8,24},{9,... | collective-permute-start | bytes 3538952 | tf_op jit(solution)/shard_map/ppermute | solution.py:727
  220.2 14.2 %collective-permute-start.40 = (bf16[192,3072]{1,0:T(8,128)(2,1)S(1)}, bf16[192,3072]{1,0:T(8,128)(2,1)S(1)}, u32[]{:S(2)}, u32[]{:S(2)}) collective-permute-start(bf16[192,3072]{1,0:T(8,128)(2,1)S(1)} %collective-permute-done.36.refs_1_), channel_id=1, source_target_pairs={{0,16},{1,17},{2,18},{3,19},{4,20},{5,21},{6,22},{7,23},{8,24},{9,... | collective-permute-start | bytes 3538952 | tf_op jit(solution)/shard_map/ppermute | solution.py:727
  223.3 10.5 %collective-permute-start.38 = (bf16[96,1664]{1,0:T(8,128)(2,1)S(1)}, bf16[96,1664]{1,0:T(8,128)(2,1)S(1)}, u32[]{:S(2)}, u32[]{:S(2)}) collective-permute-start(bf16[96,1664]{1,0:T(8,128)(2,1)S(1)} %add_convert_fusion.18), channel_id=1, source_target_pairs={{0,2},{1,3},{2,0},{3,1},{4,6},{5,7},{6,4},{7,5},{8,10},{9,11},{10,... | collective-permute-start | bytes 958472 | tf_op jit(solution)/shard_map/ppermute | solution.py:727
  223.8 10.6 %collective-permute-start.42 = (bf16[192,1536]{1,0:T(8,128)(2,1)S(1)}, bf16[192,1536]{1,0:T(8,128)(2,1)S(1)}, u32[]{:S(2)}, u32[]{:S(2)}) collective-permute-start(bf16[192,1536]{1,0:T(8,128)(2,1)S(1)} %constant_dynamic-update-slice_fusion.13.refs_0_), channel_id=1, source_target_pairs={{0,1},{1,0},{2,3},{3,2},{4,5},{5,4},{6,7},{7,6},{8,9},{9,8},{10,11... | collective-permute-start | bytes 1769480 | tf_op jit(solution)/shard_map/ppermute | solution.py:727
  233.8 10.5 %collective-permute-start.45 = (bf16[192,1664]{1,0:T(8,128)(2,1)S(1)}, bf16[192,1664]{1,0:T(8,128)(2,1)S(1)}, u32[]{:S(2)}, u32[]{:S(2)}) collective-permute-start(bf16[192,1664]{1,0:T(8,128)(2,1)S(1)} %constant_dynamic-update-slice_fusion.15.refs_0_), channel_id=1, source_target_pairs={{0,1},{1,0},{2,3},{3,2},{4,5},{5,4},{6,7},{7,6},{8,9},{9,8},{10,11... | collective-permute-start | bytes 1916936 | tf_op jit(solution)/shard_map/ppermute | solution.py:727
  234.4 12.4 %collective-permute-start.43 = (bf16[192,1536]{1,0:T(8,128)(2,1)S(1)}, bf16[192,1536]{1,0:T(8,128)(2,1)S(1)}, u32[]{:S(2)}, u32[]{:S(2)}) collective-permute-start(bf16[192,1536]{1,0:T(8,128)(2,1)S(1)} %collective-permute-done.42.refs_1_), channel_id=1, source_target_pairs={{0,16},{1,17},{2,18},{3,19},{4,20},{5,21},{6,22},{7,23},{8,24},{9,... | collective-permute-start | bytes 1769480 | tf_op jit(solution)/shard_map/ppermute | solution.py:727
  237.6 9.2 %collective-permute-start.41 = (bf16[192,1536]{1,0:T(8,128)(2,1)S(1)}, bf16[192,1536]{1,0:T(8,128)(2,1)S(1)}, u32[]{:S(2)}, u32[]{:S(2)}) collective-permute-start(bf16[192,1536]{1,0:T(8,128)(2,1)S(1)} %constant_dynamic-update-slice_fusion.13.refs_0_), channel_id=1, source_target_pairs={{0,16},{1,17},{2,18},{3,19},{4,20},{5,21},{6,22},{7,23},{8,24},{9,... | collective-permute-start | bytes 1769480 | tf_op jit(solution)/shard_map/ppermute | solution.py:727
  244.3 8.7 %collective-permute-start.46 = (bf16[192,1664]{1,0:T(8,128)(2,1)S(1)}, bf16[192,1664]{1,0:T(8,128)(2,1)S(1)}, u32[]{:S(2)}, u32[]{:S(2)}) collective-permute-start(bf16[192,1664]{1,0:T(8,128)(2,1)S(1)} %collective-permute-done.45.refs_1_), channel_id=1, source_target_pairs={{0,16},{1,17},{2,18},{3,19},{4,20},{5,21},{6,22},{7,23},{8,24},{9,... | collective-permute-start | bytes 1916936 | tf_op jit(solution)/shard_map/ppermute | solution.py:727
  249.3 3.7 %collective-permute-start.44 = (bf16[192,1664]{1,0:T(8,128)(2,1)S(1)}, bf16[192,1664]{1,0:T(8,128)(2,1)S(1)}, u32[]{:S(2)}, u32[]{:S(2)}) collective-permute-start(bf16[192,1664]{1,0:T(8,128)(2,1)S(1)} %constant_dynamic-update-slice_fusion.15.refs_0_), channel_id=1, source_target_pairs={{0,16},{1,17},{2,18},{3,19},{4,20},{5,21},{6,22},{7,23},{8,24},{9,... | collective-permute-start | bytes 1916936 | tf_op jit(solution)/shard_map/ppermute | solution.py:727
  (4 other events, 7.9 us)

commit v3 on v2

--- a/solution.py
+++ b/solution.py
@@ -517,28 +517,39 @@
 
 
 def attention_back_kernel(seq_len, q_ref, k_ref, v_ref, p_ref, dc_ref, stack_ref, d_ref, sums):
-    q, k, v, probs, dctx = (ref[...] for ref in (q_ref, k_ref, v_ref, p_ref, dc_ref))
-    count = q.shape[0]
-    cells = cells_of(count, seq_len)
+    count = q_ref.shape[0]
     factor = 1.0 / math.sqrt(HD)
-    spread_dctx = [two_heads(dctx[cell]) for cell in cells]
-    dprobs = [dot_t(v[cell], wide) for cell, wide in zip(cells, spread_dctx, strict=True)]
-    dvals = [dot(probs[cell], wide).astype(low) for cell, wide in zip(cells, spread_dctx, strict=True)]
-    dscores = []
-    for cell, dprob in zip(cells, dprobs, strict=True):
-        prob = probs[cell].astype(full)
-        dscores.append((prob * (dprob - columns_sum(prob * dprob))).astype(low))
-    dkeys = [(dot(ds, two_heads(q[cell])) * factor).astype(low) for cell, ds in zip(cells, dscores, strict=True)]
-    dqueries = [(own_head(t_dot(ds, k[cell])) * factor).astype(low) for cell, ds in zip(cells, dscores, strict=True)]
 
     @pl.when(pl.program_id(0) == 0)
     def _():
         sums[...] = jnp.zeros_like(sums)
 
-    for rank, pieces in enumerate((dqueries, dkeys, dvals)):
-        grad = joined(pieces, count, seq_len)
-        d_ref[rank] = grad
-        sums[rank : rank + 1, :] += columns_sum(grad.astype(full))
+    wide = 2 * 2 * HD
+
+    @pl.loop(0, D // wide)
+    def _(turn):
+        lanes = pl.ds(pl.multiple_of(turn * wide, LANES), wide)
+        q, k, v, probs, dctx = (ref[:, lanes] for ref in (q_ref, k_ref, v_ref, p_ref, dc_ref))
+        cells = [
+            (slice(start, start + seq_len), slice(first, first + 2 * HD))
+            for first in range(0, wide, 2 * HD)
+            for start in range(0, count, seq_len)
+        ]
+        spread_dctx = [two_heads(dctx[cell]) for cell in cells]
+        dprobs = [dot_t(v[cell], both) for cell, both in zip(cells, spread_dctx, strict=True)]
+        dvals = [dot(probs[cell], both).astype(low) for cell, both in zip(cells, spread_dctx, strict=True)]
+        dscores = []
+        for cell, dprob in zip(cells, dprobs, strict=True):
+            prob = probs[cell].astype(full)
+            dscores.append((prob * (dprob - columns_sum(prob * dprob))).astype(low))
+        dkeys = [(dot(ds, two_heads(q[cell])) * factor).astype(low) for cell, ds in zip(cells, dscores, strict=True)]
+        dqueries = [
+            (own_head(t_dot(ds, k[cell])) * factor).astype(low) for cell, ds in zip(cells, dscores, strict=True)
+        ]
+        for rank, pieces in enumerate((dqueries, dkeys, dvals)):
+            grad = joined(pieces, count, seq_len)
+            d_ref[rank, :, lanes] = grad
+            sums[rank : rank + 1, lanes] += columns_sum(grad.astype(full))
 
 
 def attention_backward(seq_len, q, k, v, probs, dctx, stack):

time: 260 us -> 248 us (0.954); the launches traced: 256 us -> 247 us
  Pallas kernels: 147 us -> 138 us
    pallas_call x2, Pallas kernels: 19.2 us -> 10.4 us  [square_gradient(): pl.pallas_call(functools.partial(square_grad_kernel, late), grid_spec=plt...]
  transfers between devices with their start and end apart: 47 -> 47, of which waited for: 14 -> 14; matrix products, arithmetic and copies ran while one was open for 4% -> 4% of each run, Pallas kernels for 45% -> 43%
where the time goes in v3:
time: 248 us; the launch traced here: 247 us
  Pallas kernels  138 us (56%)
  waiting for transfers between devices  63.4 us (26%)
  starting transfers between devices  32.7 us (13%)
  other arithmetic  8.58 us (3%)
  local copies, waits for them, and re-layouts  2.73 us (1%)
    ppermute x47, waiting for transfers between devices, swap(): return lax.ppermute(piece, ('stream', 'dp'), pairs)  63.4 us
    ppermute x47, starting transfers between devices, swap(): return lax.ppermute(piece, ('stream', 'dp'), pairs)  32.7 us
    pallas_call x2, Pallas kernels, ff_forward(): pl.pallas_call(functools.partial(ff_kernel, part, seq_len), grid=(hidden...  30.5 us
    pallas_call x8, Pallas kernels, spread(): pl.pallas_call(functools.partial(spread_kernel, widths, talls, first), gr...  22.7 us
    pallas_call x1, Pallas kernels, hidden_gradient(): pl.pallas_call(hidden_kernel, grid_spec=pltpu.PrefetchScalarGridSpec(num_...  14.9 us
    pallas_call x1, Pallas kernels, attention_forward(): pl.pallas_call(functools.partial(attention_kernel, seq_len), grid=(steps,...  14.1 us
    pallas_call x2, Pallas kernels, down_gradient(): pl.pallas_call(functools.partial(down_grad_kernel, seq_len, fresh), grid_...  12.5 us
    pallas_call x1, Pallas kernels, norm_one_backward(): pl.pallas_call(norm_one_kernel, grid=(hidden // D,), in_specs=[pl.BlockSp...  11 us
  transfers between devices with their start and end apart: 47, of which 14 were waited for; matrix products, arithmetic and copies ran while one was open for 4% of the time, Pallas kernels for 43%

profile of v3, /device:TPU:0, one launch (start us, length us, event | category | flops | bytes accessed | tf_op | source)
XLA Modules:
  0.0 247.2 jit_solution(8970708297746399784)
XLA Ops:
  1.3 14.1 %attention_forward.1 = (bf16[1024,768]{1,0:T(8,128)(2,1)}, bf16[1024,768]{1,0:T(8,128)(2,1)}, bf16[1024,768]{1,0:T(8,128)(2,1)}, bf16[1024,768]{1,0:T(8,128)(2,1...) custom-call(bf16[1024,768]{1,0:T(8,128)(2,1)} %bitcast.36, ...), custom_call_target="tpu_custom_call" | custom-call | flops 230000000 | bytes 1000 | tf_op jit(solution)/shard_map/attention_forward/pallas_call | solution.py:164
  15.5 5.7 %lead_forward.1 = (f32[16,768]{1,0:T(8,128)S(1)}, f32[16,768]{1,0:T(8,128)S(1)}, f32[16,128]{1,0:T(8,128)S(1)}, f32[16,128]{1,0:T(8,128)S(1)}, bf16[16,768]{1,0:T(8,128)(2,1)S(1)}) custom-call(f32[4,4,768]{2,1,0:T(4,128)S(1)} %get-tuple-element.149.nl_ref, f32[4,4,768]{2,1,0:T(4,128)S(1)} %get-tuple-element.150.hat_ref, bf16[768,3072]{1,0:T(8,128)(2,1)} %uw.7, ...), custom_call_target="tpu_custom_call" | custom-call | flops 69000000 | bytes 1000 | tf_op jit(solution)/shard_map/lead_forward/pallas_call | solution.py:207
  21.3 2.9 %collective-permute-start = (bf16[16,896]{1,0:T(8,128)(2,1)S(1)}, bf16[16,896]{1,0:T(8,128)(2,1)S(1)}, u32[]{:S(2)}, u32[]{:S(2)}) collective-permute-start(bf16[16,896]{1,0:T(8,128)(2,1)S(1)} %pad_maximum_fusion), channel_id=1, source_target_pairs={{0,1},{1,0},{2,3},{3,2},{4,5},{5,4},{6,7},{7,6},{8,9},{9,8},{10,11... | collective-permute-start | bytes 86024 | tf_op jit(solution)/shard_map/ppermute | solution.py:738
  24.2 1.5 collective-permute-start.1
  25.7 15.3 %ff_forward_0.1 = (bf16[1024,768]{1,0:T(8,128)(2,1)}, bf16[1024,3072]{1,0:T(8,128)(2,1)}, bf16[1024,3072]{1,0:T(8,128)(2,1)}, bf16[1024,768]{1,0:T(8,128)(2,1)},...) custom-call(bf16[1024,768]{1,0:T(8,128)(2,1)} %get-tuple-element.156.nl_ref, bf16[768,3072]{1,0:T(8,128)(2,1)} %uw.7, ...), custom_call_target="tpu_custom_call" | custom-call | flops 299000000 | bytes 1000 | tf_op jit(solution)/shard_map/ff_forward_0/pallas_call | solution.py:281
  41.1 2.1 collective-permute-start.3
  43.2 2.6 %collective-permute-start.4 = (bf16[64,896]{1,0:T(8,128)(2,1)S(1)}, bf16[64,896]{1,0:T(8,128)(2,1)S(1)}, u32[]{:S(2)}, u32[]{:S(2)}) collective-permute-start(bf16[64,896]{1,0:T(8,128)(2,1)S(1)} %constant_dynamic-update-slice_fusion), channel_id=1, source_target_pairs={{0,8},{1,9},{2,10},{3,11},{4,12},{5,13},{6,14},{7,15},{8,0},{9,1},... | collective-permute-start | bytes 344072 | tf_op jit(solution)/shard_map/ppermute | solution.py:738
  45.8 15.2 %ff_forward_1.1 = (bf16[1024,768]{1,0:T(8,128)(2,1)}, bf16[1024,3072]{1,0:T(8,128)(2,1)}, bf16[1024,3072]{1,0:T(8,128)(2,1)}, bf16[1024,768]{1,0:T(8,128)(2,1)},...) custom-call(bf16[1024,768]{1,0:T(8,128)(2,1)} %get-tuple-element.156, ...), custom_call_target="tpu_custom_call", output_to_operand_aliasing={{0}: (11, {}), {1}: (12, {}), {2}: (13, {}), {3}: (14, {}),... | custom-call | flops 299000000 | bytes 1000 | tf_op jit(solution)/shard_map/ff_forward_1/pallas_call | solution.py:281
  61.3 1.7 collective-permute-done.6.other_ref
  63.0 1.8 pair_loss.1
  64.8 6.9 %down_grad_4.1 = (bf16[768,768]{1,0:T(8,128)(2,1)}, bf16[768,768]{1,0:T(8,128)(2,1)S(1)}, bf16[1024,768]{1,0:T(8,128)(2,1)S(1)}, f32[1,768]{1,0:T(1,128)S(1)}) custom-call(s32[8]{0:T(128)S(1)} %stack.35.place, bf16[1024,768]{1,0:T(8,128)(2,1)S(1)} %copy-done, f32[16,768]{1,0:T(8,128)S(1)} %bitcast.34, f32[16,768]{1,0:T(8,128)S(1)} %get-tuple-element.175.refs_2_, ...), custom_call_target="tpu_custom_call" | custom-call | flops 92000000 | bytes 1000 | tf_op jit(solution)/shard_map/down_grad_4/pallas_call | solution.py:413
  72.2 5.6 %down_grad_0.1 = (bf16[768,768]{1,0:T(8,128)(2,1)S(1)}, bf16[768,768]{1,0:T(8,128)(2,1)S(1)}) custom-call(s32[8]{0:T(128)S(1)} %stack.35.place, bf16[1024,768]{1,0:T(8,128)(2,1)S(1)} %get-tuple-element.183.refs_0_.db_ref.branch_far, bf16[1024,3072]{1,0:T(8,128)(2,1)} %get-tuple-element.176.refs_3_.refs_1_), custom_call_target="tpu_custom_call" | custom-call | flops 92000000 | bytes 1000 | tf_op jit(solution)/shard_map/down_grad_0/pallas_call | solution.py:413
  77.8 1.3 add_convert_fusion.3
  79.1 1.7 collective-permute-start.9
  80.9 1.6 add_convert_fusion.2
  82.4 14.9 %hidden_gradient.1 = (bf16[1024,3072]{1,0:T(8,128)(2,1)}, f32[8,3072]{1,0:T(8,128)S(1)}, bf16[192,3072]{1,0:T(8,128)(2,1)S(1)}, bf16[192,3072]{1,0:T(8,128)(2,1)...) custom-call(s32[8]{0:T(128)S(1)} %stack.35.place, ...), custom_call_target="tpu_custom_call", output_to_operand_aliasing={{0}: (2, {})} | custom-call | flops 345000000 | bytes 1000 | tf_op jit(solution)/shard_map/hidden_gradient/pallas_call | solution.py:445
  97.9 1.6 add_convert_fusion.16
  99.4 1.6 collective-permute-start.10
  101.0 11.0 %norm_one_backward.1 = (bf16[4,1024,768]{2,1,0:T(8,128)(2,1)S(1)}, bf16[1024,768]{1,0:T(8,128)(2,1)S(1)}, f32[8,768]{1,0:T(8,128)S(1)}) custom-call(bf16[1024,3072]{1,0:T(8,128)(2,1)} %get-tuple-element.189.dpre_ref, bf16[768,3072]{1,0:T(8,128)(2,1)} %uw.7, f32[6,128]{1,0:T(8,128)} %bitcast.50, bf16[768,768]{1,0:T(8,128)(2,1)} %wo_far.1, ...), custom_call_target="tpu_custom_call" | custom-call | flops 299000000 | bytes 1000 | tf_op jit(solution)/shard_map/norm_one_backward/pallas_call | solution.py:501
  116.0 7.0 %attention_backward.1 = (bf16[4,1024,768]{2,1,0:T(8,128)(2,1)S(1)}, f32[8,768]{1,0:T(8,128)S(1)}) custom-call(bf16[1024,768]{1,0:T(8,128)(2,1)S(1)} %copy-done.1, bf16[1024,768]{1,0:T(8,128)(2,1)S(1)} %copy-done.2, bf16[1024,768]{1,0:T(8,128)(2,1)S(1)} %copy-done.3, bf16[1024,768]{1,0:T(8,128)(2,1)S(1)} %copy-done.4, ...), custom_call_target="tpu_custom_call", output_to_operand_aliasing={{0}: (5, {})} | custom-call | flops 184000000 | bytes 1000 | tf_op jit(solution)/shard_map/attention_backward/pallas_call | solution.py:559
  123.1 5.3 %value_gradient.1 = (bf16[192,1536]{1,0:T(8,128)(2,1)S(1)}, bf16[192,1536]{1,0:T(8,128)(2,1)S(1)}, bf16[192,1536]{1,0:T(8,128)(2,1)S(1)}, bf16[192,1536]{1,0:T(8,128)(2,1)S(1)}) custom-call(s32[8]{0:T(128)S(1)} %stack.35.place, bf16[1024,768]{1,0:T(8,128)(2,1)} %get-tuple-element.200.left_ref, bf16[4,1024,768]{2,1,0:T(8,128)(2,1)S(1)} %get-tuple-element.227.d_ref, ...), custom_call_target="tpu_custom_call" | custom-call | flops 138000000 | bytes 1000 | tf_op jit(solution)/shard_map/value_gradient/pallas_call | solution.py:612
  129.1 3.5 %collective-permute-start.18 = (bf16[384,768]{1,0:T(8,128)(2,1)S(1)}, bf16[384,768]{1,0:T(8,128)(2,1)S(1)}, u32[]{:S(2)}, u32[]{:S(2)}) collective-permute-start(bf16[384,768]{1,0:T(8,128)(2,1)S(1)} %add_convert_fusion.14), channel_id=1, source_target_pairs={{0,8},{1,9},{2,10},{3,11},{4,12},{5,13},{6,14},{7,15},{8,0},{9,1},... | collective-permute-start | bytes 1769480 | tf_op jit(solution)/shard_map/ppermute | solution.py:738
  133.6 5.1 %query_gradient.1 = (bf16[192,1664]{1,0:T(8,128)(2,1)S(1)}, bf16[192,1664]{1,0:T(8,128)(2,1)S(1)}, bf16[192,1664]{1,0:T(8,128)(2,1)S(1)}, bf16[192,1664]{1,0:T(8,128)(2,1)S(1)}) custom-call(s32[8]{0:T(128)S(1)} %stack.35.place, bf16[1024,768]{1,0:T(8,128)(2,1)} %bitcast.38, bf16[4,1024,768]{2,1,0:T(8,128)(2,1)S(1)} %get-tuple-element.227.d_ref, ...), custom_call_target="tpu_custom_call" | custom-call | flops 138000000 | bytes 1000 | tf_op jit(solution)/shard_map/query_gradient/pallas_call | solution.py:612
  139.0 1.0 collective-permute-start.21
  141.0 2.8 %collective-permute-done.17 = bf16[96,3072]{1,0:T(8,128)(2,1)S(1)} collective-permute-done((bf16[96,3072]{1,0:T(8,128)(2,1)S(1)}, bf16[96,3072]{1,0:T(8,128)(2,1)S(1)}, u32[]{:S(2)}, u32[]{:S(2)}) %collective-permute-start.17) | collective-permute-done | bytes 589856 | tf_op jit(solution)/shard_map/ppermute | solution.py:738
  144.0 2.5 %collective-permute-done.18 = bf16[384,768]{1,0:T(8,128)(2,1)S(1)} collective-permute-done((bf16[384,768]{1,0:T(8,128)(2,1)S(1)}, bf16[384,768]{1,0:T(8,128)(2,1)S(1)}, u32[]{:S(2)}, u32[]{:S(2)}) %collective-permute-start.18) | collective-permute-done | bytes 589856 | tf_op jit(solution)/shard_map/ppermute | solution.py:738
  148.5 1.2 collective-permute-done.21
  149.8 1.8 collective-permute-start.24
  151.6 8.1 %collective-permute-done.22 = bf16[96,3072]{1,0:T(8,128)(2,1)S(1)} collective-permute-done((bf16[96,3072]{1,0:T(8,128)(2,1)S(1)}, bf16[96,3072]{1,0:T(8,128)(2,1)S(1)}, u32[]{:S(2)}, u32[]{:S(2)}) %collective-permute-start.22) | collective-permute-done | bytes 589856 | tf_op jit(solution)/shard_map/ppermute | solution.py:738
  160.9 1.6 collective-permute-done.23
  163.4 7.7 %input_gradient.1 = f32[1024,768]{1,0:T(8,128)} custom-call(bf16[4,1024,768]{2,1,0:T(8,128)(2,1)S(1)} %get-tuple-element.227.d_ref, bf16[768,768]{1,0:T(8,128)(2,1)} %wq.3, bf16[768,768]{1,0:T(8,128)(2,1)} %wk.3, bf16[768,768]{1,0:T(8,128)(2,1)} %wv.3), custom_call_target="tpu_custom_call" | custom-call | flops 138000000 | bytes 1000 | tf_op jit(solution)/shard_map/input_gradient/pallas_call | solution.py:642
  171.7 1.5 collective-permute-start.29
  173.2 9.2 %collective-permute-done.26 = bf16[96,3072]{1,0:T(8,128)(2,1)S(1)} collective-permute-done((bf16[96,3072]{1,0:T(8,128)(2,1)S(1)}, bf16[96,3072]{1,0:T(8,128)(2,1)S(1)}, u32[]{:S(2)}, u32[]{:S(2)}) %collective-permute-start.26) | collective-permute-done | bytes 589856 | tf_op jit(solution)/shard_map/ppermute | solution.py:738
  182.7 1.6 collective-permute-done.27.refs_1_
  184.4 3.2 %down_spread_0.1.refs_2_ = f32[3072,768]{1,0:T(8,128)} custom-call(s32[8]{0:T(128)S(1)} %stack.35.place, bf16[768,768]{1,0:T(8,128)(2,1)S(1)} %constant_dynamic-update-slice_fusion.9.refs_0_, bf16[768,768]{1,0:T(8,128)(2,1)S(1)} %collective-permute-done.27.refs_1_), custom_call_target="tpu_custom_call" | custom-call | flops 69000000 | bytes 1000 | tf_op jit(solution)/shard_map/down_spread_0/pallas_call | solution.py:694
  188.4 4.5 %collective-permute-done.30 = bf16[96,3072]{1,0:T(8,128)(2,1)S(1)} collective-permute-done((bf16[96,3072]{1,0:T(8,128)(2,1)S(1)}, bf16[96,3072]{1,0:T(8,128)(2,1)S(1)}, u32[]{:S(2)}, u32[]{:S(2)}) %collective-permute-start.30) | collective-permute-done | bytes 589856 | tf_op jit(solution)/shard_map/ppermute | solution.py:738
  193.1 11.1 %collective-permute-done.31 = bf16[96,1664]{1,0:T(8,128)(2,1)S(1)} collective-permute-done((bf16[96,1664]{1,0:T(8,128)(2,1)S(1)}, bf16[96,1664]{1,0:T(8,128)(2,1)S(1)}, u32[]{:S(2)}, u32[]{:S(2)}) %collective-permute-start.31) | collective-permute-done | bytes 319520 | tf_op jit(solution)/shard_map/ppermute | solution.py:738
  205.0 3.2 %down_spread_4.1 = f32[3072,768]{1,0:T(8,128)} custom-call(s32[8]{0:T(128)S(1)} %stack.35.place, bf16[768,768]{1,0:T(8,128)(2,1)S(1)} %collective-permute-done.34.refs_0_, bf16[768,768]{1,0:T(8,128)(2,1)S(1)} %collective-permute-done.35.refs_1_, f32[3072,768]{1,0:T(8,128)} %down_spread_0.1.refs_2_), custom_call_target="tpu_custom_call", output_to_operand_aliasing={{}: (3, {})} | custom-call | flops 69000000 | bytes 1000 | tf_op jit(solution)/shard_map/down_spread_4/pallas_call | solution.py:694
  208.1 3.6 %collective-permute-done.36.refs_1_ = bf16[192,3072]{1,0:T(8,128)(2,1)S(1)} collective-permute-done((bf16[192,3072]{1,0:T(8,128)(2,1)S(1)}, bf16[192,3072]{1,0:T(8,128)(2,1)S(1)}, u32[]{:S(2)}, u32[]{:S(2)}) %collective-permute-start.36) | collective-permute-done | bytes 1179680 | tf_op jit(solution)/shard_map/ppermute | solution.py:738
  211.7 2.9 %collective-permute-done.33 = bf16[96,1664]{1,0:T(8,128)(2,1)S(1)} collective-permute-done((bf16[96,1664]{1,0:T(8,128)(2,1)S(1)}, bf16[96,1664]{1,0:T(8,128)(2,1)S(1)}, u32[]{:S(2)}, u32[]{:S(2)}) %collective-permute-start.33) | collective-permute-done | bytes 319520 | tf_op jit(solution)/shard_map/ppermute | solution.py:738
  216.1 3.2 %up_spread_0.1.refs_2_ = f32[768,3072]{1,0:T(8,128)} custom-call(s32[8]{0:T(128)S(1)} %stack.35.place, bf16[192,3072]{1,0:T(8,128)(2,1)S(1)} %constant_dynamic-update-slice_fusion.11.refs_0_, bf16[192,3072]{1,0:T(8,128)(2,1)S(1)} %collective-permute-done.36.refs_1_), custom_call_target="tpu_custom_call" | custom-call | flops 69000000 | bytes 1000 | tf_op jit(solution)/shard_map/up_spread_0/pallas_call | solution.py:694
  219.3 5.9 %collective-permute-done.38 = bf16[96,1664]{1,0:T(8,128)(2,1)S(1)} collective-permute-done((bf16[96,1664]{1,0:T(8,128)(2,1)S(1)}, bf16[96,1664]{1,0:T(8,128)(2,1)S(1)}, u32[]{:S(2)}, u32[]{:S(2)}) %collective-permute-start.38) | collective-permute-done | bytes 319520 | tf_op jit(solution)/shard_map/ppermute | solution.py:738
  225.5 3.2 %up_spread_4.1 = f32[768,3072]{1,0:T(8,128)} custom-call(s32[8]{0:T(128)S(1)} %stack.35.place, bf16[192,3072]{1,0:T(8,128)(2,1)S(1)} %collective-permute-done.39.refs_0_, bf16[192,3072]{1,0:T(8,128)(2,1)S(1)} %collective-permute-done.40.refs_1_, f32[768,3072]{1,0:T(8,128)} %up_spread_0.1.refs_2_), custom_call_target="tpu_custom_call", output_to_operand_aliasing={{}: (3, {})} | custom-call | flops 69000000 | bytes 1000 | tf_op jit(solution)/shard_map/up_spread_4/pallas_call | solution.py:694
  229.2 6.6 %collective-permute-done.45.refs_1_ = bf16[192,1664]{1,0:T(8,128)(2,1)S(1)} collective-permute-done((bf16[192,1664]{1,0:T(8,128)(2,1)S(1)}, bf16[192,1664]{1,0:T(8,128)(2,1)S(1)}, u32[]{:S(2)}, u32[]{:S(2)}) %collective-permute-start.45) | collective-permute-done | bytes 639008 | tf_op jit(solution)/shard_map/ppermute | solution.py:738
  235.8 2.5 %value_spread_0.1 = (f32[768,768]{1,0:T(8,128)}, f32[768,768]{1,0:T(8,128)}) custom-call(s32[8]{0:T(128)S(1)} %stack.35.place, bf16[192,1536]{1,0:T(8,128)(2,1)S(1)} %constant_dynamic-update-slice_fusion.13.refs_0_, bf16[192,1536]{1,0:T(8,128)(2,1)S(1)} %collective-permute-done.42.refs_1_), custom_call_target="tpu_custom_call" | custom-call | flops 69000000 | bytes 1000 | tf_op jit(solution)/shard_map/value_spread_0/pallas_call | solution.py:694
  238.3 2.5 %value_spread_4.1 = (f32[768,768]{1,0:T(8,128)}, f32[768,768]{1,0:T(8,128)}) custom-call(s32[8]{0:T(128)S(1)} %stack.35.place, bf16[192,1536]{1,0:T(8,128)(2,1)S(1)} %collective-permute-done.41.refs_0_, bf16[192,1536]{1,0:T(8,128)(2,1)S(1)} %collective-permute-done.43.refs_1_, ...), custom_call_target="tpu_custom_call", output_to_operand_aliasing={{0}: (3, {}), {1}: (4, {})} | custom-call | flops 69000000 | bytes 1000 | tf_op jit(solution)/shard_map/value_spread_4/pallas_call | solution.py:694
  241.9 2.5 %query_spread_0.1 = (f32[768,768]{1,0:T(8,128)}, f32[768,768]{1,0:T(8,128)}, f32[24,128]{1,0:T(8,128)S(1)}, f32[6,128]{1,0:T(8,128)S(1)}, f32[6,128]{1,0:T(8,128...) custom-call(s32[8]{0:T(128)S(1)} %stack.35.place, ...), custom_call_target="tpu_custom_call" | custom-call | flops 69000000 | bytes 1000 | tf_op jit(solution)/shard_map/query_spread_0/pallas_call | solution.py:694
  244.4 2.6 %query_spread_4.1 = (f32[768,768]{1,0:T(8,128)}, f32[768,768]{1,0:T(8,128)}, f32[24,128]{1,0:T(8,128)}, f32[6,128]{1,0:T(8,128)}, f32[6,128]{1,0:T(8,128)}, /*in...) custom-call(s32[8]{0:T(128)S(1)} %stack.35.place, ...), custom_call_target="tpu_custom_call", output_to_operand_aliasing={{0}: (12, {}), {1}: (13, {})} | custom-call | flops 69000000 | bytes 1000 | tf_op jit(solution)/shard_map/query_spread_4/pallas_call | solution.py:694
  (136 shorter events, 19.4 us)
Async XLA Ops:
  21.3 19.8 %collective-permute-start = (bf16[16,896]{1,0:T(8,128)(2,1)S(1)}, bf16[16,896]{1,0:T(8,128)(2,1)S(1)}, u32[]{:S(2)}, u32[]{:S(2)}) collective-permute-start(bf16[16,896]{1,0:T(8,128)(2,1)S(1)} %pad_maximum_fusion), channel_id=1, source_target_pairs={{0,1},{1,0},{2,3},{3,2},{4,5},{5,4},{6,7},{7,6},{8,9},{9,8},{10,11... | collective-permute-start | bytes 86024 | tf_op jit(solution)/shard_map/ppermute | solution.py:738
  24.2 16.8 %collective-permute-start.1 = (bf16[16,896]{1,0:T(8,128)(2,1)S(1)}, bf16[16,896]{1,0:T(8,128)(2,1)S(1)}, u32[]{:S(2)}, u32[]{:S(2)}) collective-permute-start(bf16[16,896]{1,0:T(8,128)(2,1)S(1)} %pad_maximum_fusion), channel_id=1, source_target_pairs={{0,2},{1,3},{2,0},{3,1},{4,6},{5,7},{6,4},{7,5},{8,10},{9,11},{10,... | collective-permute-start | bytes 86024 | tf_op jit(solution)/shard_map/ppermute | solution.py:738
  25.7 15.3 %collective-permute-start.2 = (bf16[16,896]{1,0:T(8,128)(2,1)S(1)}, bf16[16,896]{1,0:T(8,128)(2,1)S(1)}, u32[]{:S(2)}, u32[]{:S(2)}) collective-permute-start(bf16[16,896]{1,0:T(8,128)(2,1)S(1)} %pad_maximum_fusion), channel_id=1, source_target_pairs={{0,3},{1,2},{2,1},{3,0},{4,7},{5,6},{6,5},{7,4},{8,11},{9,10},{10,... | collective-permute-start | bytes 86024 | tf_op jit(solution)/shard_map/ppermute | solution.py:738
  41.1 19.9 %collective-permute-start.3 = (bf16[64,896]{1,0:T(8,128)(2,1)S(1)}, bf16[64,896]{1,0:T(8,128)(2,1)S(1)}, u32[]{:S(2)}, u32[]{:S(2)}) collective-permute-start(bf16[64,896]{1,0:T(8,128)(2,1)S(1)} %constant_dynamic-update-slice_fusion), channel_id=1, source_target_pairs={{0,4},{1,5},{2,6},{3,7},{4,0},{5,1},{6,2},{7,3},{8,12},{9,13},{10,... | collective-permute-start | bytes 344072 | tf_op jit(solution)/shard_map/ppermute | solution.py:738
  43.2 17.9 %collective-permute-start.4 = (bf16[64,896]{1,0:T(8,128)(2,1)S(1)}, bf16[64,896]{1,0:T(8,128)(2,1)S(1)}, u32[]{:S(2)}, u32[]{:S(2)}) collective-permute-start(bf16[64,896]{1,0:T(8,128)(2,1)S(1)} %constant_dynamic-update-slice_fusion), channel_id=1, source_target_pairs={{0,8},{1,9},{2,10},{3,11},{4,12},{5,13},{6,14},{7,15},{8,0},{9,1},... | collective-permute-start | bytes 344072 | tf_op jit(solution)/shard_map/ppermute | solution.py:738
  45.8 15.3 %collective-permute-start.5 = (bf16[64,896]{1,0:T(8,128)(2,1)S(1)}, bf16[64,896]{1,0:T(8,128)(2,1)S(1)}, u32[]{:S(2)}, u32[]{:S(2)}) collective-permute-start(bf16[64,896]{1,0:T(8,128)(2,1)S(1)} %constant_dynamic-update-slice_fusion), channel_id=1, source_target_pairs={{0,12},{1,13},{2,14},{3,15},{4,8},{5,9},{6,10},{7,11},{8,4},{9,5},... | collective-permute-start | bytes 344072 | tf_op jit(solution)/shard_map/ppermute | solution.py:738
  61.0 3.8 %copy-start = (bf16[1024,768]{1,0:T(8,128)(2,1)S(1)}, bf16[1024,768]{1,0:T(8,128)(2,1)}, u32[]{:S(2)}) copy-start(bf16[1024,768]{1,0:T(8,128)(2,1)} %get-tuple-element.167.refs_0_) | copy-start | bytes 4718596
  61.1 1.9 collective-permute-start.6
  71.7 6.1 %collective-permute-start.7 = (bf16[768,768]{1,0:T(8,128)(2,1)S(1)}, bf16[768,768]{1,0:T(8,128)(2,1)S(1)}, u32[]{:S(2)}, u32[]{:S(2)}) collective-permute-start(bf16[768,768]{1,0:T(8,128)(2,1)S(1)} %get-tuple-element.179), channel_id=1, source_target_pairs={{0,16},{1,17},{2,18},{3,19},{4,20},{5,21},{6,22},{7,23},{8,24},{9,... | collective-permute-start | bytes 3538952 | tf_op jit(solution)/shard_map/ppermute | solution.py:738
  71.8 9.0 %collective-permute-start.8 = (bf16[768,768]{1,0:T(8,128)(2,1)}, bf16[768,768]{1,0:T(8,128)(2,1)}, u32[]{:S(2)}, u32[]{:S(2)}) collective-permute-start(bf16[768,768]{1,0:T(8,128)(2,1)} %get-tuple-element.178), channel_id=1, source_target_pairs={{0,16},{1,17},{2,18},{3,19},{4,20},{5,21},{6,22},{7,23},{8,24},{9,... | collective-permute-start | bytes 3538952 | tf_op jit(solution)/shard_map/ppermute | solution.py:738
  79.1 18.8 %collective-permute-start.9 = (bf16[768,768]{1,0:T(8,128)(2,1)}, bf16[768,768]{1,0:T(8,128)(2,1)}, u32[]{:S(2)}, u32[]{:S(2)}) collective-permute-start(bf16[768,768]{1,0:T(8,128)(2,1)} %add_convert_fusion.3), channel_id=1, source_target_pairs={{0,1},{1,0},{2,3},{3,2},{4,5},{5,4},{6,7},{7,6},{8,9},{9,8},{10,11... | collective-permute-start | bytes 3538952 | tf_op jit(solution)/shard_map/ppermute | solution.py:738
  97.3 16.8 %collective-permute-start.12 = (bf16[192,3072]{1,0:T(8,128)(2,1)S(1)}, bf16[192,3072]{1,0:T(8,128)(2,1)S(1)}, u32[]{:S(2)}, u32[]{:S(2)}) collective-permute-start(bf16[192,3072]{1,0:T(8,128)(2,1)S(1)} %get-tuple-element.187), channel_id=1, source_target_pairs={{0,16},{1,17},{2,18},{3,19},{4,20},{5,21},{6,22},{7,23},{8,24},{9,... | collective-permute-start | bytes 3538952 | tf_op jit(solution)/shard_map/ppermute | solution.py:738
  97.4 15.7 %collective-permute-start.11 = (bf16[192,3072]{1,0:T(8,128)(2,1)S(1)}, bf16[192,3072]{1,0:T(8,128)(2,1)S(1)}, u32[]{:S(2)}, u32[]{:S(2)}) collective-permute-start(bf16[192,3072]{1,0:T(8,128)(2,1)S(1)} %get-tuple-element.188), channel_id=1, source_target_pairs={{0,16},{1,17},{2,18},{3,19},{4,20},{5,21},{6,22},{7,23},{8,24},{9,... | collective-permute-start | bytes 3538952 | tf_op jit(solution)/shard_map/ppermute | solution.py:738
  99.4 12.7 %collective-permute-start.10 = (bf16[384,768]{1,0:T(8,128)(2,1)S(1)}, bf16[384,768]{1,0:T(8,128)(2,1)S(1)}, u32[]{:S(2)}, u32[]{:S(2)}) collective-permute-start(bf16[384,768]{1,0:T(8,128)(2,1)S(1)} %get-tuple-element.289), channel_id=1, source_target_pairs={{0,2},{1,3},{2,0},{3,1},{4,6},{5,7},{6,4},{7,5},{8,10},{9,11},{10,... | collective-permute-start | bytes 1769480 | tf_op jit(solution)/shard_map/ppermute | solution.py:738
  112.3 16.7 %collective-permute-start.13 = (bf16[384,768]{1,0:T(8,128)(2,1)S(1)}, bf16[384,768]{1,0:T(8,128)(2,1)S(1)}, u32[]{:S(2)}, u32[]{:S(2)}) collective-permute-start(bf16[384,768]{1,0:T(8,128)(2,1)S(1)} %add_convert_fusion.15), channel_id=1, source_target_pairs={{0,4},{1,5},{2,6},{3,7},{4,0},{5,1},{6,2},{7,3},{8,12},{9,13},{10,... | collective-permute-start | bytes 1769480 | tf_op jit(solution)/shard_map/ppermute | solution.py:738
  113.5 19.2 %collective-permute-start.14 = (bf16[192,3072]{1,0:T(8,128)(2,1)S(1)}, bf16[192,3072]{1,0:T(8,128)(2,1)S(1)}, u32[]{:S(2)}, u32[]{:S(2)}) collective-permute-start(bf16[192,3072]{1,0:T(8,128)(2,1)S(1)} %add_convert_fusion.1), channel_id=1, source_target_pairs={{0,1},{1,0},{2,3},{3,2},{4,5},{5,4},{6,7},{7,6},{8,9},{9,8},{10,11... | collective-permute-start | bytes 3538952 | tf_op jit(solution)/shard_map/ppermute | solution.py:738
  128.3 11.6 %collective-permute-start.16 = (bf16[192,1536]{1,0:T(8,128)(2,1)S(1)}, bf16[192,1536]{1,0:T(8,128)(2,1)S(1)}, u32[]{:S(2)}, u32[]{:S(2)}) collective-permute-start(bf16[192,1536]{1,0:T(8,128)(2,1)S(1)} %get-tuple-element.202), channel_id=1, source_target_pairs={{0,16},{1,17},{2,18},{3,19},{4,20},{5,21},{6,22},{7,23},{8,24},{9,... | collective-permute-start | bytes 1769480 | tf_op jit(solution)/shard_map/ppermute | solution.py:738
  128.7 10.1 %collective-permute-start.15 = (bf16[192,1536]{1,0:T(8,128)(2,1)S(1)}, bf16[192,1536]{1,0:T(8,128)(2,1)S(1)}, u32[]{:S(2)}, u32[]{:S(2)}) collective-permute-start(bf16[192,1536]{1,0:T(8,128)(2,1)S(1)} %get-tuple-element.204), channel_id=1, source_target_pairs={{0,16},{1,17},{2,18},{3,19},{4,20},{5,21},{6,22},{7,23},{8,24},{9,... | collective-permute-start | bytes 1769480 | tf_op jit(solution)/shard_map/ppermute | solution.py:738
  129.1 17.4 %collective-permute-start.18 = (bf16[384,768]{1,0:T(8,128)(2,1)S(1)}, bf16[384,768]{1,0:T(8,128)(2,1)S(1)}, u32[]{:S(2)}, u32[]{:S(2)}) collective-permute-start(bf16[384,768]{1,0:T(8,128)(2,1)S(1)} %add_convert_fusion.14), channel_id=1, source_target_pairs={{0,8},{1,9},{2,10},{3,11},{4,12},{5,13},{6,14},{7,15},{8,0},{9,1},... | collective-permute-start | bytes 1769480 | tf_op jit(solution)/shard_map/ppermute | solution.py:738
  133.1 10.8 %collective-permute-start.17 = (bf16[96,3072]{1,0:T(8,128)(2,1)S(1)}, bf16[96,3072]{1,0:T(8,128)(2,1)S(1)}, u32[]{:S(2)}, u32[]{:S(2)}) collective-permute-start(bf16[96,3072]{1,0:T(8,128)(2,1)S(1)} %get-tuple-element.287), channel_id=1, source_target_pairs={{0,2},{1,3},{2,0},{3,1},{4,6},{5,7},{6,4},{7,5},{8,10},{9,11},{10,... | collective-permute-start | bytes 1769480 | tf_op jit(solution)/shard_map/ppermute | solution.py:738
  138.7 9.6 %collective-permute-start.20 = (bf16[192,1664]{1,0:T(8,128)(2,1)S(1)}, bf16[192,1664]{1,0:T(8,128)(2,1)S(1)}, u32[]{:S(2)}, u32[]{:S(2)}) collective-permute-start(bf16[192,1664]{1,0:T(8,128)(2,1)S(1)} %get-tuple-element.214), channel_id=1, source_target_pairs={{0,16},{1,17},{2,18},{3,19},{4,20},{5,21},{6,22},{7,23},{8,24},{9,... | collective-permute-start | bytes 1916936 | tf_op jit(solution)/shard_map/ppermute | solution.py:738
  139.0 10.7 %collective-permute-start.21 = (bf16[192,1536]{1,0:T(8,128)(2,1)S(1)}, bf16[192,1536]{1,0:T(8,128)(2,1)S(1)}, u32[]{:S(2)}, u32[]{:S(2)}) collective-permute-start(bf16[192,1536]{1,0:T(8,128)(2,1)S(1)} %add_convert_fusion.11), channel_id=1, source_target_pairs={{0,1},{1,0},{2,3},{3,2},{4,5},{5,4},{6,7},{7,6},{8,9},{9,8},{10,11... | collective-permute-start | bytes 1769480 | tf_op jit(solution)/shard_map/ppermute | solution.py:738
  140.1 7.1 %collective-permute-start.19 = (bf16[192,1664]{1,0:T(8,128)(2,1)S(1)}, bf16[192,1664]{1,0:T(8,128)(2,1)S(1)}, u32[]{:S(2)}, u32[]{:S(2)}) collective-permute-start(bf16[192,1664]{1,0:T(8,128)(2,1)S(1)} %get-tuple-element.218), channel_id=1, source_target_pairs={{0,16},{1,17},{2,18},{3,19},{4,20},{5,21},{6,22},{7,23},{8,24},{9,... | collective-permute-start | bytes 1916936 | tf_op jit(solution)/shard_map/ppermute | solution.py:738
  144.0 15.7 %collective-permute-start.22 = (bf16[96,3072]{1,0:T(8,128)(2,1)S(1)}, bf16[96,3072]{1,0:T(8,128)(2,1)S(1)}, u32[]{:S(2)}, u32[]{:S(2)}) collective-permute-start(bf16[96,3072]{1,0:T(8,128)(2,1)S(1)} %add_convert_fusion.9), channel_id=1, source_target_pairs={{0,4},{1,5},{2,6},{3,7},{4,0},{5,1},{6,2},{7,3},{8,12},{9,13},{10,... | collective-permute-start | bytes 1769480 | tf_op jit(solution)/shard_map/ppermute | solution.py:738
  146.7 15.8 %collective-permute-start.23 = (bf16[384,768]{1,0:T(8,128)(2,1)S(1)}, bf16[384,768]{1,0:T(8,128)(2,1)S(1)}, u32[]{:S(2)}, u32[]{:S(2)}) collective-permute-start(bf16[384,768]{1,0:T(8,128)(2,1)S(1)} %add_convert_fusion.8), channel_id=1, source_target_pairs={{0,2},{1,3},{2,0},{3,1},{4,6},{5,7},{6,4},{7,5},{8,10},{9,11},{10,... | collective-permute-start | bytes 1769480 | tf_op jit(solution)/shard_map/ppermute | solution.py:738
  147.4 24.1 %collective-permute-start.25 = (bf16[192,1664]{1,0:T(8,128)(2,1)S(1)}, bf16[192,1664]{1,0:T(8,128)(2,1)S(1)}, u32[]{:S(2)}, u32[]{:S(2)}) collective-permute-start(bf16[192,1664]{1,0:T(8,128)(2,1)S(1)} %add_convert_fusion.5), channel_id=1, source_target_pairs={{0,1},{1,0},{2,3},{3,2},{4,5},{5,4},{6,7},{7,6},{8,9},{9,8},{10,11... | collective-permute-start | bytes 1916936 | tf_op jit(solution)/shard_map/ppermute | solution.py:738
  149.8 21.2 %collective-permute-start.24 = (bf16[96,1536]{1,0:T(8,128)(2,1)S(1)}, bf16[96,1536]{1,0:T(8,128)(2,1)S(1)}, u32[]{:S(2)}, u32[]{:S(2)}) collective-permute-start(bf16[96,1536]{1,0:T(8,128)(2,1)S(1)} %get-tuple-element.293), channel_id=1, source_target_pairs={{0,2},{1,3},{2,0},{3,1},{4,6},{5,7},{6,4},{7,5},{8,10},{9,11},{10,... | collective-permute-start | bytes 884744 | tf_op jit(solution)/shard_map/ppermute | solution.py:738
  159.9 22.5 %collective-permute-start.26 = (bf16[96,3072]{1,0:T(8,128)(2,1)S(1)}, bf16[96,3072]{1,0:T(8,128)(2,1)S(1)}, u32[]{:S(2)}, u32[]{:S(2)}) collective-permute-start(bf16[96,3072]{1,0:T(8,128)(2,1)S(1)} %add_convert_fusion.7), channel_id=1, source_target_pairs={{0,8},{1,9},{2,10},{3,11},{4,12},{5,13},{6,14},{7,15},{8,0},{9,1},... | collective-permute-start | bytes 1769480 | tf_op jit(solution)/shard_map/ppermute | solution.py:738
  162.5 21.8 %collective-permute-start.27 = (bf16[768,768]{1,0:T(8,128)(2,1)S(1)}, bf16[768,768]{1,0:T(8,128)(2,1)S(1)}, u32[]{:S(2)}, u32[]{:S(2)}) collective-permute-start(bf16[768,768]{1,0:T(8,128)(2,1)S(1)} %constant_dynamic-update-slice_fusion.9.refs_0_), channel_id=1, source_target_pairs={{0,1},{1,0},{2,3},{3,2},{4,5},{5,4},{6,7},{7,6},{8,9},{9,8},{10,11... | collective-permute-start | bytes 3538952 | tf_op jit(solution)/shard_map/ppermute | solution.py:738
  171.2 13.2 %collective-permute-start.28 = (bf16[96,1536]{1,0:T(8,128)(2,1)S(1)}, bf16[96,1536]{1,0:T(8,128)(2,1)S(1)}, u32[]{:S(2)}, u32[]{:S(2)}) collective-permute-start(bf16[96,1536]{1,0:T(8,128)(2,1)S(1)} %add_convert_fusion.25), channel_id=1, source_target_pairs={{0,4},{1,5},{2,6},{3,7},{4,0},{5,1},{6,2},{7,3},{8,12},{9,13},{10,... | collective-permute-start | bytes 884744 | tf_op jit(solution)/shard_map/ppermute | solution.py:738
  171.7 15.9 %collective-permute-start.29 = (bf16[96,1664]{1,0:T(8,128)(2,1)S(1)}, bf16[96,1664]{1,0:T(8,128)(2,1)S(1)}, u32[]{:S(2)}, u32[]{:S(2)}) collective-permute-start(bf16[96,1664]{1,0:T(8,128)(2,1)S(1)} %get-tuple-element.291), channel_id=1, source_target_pairs={{0,2},{1,3},{2,0},{3,1},{4,6},{5,7},{6,4},{7,5},{8,10},{9,11},{10,... | collective-permute-start | bytes 958472 | tf_op jit(solution)/shard_map/ppermute | solution.py:738
  182.6 10.4 %collective-permute-start.30 = (bf16[96,3072]{1,0:T(8,128)(2,1)S(1)}, bf16[96,3072]{1,0:T(8,128)(2,1)S(1)}, u32[]{:S(2)}, u32[]{:S(2)}) collective-permute-start(bf16[96,3072]{1,0:T(8,128)(2,1)S(1)} %add_convert_fusion.6), channel_id=1, source_target_pairs={{0,2},{1,3},{2,0},{3,1},{4,6},{5,7},{6,4},{7,5},{8,10},{9,11},{10,... | collective-permute-start | bytes 1769480 | tf_op jit(solution)/shard_map/ppermute | solution.py:738
  182.6 22.3 %collective-permute-start.34 = (bf16[768,768]{1,0:T(8,128)(2,1)S(1)}, bf16[768,768]{1,0:T(8,128)(2,1)S(1)}, u32[]{:S(2)}, u32[]{:S(2)}) collective-permute-start(bf16[768,768]{1,0:T(8,128)(2,1)S(1)} %constant_dynamic-update-slice_fusion.9.refs_0_), channel_id=1, source_target_pairs={{0,16},{1,17},{2,18},{3,19},{4,20},{5,21},{6,22},{7,23},{8,24},{9,... | collective-permute-start | bytes 3538952 | tf_op jit(solution)/shard_map/ppermute | solution.py:738
  187.7 16.5 %collective-permute-start.31 = (bf16[96,1664]{1,0:T(8,128)(2,1)S(1)}, bf16[96,1664]{1,0:T(8,128)(2,1)S(1)}, u32[]{:S(2)}, u32[]{:S(2)}) collective-permute-start(bf16[96,1664]{1,0:T(8,128)(2,1)S(1)} %add_convert_fusion.20), channel_id=1, source_target_pairs={{0,4},{1,5},{2,6},{3,7},{4,0},{5,1},{6,2},{7,3},{8,12},{9,13},{10,... | collective-permute-start | bytes 958472 | tf_op jit(solution)/shard_map/ppermute | solution.py:738
  188.4 16.6 %collective-permute-start.35 = (bf16[768,768]{1,0:T(8,128)(2,1)S(1)}, bf16[768,768]{1,0:T(8,128)(2,1)S(1)}, u32[]{:S(2)}, u32[]{:S(2)}) collective-permute-start(bf16[768,768]{1,0:T(8,128)(2,1)S(1)} %collective-permute-done.27.refs_1_), channel_id=1, source_target_pairs={{0,16},{1,17},{2,18},{3,19},{4,20},{5,21},{6,22},{7,23},{8,24},{9,... | collective-permute-start | bytes 3538952 | tf_op jit(solution)/shard_map/ppermute | solution.py:738
  193.0 18.7 %collective-permute-start.36 = (bf16[192,3072]{1,0:T(8,128)(2,1)S(1)}, bf16[192,3072]{1,0:T(8,128)(2,1)S(1)}, u32[]{:S(2)}, u32[]{:S(2)}) collective-permute-start(bf16[192,3072]{1,0:T(8,128)(2,1)S(1)} %constant_dynamic-update-slice_fusion.11.refs_0_), channel_id=1, source_target_pairs={{0,1},{1,0},{2,3},{3,2},{4,5},{5,4},{6,7},{7,6},{8,9},{9,8},{10,11... | collective-permute-start | bytes 3538952 | tf_op jit(solution)/shard_map/ppermute | solution.py:738
  193.0 11.3 %collective-permute-start.32 = (bf16[96,1536]{1,0:T(8,128)(2,1)S(1)}, bf16[96,1536]{1,0:T(8,128)(2,1)S(1)}, u32[]{:S(2)}, u32[]{:S(2)}) collective-permute-start(bf16[96,1536]{1,0:T(8,128)(2,1)S(1)} %add_convert_fusion.24), channel_id=1, source_target_pairs={{0,8},{1,9},{2,10},{3,11},{4,12},{5,13},{6,14},{7,15},{8,0},{9,1},... | collective-permute-start | bytes 884744 | tf_op jit(solution)/shard_map/ppermute | solution.py:738
  204.3 10.4 %collective-permute-start.33 = (bf16[96,1664]{1,0:T(8,128)(2,1)S(1)}, bf16[96,1664]{1,0:T(8,128)(2,1)S(1)}, u32[]{:S(2)}, u32[]{:S(2)}) collective-permute-start(bf16[96,1664]{1,0:T(8,128)(2,1)S(1)} %add_convert_fusion.19), channel_id=1, source_target_pairs={{0,8},{1,9},{2,10},{3,11},{4,12},{5,13},{6,14},{7,15},{8,0},{9,1},... | collective-permute-start | bytes 958472 | tf_op jit(solution)/shard_map/ppermute | solution.py:738
  204.5 10.8 %collective-permute-start.37 = (bf16[96,1536]{1,0:T(8,128)(2,1)S(1)}, bf16[96,1536]{1,0:T(8,128)(2,1)S(1)}, u32[]{:S(2)}, u32[]{:S(2)}) collective-permute-start(bf16[96,1536]{1,0:T(8,128)(2,1)S(1)} %add_convert_fusion.23), channel_id=1, source_target_pairs={{0,2},{1,3},{2,0},{3,1},{4,6},{5,7},{6,4},{7,5},{8,10},{9,11},{10,... | collective-permute-start | bytes 884744 | tf_op jit(solution)/shard_map/ppermute | solution.py:738
  208.1 17.4 %collective-permute-start.39 = (bf16[192,3072]{1,0:T(8,128)(2,1)S(1)}, bf16[192,3072]{1,0:T(8,128)(2,1)S(1)}, u32[]{:S(2)}, u32[]{:S(2)}) collective-permute-start(bf16[192,3072]{1,0:T(8,128)(2,1)S(1)} %constant_dynamic-update-slice_fusion.11.refs_0_), channel_id=1, source_target_pairs={{0,16},{1,17},{2,18},{3,19},{4,20},{5,21},{6,22},{7,23},{8,24},{9,... | collective-permute-start | bytes 3538952 | tf_op jit(solution)/shard_map/ppermute | solution.py:738
  211.7 13.8 %collective-permute-start.40 = (bf16[192,3072]{1,0:T(8,128)(2,1)S(1)}, bf16[192,3072]{1,0:T(8,128)(2,1)S(1)}, u32[]{:S(2)}, u32[]{:S(2)}) collective-permute-start(bf16[192,3072]{1,0:T(8,128)(2,1)S(1)} %collective-permute-done.36.refs_1_), channel_id=1, source_target_pairs={{0,16},{1,17},{2,18},{3,19},{4,20},{5,21},{6,22},{7,23},{8,24},{9,... | collective-permute-start | bytes 3538952 | tf_op jit(solution)/shard_map/ppermute | solution.py:738
  214.7 10.5 %collective-permute-start.38 = (bf16[96,1664]{1,0:T(8,128)(2,1)S(1)}, bf16[96,1664]{1,0:T(8,128)(2,1)S(1)}, u32[]{:S(2)}, u32[]{:S(2)}) collective-permute-start(bf16[96,1664]{1,0:T(8,128)(2,1)S(1)} %add_convert_fusion.18), channel_id=1, source_target_pairs={{0,2},{1,3},{2,0},{3,1},{4,6},{5,7},{6,4},{7,5},{8,10},{9,11},{10,... | collective-permute-start | bytes 958472 | tf_op jit(solution)/shard_map/ppermute | solution.py:738
  215.3 10.3 %collective-permute-start.42 = (bf16[192,1536]{1,0:T(8,128)(2,1)S(1)}, bf16[192,1536]{1,0:T(8,128)(2,1)S(1)}, u32[]{:S(2)}, u32[]{:S(2)}) collective-permute-start(bf16[192,1536]{1,0:T(8,128)(2,1)S(1)} %constant_dynamic-update-slice_fusion.13.refs_0_), channel_id=1, source_target_pairs={{0,1},{1,0},{2,3},{3,2},{4,5},{5,4},{6,7},{7,6},{8,9},{9,8},{10,11... | collective-permute-start | bytes 1769480 | tf_op jit(solution)/shard_map/ppermute | solution.py:738
  225.3 10.5 %collective-permute-start.45 = (bf16[192,1664]{1,0:T(8,128)(2,1)S(1)}, bf16[192,1664]{1,0:T(8,128)(2,1)S(1)}, u32[]{:S(2)}, u32[]{:S(2)}) collective-permute-start(bf16[192,1664]{1,0:T(8,128)(2,1)S(1)} %constant_dynamic-update-slice_fusion.15.refs_0_), channel_id=1, source_target_pairs={{0,1},{1,0},{2,3},{3,2},{4,5},{5,4},{6,7},{7,6},{8,9},{9,8},{10,11... | collective-permute-start | bytes 1916936 | tf_op jit(solution)/shard_map/ppermute | solution.py:738
  225.5 12.7 %collective-permute-start.43 = (bf16[192,1536]{1,0:T(8,128)(2,1)S(1)}, bf16[192,1536]{1,0:T(8,128)(2,1)S(1)}, u32[]{:S(2)}, u32[]{:S(2)}) collective-permute-start(bf16[192,1536]{1,0:T(8,128)(2,1)S(1)} %collective-permute-done.42.refs_1_), channel_id=1, source_target_pairs={{0,16},{1,17},{2,18},{3,19},{4,20},{5,21},{6,22},{7,23},{8,24},{9,... | collective-permute-start | bytes 1769480 | tf_op jit(solution)/shard_map/ppermute | solution.py:738
  228.7 9.6 %collective-permute-start.41 = (bf16[192,1536]{1,0:T(8,128)(2,1)S(1)}, bf16[192,1536]{1,0:T(8,128)(2,1)S(1)}, u32[]{:S(2)}, u32[]{:S(2)}) collective-permute-start(bf16[192,1536]{1,0:T(8,128)(2,1)S(1)} %constant_dynamic-update-slice_fusion.13.refs_0_), channel_id=1, source_target_pairs={{0,16},{1,17},{2,18},{3,19},{4,20},{5,21},{6,22},{7,23},{8,24},{9,... | collective-permute-start | bytes 1769480 | tf_op jit(solution)/shard_map/ppermute | solution.py:738
  235.8 8.7 %collective-permute-start.46 = (bf16[192,1664]{1,0:T(8,128)(2,1)S(1)}, bf16[192,1664]{1,0:T(8,128)(2,1)S(1)}, u32[]{:S(2)}, u32[]{:S(2)}) collective-permute-start(bf16[192,1664]{1,0:T(8,128)(2,1)S(1)} %collective-permute-done.45.refs_1_), channel_id=1, source_target_pairs={{0,16},{1,17},{2,18},{3,19},{4,20},{5,21},{6,22},{7,23},{8,24},{9,... | collective-permute-start | bytes 1916936 | tf_op jit(solution)/shard_map/ppermute | solution.py:738
  240.8 3.7 %collective-permute-start.44 = (bf16[192,1664]{1,0:T(8,128)(2,1)S(1)}, bf16[192,1664]{1,0:T(8,128)(2,1)S(1)}, u32[]{:S(2)}, u32[]{:S(2)}) collective-permute-start(bf16[192,1664]{1,0:T(8,128)(2,1)S(1)} %constant_dynamic-update-slice_fusion.15.refs_0_), channel_id=1, source_target_pairs={{0,16},{1,17},{2,18},{3,19},{4,20},{5,21},{6,22},{7,23},{8,24},{9,... | collective-permute-start | bytes 1916936 | tf_op jit(solution)/shard_map/ppermute | solution.py:738
  (4 other events, 7.9 us)

commit v4 on v3

--- a/solution.py
+++ b/solution.py
@@ -889,10 +889,10 @@
     down_own = down.send(sent)
     sent = down_own
     sent = value.send(sent)
+    sent = query.send(sent)
+    sent = up.send(sent)
     down_out = spread(place, 0, tie(down_own, sent), [D], [], None, "down")
     sent = down_out
-    sent = query.send(sent)
-    sent = up.send(sent)
     sent = query.send(sent)
     sent = value.send(sent)
     sent = query.send(sent)

time: 248 us -> 246 us (level)
  waiting for transfers between devices: 63.4 us -> 60.7 us
    ppermute x47, waiting for transfers between devices: 63.4 us -> 60.7 us  [swap(): return lax.ppermute(piece, ('stream', 'dp'), pairs)]
  transfers between devices with their start and end apart: 47 -> 47, of which waited for: 14 -> 15; matrix products, arithmetic and copies ran while one was open for 4% -> 4% of each run, Pallas kernels for 43% -> 44%
where the time goes in v4:
time: 246 us
  Pallas kernels  138 us (56%)
  waiting for transfers between devices  60.7 us (25%)
  starting transfers between devices  33.7 us (14%)
  other arithmetic  8.57 us (3%)
  local copies, waits for them, and re-layouts  2.74 us (1%)
    ppermute x47, waiting for transfers between devices, swap(): return lax.ppermute(piece, ('stream', 'dp'), pairs)  60.7 us
    ppermute x47, starting transfers between devices, swap(): return lax.ppermute(piece, ('stream', 'dp'), pairs)  33.7 us
    pallas_call x2, Pallas kernels, ff_forward(): pl.pallas_call(functools.partial(ff_kernel, part, seq_len), grid=(hidden...  30.5 us
    pallas_call x8, Pallas kernels, spread(): pl.pallas_call(functools.partial(spread_kernel, widths, talls, first), gr...  22.7 us
    pallas_call x1, Pallas kernels, hidden_gradient(): pl.pallas_call(hidden_kernel, grid_spec=pltpu.PrefetchScalarGridSpec(num_...  14.9 us
    pallas_call x1, Pallas kernels, attention_forward(): pl.pallas_call(functools.partial(attention_kernel, seq_len), grid=(steps,...  14.1 us
    pallas_call x2, Pallas kernels, down_gradient(): pl.pallas_call(functools.partial(down_grad_kernel, seq_len, fresh), grid_...  12.5 us
    pallas_call x1, Pallas kernels, norm_one_backward(): pl.pallas_call(norm_one_kernel, grid=(hidden // D,), in_specs=[pl.BlockSp...  11 us
  transfers between devices with their start and end apart: 47, of which 15 were waited for; matrix products, arithmetic and copies ran while one was open for 4% of the time, Pallas kernels for 44%

profile of v4, /device:TPU:0, one launch (start us, length us, event | category | flops | bytes accessed | tf_op | source)
XLA Modules:
  0.0 245.6 jit_solution(18160675122406613293)
XLA Ops:
  1.3 14.1 %attention_forward.1 = (bf16[1024,768]{1,0:T(8,128)(2,1)}, bf16[1024,768]{1,0:T(8,128)(2,1)}, bf16[1024,768]{1,0:T(8,128)(2,1)}, bf16[1024,768]{1,0:T(8,128)(2,1...) custom-call(bf16[1024,768]{1,0:T(8,128)(2,1)} %bitcast.36, ...), custom_call_target="tpu_custom_call" | custom-call | flops 230000000 | bytes 1000 | tf_op jit(solution)/shard_map/attention_forward/pallas_call | solution.py:164
  15.5 5.7 %lead_forward.1 = (f32[16,768]{1,0:T(8,128)S(1)}, f32[16,768]{1,0:T(8,128)S(1)}, f32[16,128]{1,0:T(8,128)S(1)}, f32[16,128]{1,0:T(8,128)S(1)}, bf16[16,768]{1,0:T(8,128)(2,1)S(1)}) custom-call(f32[4,4,768]{2,1,0:T(4,128)S(1)} %get-tuple-element.149.nl_ref, f32[4,4,768]{2,1,0:T(4,128)S(1)} %get-tuple-element.150.hat_ref, bf16[768,3072]{1,0:T(8,128)(2,1)} %uw.7, ...), custom_call_target="tpu_custom_call" | custom-call | flops 69000000 | bytes 1000 | tf_op jit(solution)/shard_map/lead_forward/pallas_call | solution.py:207
  21.3 2.9 %collective-permute-start = (bf16[16,896]{1,0:T(8,128)(2,1)S(1)}, bf16[16,896]{1,0:T(8,128)(2,1)S(1)}, u32[]{:S(2)}, u32[]{:S(2)}) collective-permute-start(bf16[16,896]{1,0:T(8,128)(2,1)S(1)} %pad_maximum_fusion), channel_id=1, source_target_pairs={{0,1},{1,0},{2,3},{3,2},{4,5},{5,4},{6,7},{7,6},{8,9},{9,8},{10,11... | collective-permute-start | bytes 86024 | tf_op jit(solution)/shard_map/ppermute | solution.py:738
  24.2 1.5 collective-permute-start.1
  25.7 15.3 %ff_forward_0.1 = (bf16[1024,768]{1,0:T(8,128)(2,1)}, bf16[1024,3072]{1,0:T(8,128)(2,1)}, bf16[1024,3072]{1,0:T(8,128)(2,1)}, bf16[1024,768]{1,0:T(8,128)(2,1)},...) custom-call(bf16[1024,768]{1,0:T(8,128)(2,1)} %get-tuple-element.156.nl_ref, bf16[768,3072]{1,0:T(8,128)(2,1)} %uw.7, ...), custom_call_target="tpu_custom_call" | custom-call | flops 299000000 | bytes 1000 | tf_op jit(solution)/shard_map/ff_forward_0/pallas_call | solution.py:281
  41.1 2.1 collective-permute-start.3
  43.2 2.6 %collective-permute-start.4 = (bf16[64,896]{1,0:T(8,128)(2,1)S(1)}, bf16[64,896]{1,0:T(8,128)(2,1)S(1)}, u32[]{:S(2)}, u32[]{:S(2)}) collective-permute-start(bf16[64,896]{1,0:T(8,128)(2,1)S(1)} %constant_dynamic-update-slice_fusion), channel_id=1, source_target_pairs={{0,8},{1,9},{2,10},{3,11},{4,12},{5,13},{6,14},{7,15},{8,0},{9,1},... | collective-permute-start | bytes 344072 | tf_op jit(solution)/shard_map/ppermute | solution.py:738
  45.8 15.2 %ff_forward_1.1 = (bf16[1024,768]{1,0:T(8,128)(2,1)}, bf16[1024,3072]{1,0:T(8,128)(2,1)}, bf16[1024,3072]{1,0:T(8,128)(2,1)}, bf16[1024,768]{1,0:T(8,128)(2,1)},...) custom-call(bf16[1024,768]{1,0:T(8,128)(2,1)} %get-tuple-element.156, ...), custom_call_target="tpu_custom_call", output_to_operand_aliasing={{0}: (11, {}), {1}: (12, {}), {2}: (13, {}), {3}: (14, {}),... | custom-call | flops 299000000 | bytes 1000 | tf_op jit(solution)/shard_map/ff_forward_1/pallas_call | solution.py:281
  61.3 1.7 collective-permute-done.6.other_ref
  63.0 1.8 pair_loss.1
  64.8 6.9 %down_grad_4.1 = (bf16[768,768]{1,0:T(8,128)(2,1)}, bf16[768,768]{1,0:T(8,128)(2,1)S(1)}, bf16[1024,768]{1,0:T(8,128)(2,1)S(1)}, f32[1,768]{1,0:T(1,128)S(1)}) custom-call(s32[8]{0:T(128)S(1)} %stack.35.place, bf16[1024,768]{1,0:T(8,128)(2,1)S(1)} %copy-done, f32[16,768]{1,0:T(8,128)S(1)} %bitcast.34, f32[16,768]{1,0:T(8,128)S(1)} %get-tuple-element.175.refs_2_, ...), custom_call_target="tpu_custom_call" | custom-call | flops 92000000 | bytes 1000 | tf_op jit(solution)/shard_map/down_grad_4/pallas_call | solution.py:413
  72.2 5.6 %down_grad_0.1 = (bf16[768,768]{1,0:T(8,128)(2,1)S(1)}, bf16[768,768]{1,0:T(8,128)(2,1)S(1)}) custom-call(s32[8]{0:T(128)S(1)} %stack.35.place, bf16[1024,768]{1,0:T(8,128)(2,1)S(1)} %get-tuple-element.183.refs_0_.db_ref.branch_far, bf16[1024,3072]{1,0:T(8,128)(2,1)} %get-tuple-element.176.refs_3_.refs_1_), custom_call_target="tpu_custom_call" | custom-call | flops 92000000 | bytes 1000 | tf_op jit(solution)/shard_map/down_grad_0/pallas_call | solution.py:413
  77.8 1.3 add_convert_fusion.3
  79.1 1.7 collective-permute-start.9
  80.9 1.6 add_convert_fusion.2
  82.4 14.9 %hidden_gradient.1 = (bf16[1024,3072]{1,0:T(8,128)(2,1)}, f32[8,3072]{1,0:T(8,128)S(1)}, bf16[192,3072]{1,0:T(8,128)(2,1)S(1)}, bf16[192,3072]{1,0:T(8,128)(2,1)...) custom-call(s32[8]{0:T(128)S(1)} %stack.35.place, ...), custom_call_target="tpu_custom_call", output_to_operand_aliasing={{0}: (2, {})} | custom-call | flops 345000000 | bytes 1000 | tf_op jit(solution)/shard_map/hidden_gradient/pallas_call | solution.py:445
  97.9 1.6 add_convert_fusion.16
  99.4 1.6 collective-permute-start.10
  101.0 11.0 %norm_one_backward.1 = (bf16[4,1024,768]{2,1,0:T(8,128)(2,1)S(1)}, bf16[1024,768]{1,0:T(8,128)(2,1)S(1)}, f32[8,768]{1,0:T(8,128)S(1)}) custom-call(bf16[1024,3072]{1,0:T(8,128)(2,1)} %get-tuple-element.189.dpre_ref, bf16[768,3072]{1,0:T(8,128)(2,1)} %uw.7, f32[6,128]{1,0:T(8,128)} %bitcast.50, bf16[768,768]{1,0:T(8,128)(2,1)} %wo_far.1, ...), custom_call_target="tpu_custom_call" | custom-call | flops 299000000 | bytes 1000 | tf_op jit(solution)/shard_map/norm_one_backward/pallas_call | solution.py:501
  116.0 7.0 %attention_backward.1 = (bf16[4,1024,768]{2,1,0:T(8,128)(2,1)S(1)}, f32[8,768]{1,0:T(8,128)S(1)}) custom-call(bf16[1024,768]{1,0:T(8,128)(2,1)S(1)} %copy-done.1, bf16[1024,768]{1,0:T(8,128)(2,1)S(1)} %copy-done.2, bf16[1024,768]{1,0:T(8,128)(2,1)S(1)} %copy-done.3, bf16[1024,768]{1,0:T(8,128)(2,1)S(1)} %copy-done.4, ...), custom_call_target="tpu_custom_call", output_to_operand_aliasing={{0}: (5, {})} | custom-call | flops 184000000 | bytes 1000 | tf_op jit(solution)/shard_map/attention_backward/pallas_call | solution.py:559
  123.1 5.3 %value_gradient.1 = (bf16[192,1536]{1,0:T(8,128)(2,1)S(1)}, bf16[192,1536]{1,0:T(8,128)(2,1)S(1)}, bf16[192,1536]{1,0:T(8,128)(2,1)S(1)}, bf16[192,1536]{1,0:T(8,128)(2,1)S(1)}) custom-call(s32[8]{0:T(128)S(1)} %stack.35.place, bf16[1024,768]{1,0:T(8,128)(2,1)} %get-tuple-element.200.left_ref, bf16[4,1024,768]{2,1,0:T(8,128)(2,1)S(1)} %get-tuple-element.227.d_ref, ...), custom_call_target="tpu_custom_call" | custom-call | flops 138000000 | bytes 1000 | tf_op jit(solution)/shard_map/value_gradient/pallas_call | solution.py:612
  129.1 3.5 %collective-permute-start.18 = (bf16[384,768]{1,0:T(8,128)(2,1)S(1)}, bf16[384,768]{1,0:T(8,128)(2,1)S(1)}, u32[]{:S(2)}, u32[]{:S(2)}) collective-permute-start(bf16[384,768]{1,0:T(8,128)(2,1)S(1)} %add_convert_fusion.14), channel_id=1, source_target_pairs={{0,8},{1,9},{2,10},{3,11},{4,12},{5,13},{6,14},{7,15},{8,0},{9,1},... | collective-permute-start | bytes 1769480 | tf_op jit(solution)/shard_map/ppermute | solution.py:738
  133.6 5.1 %query_gradient.1 = (bf16[192,1664]{1,0:T(8,128)(2,1)S(1)}, bf16[192,1664]{1,0:T(8,128)(2,1)S(1)}, bf16[192,1664]{1,0:T(8,128)(2,1)S(1)}, bf16[192,1664]{1,0:T(8,128)(2,1)S(1)}) custom-call(s32[8]{0:T(128)S(1)} %stack.35.place, bf16[1024,768]{1,0:T(8,128)(2,1)} %bitcast.38, bf16[4,1024,768]{2,1,0:T(8,128)(2,1)S(1)} %get-tuple-element.227.d_ref, ...), custom_call_target="tpu_custom_call" | custom-call | flops 138000000 | bytes 1000 | tf_op jit(solution)/shard_map/query_gradient/pallas_call | solution.py:612
  141.0 2.8 %collective-permute-done.17 = bf16[96,3072]{1,0:T(8,128)(2,1)S(1)} collective-permute-done((bf16[96,3072]{1,0:T(8,128)(2,1)S(1)}, bf16[96,3072]{1,0:T(8,128)(2,1)S(1)}, u32[]{:S(2)}, u32[]{:S(2)}) %collective-permute-start.17) | collective-permute-done | bytes 589856 | tf_op jit(solution)/shard_map/ppermute | solution.py:738
  144.0 2.5 %collective-permute-done.18 = bf16[384,768]{1,0:T(8,128)(2,1)S(1)} collective-permute-done((bf16[384,768]{1,0:T(8,128)(2,1)S(1)}, bf16[384,768]{1,0:T(8,128)(2,1)S(1)}, u32[]{:S(2)}, u32[]{:S(2)}) %collective-permute-start.18) | collective-permute-done | bytes 589856 | tf_op jit(solution)/shard_map/ppermute | solution.py:738
  148.5 1.2 collective-permute-done.21
  149.8 1.8 collective-permute-start.24
  151.6 8.1 %collective-permute-done.22 = bf16[96,3072]{1,0:T(8,128)(2,1)S(1)} collective-permute-done((bf16[96,3072]{1,0:T(8,128)(2,1)S(1)}, bf16[96,3072]{1,0:T(8,128)(2,1)S(1)}, u32[]{:S(2)}, u32[]{:S(2)}) %collective-permute-start.22) | collective-permute-done | bytes 589856 | tf_op jit(solution)/shard_map/ppermute | solution.py:738
  160.9 1.6 collective-permute-done.23
  163.4 7.7 %input_gradient.1 = f32[1024,768]{1,0:T(8,128)} custom-call(bf16[4,1024,768]{2,1,0:T(8,128)(2,1)S(1)} %get-tuple-element.227.d_ref, bf16[768,768]{1,0:T(8,128)(2,1)} %wq.3, bf16[768,768]{1,0:T(8,128)(2,1)} %wk.3, bf16[768,768]{1,0:T(8,128)(2,1)} %wv.3), custom_call_target="tpu_custom_call" | custom-call | flops 138000000 | bytes 1000 | tf_op jit(solution)/shard_map/input_gradient/pallas_call | solution.py:642
  171.7 1.5 collective-permute-start.29
  173.2 9.2 %collective-permute-done.26 = bf16[96,3072]{1,0:T(8,128)(2,1)S(1)} collective-permute-done((bf16[96,3072]{1,0:T(8,128)(2,1)S(1)}, bf16[96,3072]{1,0:T(8,128)(2,1)S(1)}, u32[]{:S(2)}, u32[]{:S(2)}) %collective-permute-start.26) | collective-permute-done | bytes 589856 | tf_op jit(solution)/shard_map/ppermute | solution.py:738
  182.7 1.6 collective-permute-done.27.refs_1_
  185.3 8.3 %collective-permute-done.30 = bf16[96,3072]{1,0:T(8,128)(2,1)S(1)} collective-permute-done((bf16[96,3072]{1,0:T(8,128)(2,1)S(1)}, bf16[96,3072]{1,0:T(8,128)(2,1)S(1)}, u32[]{:S(2)}, u32[]{:S(2)}) %collective-permute-start.30) | collective-permute-done | bytes 589856 | tf_op jit(solution)/shard_map/ppermute | solution.py:738
  193.8 3.2 %down_spread_0.1.refs_2_ = f32[3072,768]{1,0:T(8,128)} custom-call(s32[8]{0:T(128)S(1)} %stack.35.place, bf16[768,768]{1,0:T(8,128)(2,1)S(1)} %constant_dynamic-update-slice_fusion.9.refs_0_, bf16[768,768]{1,0:T(8,128)(2,1)S(1)} %collective-permute-done.27.refs_1_), custom_call_target="tpu_custom_call" | custom-call | flops 69000000 | bytes 1000 | tf_op jit(solution)/shard_map/down_spread_0/pallas_call | solution.py:694
  197.2 2.9 %collective-permute-start.33 = (bf16[96,1664]{1,0:T(8,128)(2,1)S(1)}, bf16[96,1664]{1,0:T(8,128)(2,1)S(1)}, u32[]{:S(2)}, u32[]{:S(2)}) collective-permute-start(bf16[96,1664]{1,0:T(8,128)(2,1)S(1)} %add_convert_fusion.19), channel_id=1, source_target_pairs={{0,8},{1,9},{2,10},{3,11},{4,12},{5,13},{6,14},{7,15},{8,0},{9,1},... | collective-permute-start | bytes 958472 | tf_op jit(solution)/shard_map/ppermute | solution.py:738
  200.0 4.5 %collective-permute-done.32 = bf16[96,1536]{1,0:T(8,128)(2,1)S(1)} collective-permute-done((bf16[96,1536]{1,0:T(8,128)(2,1)S(1)}, bf16[96,1536]{1,0:T(8,128)(2,1)S(1)}, u32[]{:S(2)}, u32[]{:S(2)}) %collective-permute-start.32) | collective-permute-done | bytes 294944 | tf_op jit(solution)/shard_map/ppermute | solution.py:738
  204.7 3.2 %down_spread_4.1 = f32[3072,768]{1,0:T(8,128)} custom-call(s32[8]{0:T(128)S(1)} %stack.35.place, bf16[768,768]{1,0:T(8,128)(2,1)S(1)} %collective-permute-done.34.refs_0_, bf16[768,768]{1,0:T(8,128)(2,1)S(1)} %collective-permute-done.35.refs_1_, f32[3072,768]{1,0:T(8,128)} %down_spread_0.1.refs_2_), custom_call_target="tpu_custom_call", output_to_operand_aliasing={{}: (3, {})} | custom-call | flops 69000000 | bytes 1000 | tf_op jit(solution)/shard_map/down_spread_4/pallas_call | solution.py:694
  207.9 5.2 %collective-permute-done.36.refs_1_ = bf16[192,3072]{1,0:T(8,128)(2,1)S(1)} collective-permute-done((bf16[192,3072]{1,0:T(8,128)(2,1)S(1)}, bf16[192,3072]{1,0:T(8,128)(2,1)S(1)}, u32[]{:S(2)}, u32[]{:S(2)}) %collective-permute-start.36) | collective-permute-done | bytes 1179680 | tf_op jit(solution)/shard_map/ppermute | solution.py:738
  213.4 3.2 %up_spread_0.1.refs_2_ = f32[768,3072]{1,0:T(8,128)} custom-call(s32[8]{0:T(128)S(1)} %stack.35.place, bf16[192,3072]{1,0:T(8,128)(2,1)S(1)} %constant_dynamic-update-slice_fusion.11.refs_0_, bf16[192,3072]{1,0:T(8,128)(2,1)S(1)} %collective-permute-done.36.refs_1_), custom_call_target="tpu_custom_call" | custom-call | flops 69000000 | bytes 1000 | tf_op jit(solution)/shard_map/up_spread_0/pallas_call | solution.py:694
  216.6 7.1 %collective-permute-done.38 = bf16[96,1664]{1,0:T(8,128)(2,1)S(1)} collective-permute-done((bf16[96,1664]{1,0:T(8,128)(2,1)S(1)}, bf16[96,1664]{1,0:T(8,128)(2,1)S(1)}, u32[]{:S(2)}, u32[]{:S(2)}) %collective-permute-start.38) | collective-permute-done | bytes 319520 | tf_op jit(solution)/shard_map/ppermute | solution.py:738
  223.7 2.3 collective-permute-done.42.refs_1_
  226.2 3.2 %up_spread_4.1 = f32[768,3072]{1,0:T(8,128)} custom-call(s32[8]{0:T(128)S(1)} %stack.35.place, bf16[192,3072]{1,0:T(8,128)(2,1)S(1)} %collective-permute-done.39.refs_0_, bf16[192,3072]{1,0:T(8,128)(2,1)S(1)} %collective-permute-done.40.refs_1_, f32[768,3072]{1,0:T(8,128)} %up_spread_0.1.refs_2_), custom_call_target="tpu_custom_call", output_to_operand_aliasing={{}: (3, {})} | custom-call | flops 69000000 | bytes 1000 | tf_op jit(solution)/shard_map/up_spread_4/pallas_call | solution.py:694
  229.7 4.4 %collective-permute-done.45.refs_1_ = bf16[192,1664]{1,0:T(8,128)(2,1)S(1)} collective-permute-done((bf16[192,1664]{1,0:T(8,128)(2,1)S(1)}, bf16[192,1664]{1,0:T(8,128)(2,1)S(1)}, u32[]{:S(2)}, u32[]{:S(2)}) %collective-permute-start.45) | collective-permute-done | bytes 639008 | tf_op jit(solution)/shard_map/ppermute | solution.py:738
  234.1 2.5 %value_spread_0.1 = (f32[768,768]{1,0:T(8,128)}, f32[768,768]{1,0:T(8,128)}) custom-call(s32[8]{0:T(128)S(1)} %stack.35.place, bf16[192,1536]{1,0:T(8,128)(2,1)S(1)} %constant_dynamic-update-slice_fusion.13.refs_0_, bf16[192,1536]{1,0:T(8,128)(2,1)S(1)} %collective-permute-done.42.refs_1_), custom_call_target="tpu_custom_call" | custom-call | flops 69000000 | bytes 1000 | tf_op jit(solution)/shard_map/value_spread_0/pallas_call | solution.py:694
  236.7 2.5 %value_spread_4.1 = (f32[768,768]{1,0:T(8,128)}, f32[768,768]{1,0:T(8,128)}) custom-call(s32[8]{0:T(128)S(1)} %stack.35.place, bf16[192,1536]{1,0:T(8,128)(2,1)S(1)} %collective-permute-done.41.refs_0_, bf16[192,1536]{1,0:T(8,128)(2,1)S(1)} %collective-permute-done.43.refs_1_, ...), custom_call_target="tpu_custom_call", output_to_operand_aliasing={{0}: (3, {}), {1}: (4, {})} | custom-call | flops 69000000 | bytes 1000 | tf_op jit(solution)/shard_map/value_spread_4/pallas_call | solution.py:694
  240.3 2.5 %query_spread_0.1 = (f32[768,768]{1,0:T(8,128)}, f32[768,768]{1,0:T(8,128)}, f32[24,128]{1,0:T(8,128)S(1)}, f32[6,128]{1,0:T(8,128)S(1)}, f32[6,128]{1,0:T(8,128...) custom-call(s32[8]{0:T(128)S(1)} %stack.35.place, ...), custom_call_target="tpu_custom_call" | custom-call | flops 69000000 | bytes 1000 | tf_op jit(solution)/shard_map/query_spread_0/pallas_call | solution.py:694
  242.8 2.6 %query_spread_4.1 = (f32[768,768]{1,0:T(8,128)}, f32[768,768]{1,0:T(8,128)}, f32[24,128]{1,0:T(8,128)}, f32[6,128]{1,0:T(8,128)}, f32[6,128]{1,0:T(8,128)}, /*in...) custom-call(s32[8]{0:T(128)S(1)} %stack.35.place, ...), custom_call_target="tpu_custom_call", output_to_operand_aliasing={{0}: (12, {}), {1}: (13, {})} | custom-call | flops 69000000 | bytes 1000 | tf_op jit(solution)/shard_map/query_spread_4/pallas_call | solution.py:694
  (136 shorter events, 18.7 us)
Async XLA Ops:
  21.3 19.8 %collective-permute-start = (bf16[16,896]{1,0:T(8,128)(2,1)S(1)}, bf16[16,896]{1,0:T(8,128)(2,1)S(1)}, u32[]{:S(2)}, u32[]{:S(2)}) collective-permute-start(bf16[16,896]{1,0:T(8,128)(2,1)S(1)} %pad_maximum_fusion), channel_id=1, source_target_pairs={{0,1},{1,0},{2,3},{3,2},{4,5},{5,4},{6,7},{7,6},{8,9},{9,8},{10,11... | collective-permute-start | bytes 86024 | tf_op jit(solution)/shard_map/ppermute | solution.py:738
  24.2 16.8 %collective-permute-start.1 = (bf16[16,896]{1,0:T(8,128)(2,1)S(1)}, bf16[16,896]{1,0:T(8,128)(2,1)S(1)}, u32[]{:S(2)}, u32[]{:S(2)}) collective-permute-start(bf16[16,896]{1,0:T(8,128)(2,1)S(1)} %pad_maximum_fusion), channel_id=1, source_target_pairs={{0,2},{1,3},{2,0},{3,1},{4,6},{5,7},{6,4},{7,5},{8,10},{9,11},{10,... | collective-permute-start | bytes 86024 | tf_op jit(solution)/shard_map/ppermute | solution.py:738
  25.7 15.3 %collective-permute-start.2 = (bf16[16,896]{1,0:T(8,128)(2,1)S(1)}, bf16[16,896]{1,0:T(8,128)(2,1)S(1)}, u32[]{:S(2)}, u32[]{:S(2)}) collective-permute-start(bf16[16,896]{1,0:T(8,128)(2,1)S(1)} %pad_maximum_fusion), channel_id=1, source_target_pairs={{0,3},{1,2},{2,1},{3,0},{4,7},{5,6},{6,5},{7,4},{8,11},{9,10},{10,... | collective-permute-start | bytes 86024 | tf_op jit(solution)/shard_map/ppermute | solution.py:738
  41.1 19.9 %collective-permute-start.3 = (bf16[64,896]{1,0:T(8,128)(2,1)S(1)}, bf16[64,896]{1,0:T(8,128)(2,1)S(1)}, u32[]{:S(2)}, u32[]{:S(2)}) collective-permute-start(bf16[64,896]{1,0:T(8,128)(2,1)S(1)} %constant_dynamic-update-slice_fusion), channel_id=1, source_target_pairs={{0,4},{1,5},{2,6},{3,7},{4,0},{5,1},{6,2},{7,3},{8,12},{9,13},{10,... | collective-permute-start | bytes 344072 | tf_op jit(solution)/shard_map/ppermute | solution.py:738
  43.2 17.9 %collective-permute-start.4 = (bf16[64,896]{1,0:T(8,128)(2,1)S(1)}, bf16[64,896]{1,0:T(8,128)(2,1)S(1)}, u32[]{:S(2)}, u32[]{:S(2)}) collective-permute-start(bf16[64,896]{1,0:T(8,128)(2,1)S(1)} %constant_dynamic-update-slice_fusion), channel_id=1, source_target_pairs={{0,8},{1,9},{2,10},{3,11},{4,12},{5,13},{6,14},{7,15},{8,0},{9,1},... | collective-permute-start | bytes 344072 | tf_op jit(solution)/shard_map/ppermute | solution.py:738
  45.8 15.3 %collective-permute-start.5 = (bf16[64,896]{1,0:T(8,128)(2,1)S(1)}, bf16[64,896]{1,0:T(8,128)(2,1)S(1)}, u32[]{:S(2)}, u32[]{:S(2)}) collective-permute-start(bf16[64,896]{1,0:T(8,128)(2,1)S(1)} %constant_dynamic-update-slice_fusion), channel_id=1, source_target_pairs={{0,12},{1,13},{2,14},{3,15},{4,8},{5,9},{6,10},{7,11},{8,4},{9,5},... | collective-permute-start | bytes 344072 | tf_op jit(solution)/shard_map/ppermute | solution.py:738
  61.0 3.8 %copy-start = (bf16[1024,768]{1,0:T(8,128)(2,1)S(1)}, bf16[1024,768]{1,0:T(8,128)(2,1)}, u32[]{:S(2)}) copy-start(bf16[1024,768]{1,0:T(8,128)(2,1)} %get-tuple-element.167.refs_0_) | copy-start | bytes 4718596
  61.1 1.9 collective-permute-start.6
  71.7 6.1 %collective-permute-start.7 = (bf16[768,768]{1,0:T(8,128)(2,1)S(1)}, bf16[768,768]{1,0:T(8,128)(2,1)S(1)}, u32[]{:S(2)}, u32[]{:S(2)}) collective-permute-start(bf16[768,768]{1,0:T(8,128)(2,1)S(1)} %get-tuple-element.179), channel_id=1, source_target_pairs={{0,16},{1,17},{2,18},{3,19},{4,20},{5,21},{6,22},{7,23},{8,24},{9,... | collective-permute-start | bytes 3538952 | tf_op jit(solution)/shard_map/ppermute | solution.py:738
  71.8 9.0 %collective-permute-start.8 = (bf16[768,768]{1,0:T(8,128)(2,1)}, bf16[768,768]{1,0:T(8,128)(2,1)}, u32[]{:S(2)}, u32[]{:S(2)}) collective-permute-start(bf16[768,768]{1,0:T(8,128)(2,1)} %get-tuple-element.178), channel_id=1, source_target_pairs={{0,16},{1,17},{2,18},{3,19},{4,20},{5,21},{6,22},{7,23},{8,24},{9,... | collective-permute-start | bytes 3538952 | tf_op jit(solution)/shard_map/ppermute | solution.py:738
  79.1 18.8 %collective-permute-start.9 = (bf16[768,768]{1,0:T(8,128)(2,1)}, bf16[768,768]{1,0:T(8,128)(2,1)}, u32[]{:S(2)}, u32[]{:S(2)}) collective-permute-start(bf16[768,768]{1,0:T(8,128)(2,1)} %add_convert_fusion.3), channel_id=1, source_target_pairs={{0,1},{1,0},{2,3},{3,2},{4,5},{5,4},{6,7},{7,6},{8,9},{9,8},{10,11... | collective-permute-start | bytes 3538952 | tf_op jit(solution)/shard_map/ppermute | solution.py:738
  97.3 16.8 %collective-permute-start.12 = (bf16[192,3072]{1,0:T(8,128)(2,1)S(1)}, bf16[192,3072]{1,0:T(8,128)(2,1)S(1)}, u32[]{:S(2)}, u32[]{:S(2)}) collective-permute-start(bf16[192,3072]{1,0:T(8,128)(2,1)S(1)} %get-tuple-element.187), channel_id=1, source_target_pairs={{0,16},{1,17},{2,18},{3,19},{4,20},{5,21},{6,22},{7,23},{8,24},{9,... | collective-permute-start | bytes 3538952 | tf_op jit(solution)/shard_map/ppermute | solution.py:738
  97.4 15.7 %collective-permute-start.11 = (bf16[192,3072]{1,0:T(8,128)(2,1)S(1)}, bf16[192,3072]{1,0:T(8,128)(2,1)S(1)}, u32[]{:S(2)}, u32[]{:S(2)}) collective-permute-start(bf16[192,3072]{1,0:T(8,128)(2,1)S(1)} %get-tuple-element.188), channel_id=1, source_target_pairs={{0,16},{1,17},{2,18},{3,19},{4,20},{5,21},{6,22},{7,23},{8,24},{9,... | collective-permute-start | bytes 3538952 | tf_op jit(solution)/shard_map/ppermute | solution.py:738
  99.4 12.7 %collective-permute-start.10 = (bf16[384,768]{1,0:T(8,128)(2,1)S(1)}, bf16[384,768]{1,0:T(8,128)(2,1)S(1)}, u32[]{:S(2)}, u32[]{:S(2)}) collective-permute-start(bf16[384,768]{1,0:T(8,128)(2,1)S(1)} %get-tuple-element.289), channel_id=1, source_target_pairs={{0,2},{1,3},{2,0},{3,1},{4,6},{5,7},{6,4},{7,5},{8,10},{9,11},{10,... | collective-permute-start | bytes 1769480 | tf_op jit(solution)/shard_map/ppermute | solution.py:738
  112.3 16.7 %collective-permute-start.13 = (bf16[384,768]{1,0:T(8,128)(2,1)S(1)}, bf16[384,768]{1,0:T(8,128)(2,1)S(1)}, u32[]{:S(2)}, u32[]{:S(2)}) collective-permute-start(bf16[384,768]{1,0:T(8,128)(2,1)S(1)} %add_convert_fusion.15), channel_id=1, source_target_pairs={{0,4},{1,5},{2,6},{3,7},{4,0},{5,1},{6,2},{7,3},{8,12},{9,13},{10,... | collective-permute-start | bytes 1769480 | tf_op jit(solution)/shard_map/ppermute | solution.py:738
  113.5 19.2 %collective-permute-start.14 = (bf16[192,3072]{1,0:T(8,128)(2,1)S(1)}, bf16[192,3072]{1,0:T(8,128)(2,1)S(1)}, u32[]{:S(2)}, u32[]{:S(2)}) collective-permute-start(bf16[192,3072]{1,0:T(8,128)(2,1)S(1)} %add_convert_fusion.1), channel_id=1, source_target_pairs={{0,1},{1,0},{2,3},{3,2},{4,5},{5,4},{6,7},{7,6},{8,9},{9,8},{10,11... | collective-permute-start | bytes 3538952 | tf_op jit(solution)/shard_map/ppermute | solution.py:738
  128.3 11.6 %collective-permute-start.16 = (bf16[192,1536]{1,0:T(8,128)(2,1)S(1)}, bf16[192,1536]{1,0:T(8,128)(2,1)S(1)}, u32[]{:S(2)}, u32[]{:S(2)}) collective-permute-start(bf16[192,1536]{1,0:T(8,128)(2,1)S(1)} %get-tuple-element.202), channel_id=1, source_target_pairs={{0,16},{1,17},{2,18},{3,19},{4,20},{5,21},{6,22},{7,23},{8,24},{9,... | collective-permute-start | bytes 1769480 | tf_op jit(solution)/shard_map/ppermute | solution.py:738
  128.7 10.1 %collective-permute-start.15 = (bf16[192,1536]{1,0:T(8,128)(2,1)S(1)}, bf16[192,1536]{1,0:T(8,128)(2,1)S(1)}, u32[]{:S(2)}, u32[]{:S(2)}) collective-permute-start(bf16[192,1536]{1,0:T(8,128)(2,1)S(1)} %get-tuple-element.204), channel_id=1, source_target_pairs={{0,16},{1,17},{2,18},{3,19},{4,20},{5,21},{6,22},{7,23},{8,24},{9,... | collective-permute-start | bytes 1769480 | tf_op jit(solution)/shard_map/ppermute | solution.py:738
  129.1 17.4 %collective-permute-start.18 = (bf16[384,768]{1,0:T(8,128)(2,1)S(1)}, bf16[384,768]{1,0:T(8,128)(2,1)S(1)}, u32[]{:S(2)}, u32[]{:S(2)}) collective-permute-start(bf16[384,768]{1,0:T(8,128)(2,1)S(1)} %add_convert_fusion.14), channel_id=1, source_target_pairs={{0,8},{1,9},{2,10},{3,11},{4,12},{5,13},{6,14},{7,15},{8,0},{9,1},... | collective-permute-start | bytes 1769480 | tf_op jit(solution)/shard_map/ppermute | solution.py:738
  133.1 10.8 %collective-permute-start.17 = (bf16[96,3072]{1,0:T(8,128)(2,1)S(1)}, bf16[96,3072]{1,0:T(8,128)(2,1)S(1)}, u32[]{:S(2)}, u32[]{:S(2)}) collective-permute-start(bf16[96,3072]{1,0:T(8,128)(2,1)S(1)} %get-tuple-element.287), channel_id=1, source_target_pairs={{0,2},{1,3},{2,0},{3,1},{4,6},{5,7},{6,4},{7,5},{8,10},{9,11},{10,... | collective-permute-start | bytes 1769480 | tf_op jit(solution)/shard_map/ppermute | solution.py:738
  138.7 9.6 %collective-permute-start.20 = (bf16[192,1664]{1,0:T(8,128)(2,1)S(1)}, bf16[192,1664]{1,0:T(8,128)(2,1)S(1)}, u32[]{:S(2)}, u32[]{:S(2)}) collective-permute-start(bf16[192,1664]{1,0:T(8,128)(2,1)S(1)} %get-tuple-element.214), channel_id=1, source_target_pairs={{0,16},{1,17},{2,18},{3,19},{4,20},{5,21},{6,22},{7,23},{8,24},{9,... | collective-permute-start | bytes 1916936 | tf_op jit(solution)/shard_map/ppermute | solution.py:738
  139.0 10.7 %collective-permute-start.21 = (bf16[192,1536]{1,0:T(8,128)(2,1)S(1)}, bf16[192,1536]{1,0:T(8,128)(2,1)S(1)}, u32[]{:S(2)}, u32[]{:S(2)}) collective-permute-start(bf16[192,1536]{1,0:T(8,128)(2,1)S(1)} %add_convert_fusion.11), channel_id=1, source_target_pairs={{0,1},{1,0},{2,3},{3,2},{4,5},{5,4},{6,7},{7,6},{8,9},{9,8},{10,11... | collective-permute-start | bytes 1769480 | tf_op jit(solution)/shard_map/ppermute | solution.py:738
  140.1 7.1 %collective-permute-start.19 = (bf16[192,1664]{1,0:T(8,128)(2,1)S(1)}, bf16[192,1664]{1,0:T(8,128)(2,1)S(1)}, u32[]{:S(2)}, u32[]{:S(2)}) collective-permute-start(bf16[192,1664]{1,0:T(8,128)(2,1)S(1)} %get-tuple-element.218), channel_id=1, source_target_pairs={{0,16},{1,17},{2,18},{3,19},{4,20},{5,21},{6,22},{7,23},{8,24},{9,... | collective-permute-start | bytes 1916936 | tf_op jit(solution)/shard_map/ppermute | solution.py:738
  144.0 15.7 %collective-permute-start.22 = (bf16[96,3072]{1,0:T(8,128)(2,1)S(1)}, bf16[96,3072]{1,0:T(8,128)(2,1)S(1)}, u32[]{:S(2)}, u32[]{:S(2)}) collective-permute-start(bf16[96,3072]{1,0:T(8,128)(2,1)S(1)} %add_convert_fusion.9), channel_id=1, source_target_pairs={{0,4},{1,5},{2,6},{3,7},{4,0},{5,1},{6,2},{7,3},{8,12},{9,13},{10,... | collective-permute-start | bytes 1769480 | tf_op jit(solution)/shard_map/ppermute | solution.py:738
  146.7 15.8 %collective-permute-start.23 = (bf16[384,768]{1,0:T(8,128)(2,1)S(1)}, bf16[384,768]{1,0:T(8,128)(2,1)S(1)}, u32[]{:S(2)}, u32[]{:S(2)}) collective-permute-start(bf16[384,768]{1,0:T(8,128)(2,1)S(1)} %add_convert_fusion.8), channel_id=1, source_target_pairs={{0,2},{1,3},{2,0},{3,1},{4,6},{5,7},{6,4},{7,5},{8,10},{9,11},{10,... | collective-permute-start | bytes 1769480 | tf_op jit(solution)/shard_map/ppermute | solution.py:738
  147.4 24.1 %collective-permute-start.25 = (bf16[192,1664]{1,0:T(8,128)(2,1)S(1)}, bf16[192,1664]{1,0:T(8,128)(2,1)S(1)}, u32[]{:S(2)}, u32[]{:S(2)}) collective-permute-start(bf16[192,1664]{1,0:T(8,128)(2,1)S(1)} %add_convert_fusion.5), channel_id=1, source_target_pairs={{0,1},{1,0},{2,3},{3,2},{4,5},{5,4},{6,7},{7,6},{8,9},{9,8},{10,11... | collective-permute-start | bytes 1916936 | tf_op jit(solution)/shard_map/ppermute | solution.py:738
  149.8 21.2 %collective-permute-start.24 = (bf16[96,1536]{1,0:T(8,128)(2,1)S(1)}, bf16[96,1536]{1,0:T(8,128)(2,1)S(1)}, u32[]{:S(2)}, u32[]{:S(2)}) collective-permute-start(bf16[96,1536]{1,0:T(8,128)(2,1)S(1)} %get-tuple-element.293), channel_id=1, source_target_pairs={{0,2},{1,3},{2,0},{3,1},{4,6},{5,7},{6,4},{7,5},{8,10},{9,11},{10,... | collective-permute-start | bytes 884744 | tf_op jit(solution)/shard_map/ppermute | solution.py:738
  159.9 22.5 %collective-permute-start.26 = (bf16[96,3072]{1,0:T(8,128)(2,1)S(1)}, bf16[96,3072]{1,0:T(8,128)(2,1)S(1)}, u32[]{:S(2)}, u32[]{:S(2)}) collective-permute-start(bf16[96,3072]{1,0:T(8,128)(2,1)S(1)} %add_convert_fusion.7), channel_id=1, source_target_pairs={{0,8},{1,9},{2,10},{3,11},{4,12},{5,13},{6,14},{7,15},{8,0},{9,1},... | collective-permute-start | bytes 1769480 | tf_op jit(solution)/shard_map/ppermute | solution.py:738
  162.5 21.8 %collective-permute-start.27 = (bf16[768,768]{1,0:T(8,128)(2,1)S(1)}, bf16[768,768]{1,0:T(8,128)(2,1)S(1)}, u32[]{:S(2)}, u32[]{:S(2)}) collective-permute-start(bf16[768,768]{1,0:T(8,128)(2,1)S(1)} %constant_dynamic-update-slice_fusion.9.refs_0_), channel_id=1, source_target_pairs={{0,1},{1,0},{2,3},{3,2},{4,5},{5,4},{6,7},{7,6},{8,9},{9,8},{10,11... | collective-permute-start | bytes 3538952 | tf_op jit(solution)/shard_map/ppermute | solution.py:738
  171.2 13.2 %collective-permute-start.28 = (bf16[96,1536]{1,0:T(8,128)(2,1)S(1)}, bf16[96,1536]{1,0:T(8,128)(2,1)S(1)}, u32[]{:S(2)}, u32[]{:S(2)}) collective-permute-start(bf16[96,1536]{1,0:T(8,128)(2,1)S(1)} %add_convert_fusion.25), channel_id=1, source_target_pairs={{0,4},{1,5},{2,6},{3,7},{4,0},{5,1},{6,2},{7,3},{8,12},{9,13},{10,... | collective-permute-start | bytes 884744 | tf_op jit(solution)/shard_map/ppermute | solution.py:738
  171.7 12.8 %collective-permute-start.29 = (bf16[96,1664]{1,0:T(8,128)(2,1)S(1)}, bf16[96,1664]{1,0:T(8,128)(2,1)S(1)}, u32[]{:S(2)}, u32[]{:S(2)}) collective-permute-start(bf16[96,1664]{1,0:T(8,128)(2,1)S(1)} %get-tuple-element.291), channel_id=1, source_target_pairs={{0,2},{1,3},{2,0},{3,1},{4,6},{5,7},{6,4},{7,5},{8,10},{9,11},{10,... | collective-permute-start | bytes 958472 | tf_op jit(solution)/shard_map/ppermute | solution.py:738
  182.6 11.0 %collective-permute-start.30 = (bf16[96,3072]{1,0:T(8,128)(2,1)S(1)}, bf16[96,3072]{1,0:T(8,128)(2,1)S(1)}, u32[]{:S(2)}, u32[]{:S(2)}) collective-permute-start(bf16[96,3072]{1,0:T(8,128)(2,1)S(1)} %add_convert_fusion.6), channel_id=1, source_target_pairs={{0,2},{1,3},{2,0},{3,1},{4,6},{5,7},{6,4},{7,5},{8,10},{9,11},{10,... | collective-permute-start | bytes 1769480 | tf_op jit(solution)/shard_map/ppermute | solution.py:738
  182.6 22.1 %collective-permute-start.34 = (bf16[768,768]{1,0:T(8,128)(2,1)S(1)}, bf16[768,768]{1,0:T(8,128)(2,1)S(1)}, u32[]{:S(2)}, u32[]{:S(2)}) collective-permute-start(bf16[768,768]{1,0:T(8,128)(2,1)S(1)} %constant_dynamic-update-slice_fusion.9.refs_0_), channel_id=1, source_target_pairs={{0,16},{1,17},{2,18},{3,19},{4,20},{5,21},{6,22},{7,23},{8,24},{9,... | collective-permute-start | bytes 3538952 | tf_op jit(solution)/shard_map/ppermute | solution.py:738
  184.5 12.5 %collective-permute-start.31 = (bf16[96,1664]{1,0:T(8,128)(2,1)S(1)}, bf16[96,1664]{1,0:T(8,128)(2,1)S(1)}, u32[]{:S(2)}, u32[]{:S(2)}) collective-permute-start(bf16[96,1664]{1,0:T(8,128)(2,1)S(1)} %add_convert_fusion.20), channel_id=1, source_target_pairs={{0,4},{1,5},{2,6},{3,7},{4,0},{5,1},{6,2},{7,3},{8,12},{9,13},{10,... | collective-permute-start | bytes 958472 | tf_op jit(solution)/shard_map/ppermute | solution.py:738
  185.2 19.5 %collective-permute-start.35 = (bf16[768,768]{1,0:T(8,128)(2,1)S(1)}, bf16[768,768]{1,0:T(8,128)(2,1)S(1)}, u32[]{:S(2)}, u32[]{:S(2)}) collective-permute-start(bf16[768,768]{1,0:T(8,128)(2,1)S(1)} %collective-permute-done.27.refs_1_), channel_id=1, source_target_pairs={{0,16},{1,17},{2,18},{3,19},{4,20},{5,21},{6,22},{7,23},{8,24},{9,... | collective-permute-start | bytes 3538952 | tf_op jit(solution)/shard_map/ppermute | solution.py:738
  193.6 19.4 %collective-permute-start.36 = (bf16[192,3072]{1,0:T(8,128)(2,1)S(1)}, bf16[192,3072]{1,0:T(8,128)(2,1)S(1)}, u32[]{:S(2)}, u32[]{:S(2)}) collective-permute-start(bf16[192,3072]{1,0:T(8,128)(2,1)S(1)} %constant_dynamic-update-slice_fusion.11.refs_0_), channel_id=1, source_target_pairs={{0,1},{1,0},{2,3},{3,2},{4,5},{5,4},{6,7},{7,6},{8,9},{9,8},{10,11... | collective-permute-start | bytes 3538952 | tf_op jit(solution)/shard_map/ppermute | solution.py:738
  193.7 10.8 %collective-permute-start.32 = (bf16[96,1536]{1,0:T(8,128)(2,1)S(1)}, bf16[96,1536]{1,0:T(8,128)(2,1)S(1)}, u32[]{:S(2)}, u32[]{:S(2)}) collective-permute-start(bf16[96,1536]{1,0:T(8,128)(2,1)S(1)} %add_convert_fusion.24), channel_id=1, source_target_pairs={{0,8},{1,9},{2,10},{3,11},{4,12},{5,13},{6,14},{7,15},{8,0},{9,1},... | collective-permute-start | bytes 884744 | tf_op jit(solution)/shard_map/ppermute | solution.py:738
  197.2 15.9 %collective-permute-start.33 = (bf16[96,1664]{1,0:T(8,128)(2,1)S(1)}, bf16[96,1664]{1,0:T(8,128)(2,1)S(1)}, u32[]{:S(2)}, u32[]{:S(2)}) collective-permute-start(bf16[96,1664]{1,0:T(8,128)(2,1)S(1)} %add_convert_fusion.19), channel_id=1, source_target_pairs={{0,8},{1,9},{2,10},{3,11},{4,12},{5,13},{6,14},{7,15},{8,0},{9,1},... | collective-permute-start | bytes 958472 | tf_op jit(solution)/shard_map/ppermute | solution.py:738
  204.6 8.6 %collective-permute-start.37 = (bf16[96,1536]{1,0:T(8,128)(2,1)S(1)}, bf16[96,1536]{1,0:T(8,128)(2,1)S(1)}, u32[]{:S(2)}, u32[]{:S(2)}) collective-permute-start(bf16[96,1536]{1,0:T(8,128)(2,1)S(1)} %add_convert_fusion.23), channel_id=1, source_target_pairs={{0,2},{1,3},{2,0},{3,1},{4,6},{5,7},{6,4},{7,5},{8,10},{9,11},{10,... | collective-permute-start | bytes 884744 | tf_op jit(solution)/shard_map/ppermute | solution.py:738
  207.9 18.3 %collective-permute-start.39 = (bf16[192,3072]{1,0:T(8,128)(2,1)S(1)}, bf16[192,3072]{1,0:T(8,128)(2,1)S(1)}, u32[]{:S(2)}, u32[]{:S(2)}) collective-permute-start(bf16[192,3072]{1,0:T(8,128)(2,1)S(1)} %constant_dynamic-update-slice_fusion.11.refs_0_), channel_id=1, source_target_pairs={{0,16},{1,17},{2,18},{3,19},{4,20},{5,21},{6,22},{7,23},{8,24},{9,... | collective-permute-start | bytes 3538952 | tf_op jit(solution)/shard_map/ppermute | solution.py:738
  213.1 13.1 %collective-permute-start.40 = (bf16[192,3072]{1,0:T(8,128)(2,1)S(1)}, bf16[192,3072]{1,0:T(8,128)(2,1)S(1)}, u32[]{:S(2)}, u32[]{:S(2)}) collective-permute-start(bf16[192,3072]{1,0:T(8,128)(2,1)S(1)} %collective-permute-done.36.refs_1_), channel_id=1, source_target_pairs={{0,16},{1,17},{2,18},{3,19},{4,20},{5,21},{6,22},{7,23},{8,24},{9,... | collective-permute-start | bytes 3538952 | tf_op jit(solution)/shard_map/ppermute | solution.py:738
  213.2 10.5 %collective-permute-start.38 = (bf16[96,1664]{1,0:T(8,128)(2,1)S(1)}, bf16[96,1664]{1,0:T(8,128)(2,1)S(1)}, u32[]{:S(2)}, u32[]{:S(2)}) collective-permute-start(bf16[96,1664]{1,0:T(8,128)(2,1)S(1)} %add_convert_fusion.18), channel_id=1, source_target_pairs={{0,2},{1,3},{2,0},{3,1},{4,6},{5,7},{6,4},{7,5},{8,10},{9,11},{10,... | collective-permute-start | bytes 958472 | tf_op jit(solution)/shard_map/ppermute | solution.py:738
  213.3 12.8 %collective-permute-start.42 = (bf16[192,1536]{1,0:T(8,128)(2,1)S(1)}, bf16[192,1536]{1,0:T(8,128)(2,1)S(1)}, u32[]{:S(2)}, u32[]{:S(2)}) collective-permute-start(bf16[192,1536]{1,0:T(8,128)(2,1)S(1)} %constant_dynamic-update-slice_fusion.13.refs_0_), channel_id=1, source_target_pairs={{0,1},{1,0},{2,3},{3,2},{4,5},{5,4},{6,7},{7,6},{8,9},{9,8},{10,11... | collective-permute-start | bytes 1769480 | tf_op jit(solution)/shard_map/ppermute | solution.py:738
  223.7 10.5 %collective-permute-start.45 = (bf16[192,1664]{1,0:T(8,128)(2,1)S(1)}, bf16[192,1664]{1,0:T(8,128)(2,1)S(1)}, u32[]{:S(2)}, u32[]{:S(2)}) collective-permute-start(bf16[192,1664]{1,0:T(8,128)(2,1)S(1)} %constant_dynamic-update-slice_fusion.15.refs_0_), channel_id=1, source_target_pairs={{0,1},{1,0},{2,3},{3,2},{4,5},{5,4},{6,7},{7,6},{8,9},{9,8},{10,11... | collective-permute-start | bytes 1916936 | tf_op jit(solution)/shard_map/ppermute | solution.py:738
  226.1 10.6 %collective-permute-start.43 = (bf16[192,1536]{1,0:T(8,128)(2,1)S(1)}, bf16[192,1536]{1,0:T(8,128)(2,1)S(1)}, u32[]{:S(2)}, u32[]{:S(2)}) collective-permute-start(bf16[192,1536]{1,0:T(8,128)(2,1)S(1)} %collective-permute-done.42.refs_1_), channel_id=1, source_target_pairs={{0,16},{1,17},{2,18},{3,19},{4,20},{5,21},{6,22},{7,23},{8,24},{9,... | collective-permute-start | bytes 1769480 | tf_op jit(solution)/shard_map/ppermute | solution.py:738
  229.4 7.3 %collective-permute-start.41 = (bf16[192,1536]{1,0:T(8,128)(2,1)S(1)}, bf16[192,1536]{1,0:T(8,128)(2,1)S(1)}, u32[]{:S(2)}, u32[]{:S(2)}) collective-permute-start(bf16[192,1536]{1,0:T(8,128)(2,1)S(1)} %constant_dynamic-update-slice_fusion.13.refs_0_), channel_id=1, source_target_pairs={{0,16},{1,17},{2,18},{3,19},{4,20},{5,21},{6,22},{7,23},{8,24},{9,... | collective-permute-start | bytes 1769480 | tf_op jit(solution)/shard_map/ppermute | solution.py:738
  234.1 8.7 %collective-permute-start.46 = (bf16[192,1664]{1,0:T(8,128)(2,1)S(1)}, bf16[192,1664]{1,0:T(8,128)(2,1)S(1)}, u32[]{:S(2)}, u32[]{:S(2)}) collective-permute-start(bf16[192,1664]{1,0:T(8,128)(2,1)S(1)} %collective-permute-done.45.refs_1_), channel_id=1, source_target_pairs={{0,16},{1,17},{2,18},{3,19},{4,20},{5,21},{6,22},{7,23},{8,24},{9,... | collective-permute-start | bytes 1916936 | tf_op jit(solution)/shard_map/ppermute | solution.py:738
  239.2 3.7 %collective-permute-start.44 = (bf16[192,1664]{1,0:T(8,128)(2,1)S(1)}, bf16[192,1664]{1,0:T(8,128)(2,1)S(1)}, u32[]{:S(2)}, u32[]{:S(2)}) collective-permute-start(bf16[192,1664]{1,0:T(8,128)(2,1)S(1)} %constant_dynamic-update-slice_fusion.15.refs_0_), channel_id=1, source_target_pairs={{0,16},{1,17},{2,18},{3,19},{4,20},{5,21},{6,22},{7,23},{8,24},{9,... | collective-permute-start | bytes 1916936 | tf_op jit(solution)/shard_map/ppermute | solution.py:738
  (4 other events, 7.9 us)

commit v5 on v4

--- a/solution.py
+++ b/solution.py
@@ -809,7 +809,7 @@
     hidden = up_bias.shape[0]
     tokens, upstream = in_far(layer_input[0]), in_far(upstream[0])
     wq, wk, wv, wo = map(in_far, (query_weight, key_weight, value_weight, out_weight))
-    uw, dw = in_far(up_weight), in_far(down_weight)
+    uw, dw = in_near(up_weight), in_near(down_weight)
     fold = lambda vector: in_far(vector.reshape(-1, LANES))
     bq, bv, bo, g1, s1 = map(fold, (query_bias, value_bias, out_bias, mixer_gain, mixer_shift))
     ub, db, g2, s2 = map(fold, (up_bias, down_bias, final_gain, final_shift))
@@ -843,13 +843,13 @@
     down_kept = down_gradient(place, 0, act, tie(dbranch, sent))
     sent = down_kept
     sent = down.send(tie(down_kept, sent))
-    dpre, up_sums, *up_blocks = hidden_gradient(place, tie(dbranch, sent), slope, dw, nl)
+    dpre, up_sums, *up_blocks = hidden_gradient(place, tie(dbranch, sent), slope, in_far(down_weight), nl)
     sent = dpre
     sent = down.send(sent)
     up = all_sum(up_blocks[2:])
     next(up)
     sent = (sent, up_blocks[2:])
-    stack, dctx, mixer = norm_one_backward(tie(dpre, sent), dbranch, hat, inv, uw, wo, g1)
+    stack, dctx, mixer = norm_one_backward(tie(dpre, sent), dbranch, hat, inv, in_far(up_weight), wo, g1)
     sent = dctx
     sent = down.send(sent)
     sent = up.send(tie(up_blocks[:2], sent))

time: 246 us -> 245 us (level)
  Pallas kernels: 138 us -> 135 us
  transfers between devices with their start and end apart: 47 -> 47, of which waited for: 15 -> 15; matrix products, arithmetic and copies ran while one was open for 4% -> 4% of each run, Pallas kernels for 44% -> 43%
where the time goes in v5:
time: 245 us
  Pallas kernels  135 us (55%)
  waiting for transfers between devices  60.7 us (25%)
  starting transfers between devices  33.7 us (14%)
  other arithmetic  8.57 us (3%)
  local copies, waits for them, and re-layouts  5.05 us (2%)
    ppermute x47, waiting for transfers between devices, swap(): return lax.ppermute(piece, ('stream', 'dp'), pairs)  60.7 us
    ppermute x47, starting transfers between devices, swap(): return lax.ppermute(piece, ('stream', 'dp'), pairs)  33.7 us
    pallas_call x2, Pallas kernels, ff_forward(): pl.pallas_call(functools.partial(ff_kernel, part, seq_len), grid=(hidden...  29.6 us
    pallas_call x8, Pallas kernels, spread(): pl.pallas_call(functools.partial(spread_kernel, widths, talls, first), gr...  22.7 us
    pallas_call x1, Pallas kernels, hidden_gradient(): pl.pallas_call(hidden_kernel, grid_spec=pltpu.PrefetchScalarGridSpec(num_...  14.9 us
    pallas_call x1, Pallas kernels, attention_forward(): pl.pallas_call(functools.partial(attention_kernel, seq_len), grid=(steps,...  14.3 us
    pallas_call x2, Pallas kernels, down_gradient(): pl.pallas_call(functools.partial(down_grad_kernel, seq_len, fresh), grid_...  12.3 us
    pallas_call x1, Pallas kernels, norm_one_backward(): pl.pallas_call(norm_one_kernel, grid=(hidden // D,), in_specs=[pl.BlockSp...  11 us
  transfers between devices with their start and end apart: 47, of which 15 were waited for; matrix products, arithmetic and copies ran while one was open for 4% of the time, Pallas kernels for 43%

profile of v5, /device:TPU:0, one launch (start us, length us, event | category | flops | bytes accessed | tf_op | source)
XLA Modules:
  0.0 244.8 jit_solution(15836502389442875238)
XLA Ops:
  1.3 14.3 %attention_forward.1 = (bf16[1024,768]{1,0:T(8,128)(2,1)}, bf16[1024,768]{1,0:T(8,128)(2,1)}, bf16[1024,768]{1,0:T(8,128)(2,1)}, bf16[1024,768]{1,0:T(8,128)(2,1...) custom-call(bf16[1024,768]{1,0:T(8,128)(2,1)} %bitcast.36, ...), custom_call_target="tpu_custom_call" | custom-call | flops 230000000 | bytes 1000 | tf_op jit(solution)/shard_map/attention_forward/pallas_call | solution.py:164
  15.6 2.3 copy-done.1
  17.9 3.6 %lead_forward.1 = (f32[16,768]{1,0:T(8,128)S(1)}, f32[16,768]{1,0:T(8,128)S(1)}, f32[16,128]{1,0:T(8,128)S(1)}, f32[16,128]{1,0:T(8,128)S(1)}, bf16[16,768]{1,0:T(8,128)(2,1)S(1)}) custom-call(f32[4,4,768]{2,1,0:T(4,128)S(1)} %get-tuple-element.149.nl_ref, f32[4,4,768]{2,1,0:T(4,128)S(1)} %get-tuple-element.150.hat_ref, bf16[768,3072]{1,0:T(8,128)(2,1)S(1)} %copy-done, ...), custom_call_target="tpu_custom_call" | custom-call | flops 69000000 | bytes 1000 | tf_op jit(solution)/shard_map/lead_forward/pallas_call | solution.py:207
  21.6 2.9 %collective-permute-start = (bf16[16,896]{1,0:T(8,128)(2,1)S(1)}, bf16[16,896]{1,0:T(8,128)(2,1)S(1)}, u32[]{:S(2)}, u32[]{:S(2)}) collective-permute-start(bf16[16,896]{1,0:T(8,128)(2,1)S(1)} %pad_maximum_fusion), channel_id=1, source_target_pairs={{0,1},{1,0},{2,3},{3,2},{4,5},{5,4},{6,7},{7,6},{8,9},{9,8},{10,11... | collective-permute-start | bytes 86024 | tf_op jit(solution)/shard_map/ppermute | solution.py:738
  24.6 1.5 collective-permute-start.1
  26.1 14.8 %ff_forward_0.1 = (bf16[1024,768]{1,0:T(8,128)(2,1)}, bf16[1024,3072]{1,0:T(8,128)(2,1)}, bf16[1024,3072]{1,0:T(8,128)(2,1)}, bf16[1024,768]{1,0:T(8,128)(2,1)},...) custom-call(bf16[1024,768]{1,0:T(8,128)(2,1)} %get-tuple-element.156.nl_ref, bf16[768,3072]{1,0:T(8,128)(2,1)S(1)} %copy-done, ...), custom_call_target="tpu_custom_call" | custom-call | flops 299000000 | bytes 1000 | tf_op jit(solution)/shard_map/ff_forward_0/pallas_call | solution.py:281
  41.0 2.1 collective-permute-start.3
  43.1 2.6 %collective-permute-start.4 = (bf16[64,896]{1,0:T(8,128)(2,1)S(1)}, bf16[64,896]{1,0:T(8,128)(2,1)S(1)}, u32[]{:S(2)}, u32[]{:S(2)}) collective-permute-start(bf16[64,896]{1,0:T(8,128)(2,1)S(1)} %constant_dynamic-update-slice_fusion), channel_id=1, source_target_pairs={{0,8},{1,9},{2,10},{3,11},{4,12},{5,13},{6,14},{7,15},{8,0},{9,1},... | collective-permute-start | bytes 344072 | tf_op jit(solution)/shard_map/ppermute | solution.py:738
  45.7 14.8 %ff_forward_1.1 = (bf16[1024,768]{1,0:T(8,128)(2,1)}, bf16[1024,3072]{1,0:T(8,128)(2,1)}, bf16[1024,3072]{1,0:T(8,128)(2,1)}, bf16[1024,768]{1,0:T(8,128)(2,1)},...) custom-call(bf16[1024,768]{1,0:T(8,128)(2,1)} %get-tuple-element.156, ...), custom_call_target="tpu_custom_call", output_to_operand_aliasing={{0}: (11, {}), {1}: (12, {}), {2}: (13, {}), {3}: (14, {}),... | custom-call | flops 299000000 | bytes 1000 | tf_op jit(solution)/shard_map/ff_forward_1/pallas_call | solution.py:281
  60.8 1.7 collective-permute-done.6.other_ref
  62.5 1.8 pair_loss.1
  64.2 6.8 %down_grad_4.1 = (bf16[768,768]{1,0:T(8,128)(2,1)}, bf16[768,768]{1,0:T(8,128)(2,1)S(1)}, bf16[1024,768]{1,0:T(8,128)(2,1)S(1)}, f32[1,768]{1,0:T(1,128)S(1)}) custom-call(s32[8]{0:T(128)S(1)} %stack.35.place, bf16[1024,768]{1,0:T(8,128)(2,1)S(1)} %copy-done.2, f32[16,768]{1,0:T(8,128)S(1)} %bitcast.34, f32[16,768]{1,0:T(8,128)S(1)} %get-tuple-element.175.refs_2_, ...), custom_call_target="tpu_custom_call" | custom-call | flops 92000000 | bytes 1000 | tf_op jit(solution)/shard_map/down_grad_4/pallas_call | solution.py:413
  71.5 5.6 %down_grad_0.1 = (bf16[768,768]{1,0:T(8,128)(2,1)S(1)}, bf16[768,768]{1,0:T(8,128)(2,1)S(1)}) custom-call(s32[8]{0:T(128)S(1)} %stack.35.place, bf16[1024,768]{1,0:T(8,128)(2,1)S(1)} %get-tuple-element.183.refs_0_.db_ref.branch_far, bf16[1024,3072]{1,0:T(8,128)(2,1)} %get-tuple-element.176.refs_3_.refs_1_), custom_call_target="tpu_custom_call" | custom-call | flops 92000000 | bytes 1000 | tf_op jit(solution)/shard_map/down_grad_0/pallas_call | solution.py:413
  77.1 1.3 add_convert_fusion.3
  78.4 1.7 collective-permute-start.9
  80.1 1.6 add_convert_fusion.2
  81.7 14.9 %hidden_gradient.1 = (bf16[1024,3072]{1,0:T(8,128)(2,1)}, f32[8,3072]{1,0:T(8,128)S(1)}, bf16[192,3072]{1,0:T(8,128)(2,1)S(1)}, bf16[192,3072]{1,0:T(8,128)(2,1)...) custom-call(s32[8]{0:T(128)S(1)} %stack.35.place, ...), custom_call_target="tpu_custom_call", output_to_operand_aliasing={{0}: (2, {})} | custom-call | flops 345000000 | bytes 1000 | tf_op jit(solution)/shard_map/hidden_gradient/pallas_call | solution.py:445
  97.2 1.6 add_convert_fusion.16
  98.7 1.6 collective-permute-start.10
  100.3 11.0 %norm_one_backward.1 = (bf16[4,1024,768]{2,1,0:T(8,128)(2,1)S(1)}, bf16[1024,768]{1,0:T(8,128)(2,1)S(1)}, f32[8,768]{1,0:T(8,128)S(1)}) custom-call(bf16[1024,3072]{1,0:T(8,128)(2,1)} %get-tuple-element.189.dpre_ref, bf16[768,3072]{1,0:T(8,128)(2,1)} %uw.7, f32[6,128]{1,0:T(8,128)} %bitcast.50, bf16[768,768]{1,0:T(8,128)(2,1)} %wo_far.1, ...), custom_call_target="tpu_custom_call" | custom-call | flops 299000000 | bytes 1000 | tf_op jit(solution)/shard_map/norm_one_backward/pallas_call | solution.py:501
  115.3 7.0 %attention_backward.1 = (bf16[4,1024,768]{2,1,0:T(8,128)(2,1)S(1)}, f32[8,768]{1,0:T(8,128)S(1)}) custom-call(bf16[1024,768]{1,0:T(8,128)(2,1)S(1)} %copy-done.3, bf16[1024,768]{1,0:T(8,128)(2,1)S(1)} %copy-done.4, bf16[1024,768]{1,0:T(8,128)(2,1)S(1)} %copy-done.5, bf16[1024,768]{1,0:T(8,128)(2,1)S(1)} %copy-done.6, ...), custom_call_target="tpu_custom_call", output_to_operand_aliasing={{0}: (5, {})} | custom-call | flops 184000000 | bytes 1000 | tf_op jit(solution)/shard_map/attention_backward/pallas_call | solution.py:559
  122.3 5.3 %value_gradient.1 = (bf16[192,1536]{1,0:T(8,128)(2,1)S(1)}, bf16[192,1536]{1,0:T(8,128)(2,1)S(1)}, bf16[192,1536]{1,0:T(8,128)(2,1)S(1)}, bf16[192,1536]{1,0:T(8,128)(2,1)S(1)}) custom-call(s32[8]{0:T(128)S(1)} %stack.35.place, bf16[1024,768]{1,0:T(8,128)(2,1)} %get-tuple-element.200.left_ref, bf16[4,1024,768]{2,1,0:T(8,128)(2,1)S(1)} %get-tuple-element.227.d_ref, ...), custom_call_target="tpu_custom_call" | custom-call | flops 138000000 | bytes 1000 | tf_op jit(solution)/shard_map/value_gradient/pallas_call | solution.py:612
  128.4 3.6 %collective-permute-start.18 = (bf16[384,768]{1,0:T(8,128)(2,1)S(1)}, bf16[384,768]{1,0:T(8,128)(2,1)S(1)}, u32[]{:S(2)}, u32[]{:S(2)}) collective-permute-start(bf16[384,768]{1,0:T(8,128)(2,1)S(1)} %add_convert_fusion.14), channel_id=1, source_target_pairs={{0,8},{1,9},{2,10},{3,11},{4,12},{5,13},{6,14},{7,15},{8,0},{9,1},... | collective-permute-start | bytes 1769480 | tf_op jit(solution)/shard_map/ppermute | solution.py:738
  132.9 5.1 %query_gradient.1 = (bf16[192,1664]{1,0:T(8,128)(2,1)S(1)}, bf16[192,1664]{1,0:T(8,128)(2,1)S(1)}, bf16[192,1664]{1,0:T(8,128)(2,1)S(1)}, bf16[192,1664]{1,0:T(8,128)(2,1)S(1)}) custom-call(s32[8]{0:T(128)S(1)} %stack.35.place, bf16[1024,768]{1,0:T(8,128)(2,1)} %bitcast.38, bf16[4,1024,768]{2,1,0:T(8,128)(2,1)S(1)} %get-tuple-element.227.d_ref, ...), custom_call_target="tpu_custom_call" | custom-call | flops 138000000 | bytes 1000 | tf_op jit(solution)/shard_map/query_gradient/pallas_call | solution.py:612
  140.3 2.8 %collective-permute-done.17 = bf16[96,3072]{1,0:T(8,128)(2,1)S(1)} collective-permute-done((bf16[96,3072]{1,0:T(8,128)(2,1)S(1)}, bf16[96,3072]{1,0:T(8,128)(2,1)S(1)}, u32[]{:S(2)}, u32[]{:S(2)}) %collective-permute-start.17) | collective-permute-done | bytes 589856 | tf_op jit(solution)/shard_map/ppermute | solution.py:738
  143.3 2.5 %collective-permute-done.18 = bf16[384,768]{1,0:T(8,128)(2,1)S(1)} collective-permute-done((bf16[384,768]{1,0:T(8,128)(2,1)S(1)}, bf16[384,768]{1,0:T(8,128)(2,1)S(1)}, u32[]{:S(2)}, u32[]{:S(2)}) %collective-permute-start.18) | collective-permute-done | bytes 589856 | tf_op jit(solution)/shard_map/ppermute | solution.py:738
  149.1 1.8 collective-permute-start.24
  150.9 8.1 %collective-permute-done.22 = bf16[96,3072]{1,0:T(8,128)(2,1)S(1)} collective-permute-done((bf16[96,3072]{1,0:T(8,128)(2,1)S(1)}, bf16[96,3072]{1,0:T(8,128)(2,1)S(1)}, u32[]{:S(2)}, u32[]{:S(2)}) %collective-permute-start.22) | collective-permute-done | bytes 589856 | tf_op jit(solution)/shard_map/ppermute | solution.py:738
  160.2 1.6 collective-permute-done.23
  162.7 7.7 %input_gradient.1 = f32[1024,768]{1,0:T(8,128)} custom-call(bf16[4,1024,768]{2,1,0:T(8,128)(2,1)S(1)} %get-tuple-element.227.d_ref, bf16[768,768]{1,0:T(8,128)(2,1)} %wq.3, bf16[768,768]{1,0:T(8,128)(2,1)} %wk.3, bf16[768,768]{1,0:T(8,128)(2,1)} %wv.3), custom_call_target="tpu_custom_call" | custom-call | flops 138000000 | bytes 1000 | tf_op jit(solution)/shard_map/input_gradient/pallas_call | solution.py:642
  171.0 1.4 collective-permute-start.29
  172.4 9.2 %collective-permute-done.26 = bf16[96,3072]{1,0:T(8,128)(2,1)S(1)} collective-permute-done((bf16[96,3072]{1,0:T(8,128)(2,1)S(1)}, bf16[96,3072]{1,0:T(8,128)(2,1)S(1)}, u32[]{:S(2)}, u32[]{:S(2)}) %collective-permute-start.26) | collective-permute-done | bytes 589856 | tf_op jit(solution)/shard_map/ppermute | solution.py:738
  182.0 1.6 collective-permute-done.27.refs_1_
  184.5 8.3 %collective-permute-done.30 = bf16[96,3072]{1,0:T(8,128)(2,1)S(1)} collective-permute-done((bf16[96,3072]{1,0:T(8,128)(2,1)S(1)}, bf16[96,3072]{1,0:T(8,128)(2,1)S(1)}, u32[]{:S(2)}, u32[]{:S(2)}) %collective-permute-start.30) | collective-permute-done | bytes 589856 | tf_op jit(solution)/shard_map/ppermute | solution.py:738
  193.1 3.2 %down_spread_0.1.refs_2_ = f32[3072,768]{1,0:T(8,128)} custom-call(s32[8]{0:T(128)S(1)} %stack.35.place, bf16[768,768]{1,0:T(8,128)(2,1)S(1)} %constant_dynamic-update-slice_fusion.9.refs_0_, bf16[768,768]{1,0:T(8,128)(2,1)S(1)} %collective-permute-done.27.refs_1_), custom_call_target="tpu_custom_call" | custom-call | flops 69000000 | bytes 1000 | tf_op jit(solution)/shard_map/down_spread_0/pallas_call | solution.py:694
  196.4 2.8 %collective-permute-start.33 = (bf16[96,1664]{1,0:T(8,128)(2,1)S(1)}, bf16[96,1664]{1,0:T(8,128)(2,1)S(1)}, u32[]{:S(2)}, u32[]{:S(2)}) collective-permute-start(bf16[96,1664]{1,0:T(8,128)(2,1)S(1)} %add_convert_fusion.19), channel_id=1, source_target_pairs={{0,8},{1,9},{2,10},{3,11},{4,12},{5,13},{6,14},{7,15},{8,0},{9,1},... | collective-permute-start | bytes 958472 | tf_op jit(solution)/shard_map/ppermute | solution.py:738
  199.3 4.6 %collective-permute-done.32 = bf16[96,1536]{1,0:T(8,128)(2,1)S(1)} collective-permute-done((bf16[96,1536]{1,0:T(8,128)(2,1)S(1)}, bf16[96,1536]{1,0:T(8,128)(2,1)S(1)}, u32[]{:S(2)}, u32[]{:S(2)}) %collective-permute-start.32) | collective-permute-done | bytes 294944 | tf_op jit(solution)/shard_map/ppermute | solution.py:738
  204.0 3.2 %down_spread_4.1 = f32[3072,768]{1,0:T(8,128)} custom-call(s32[8]{0:T(128)S(1)} %stack.35.place, bf16[768,768]{1,0:T(8,128)(2,1)S(1)} %collective-permute-done.34.refs_0_, bf16[768,768]{1,0:T(8,128)(2,1)S(1)} %collective-permute-done.35.refs_1_, f32[3072,768]{1,0:T(8,128)} %down_spread_0.1.refs_2_), custom_call_target="tpu_custom_call", output_to_operand_aliasing={{}: (3, {})} | custom-call | flops 69000000 | bytes 1000 | tf_op jit(solution)/shard_map/down_spread_4/pallas_call | solution.py:694
  207.2 5.2 %collective-permute-done.36.refs_1_ = bf16[192,3072]{1,0:T(8,128)(2,1)S(1)} collective-permute-done((bf16[192,3072]{1,0:T(8,128)(2,1)S(1)}, bf16[192,3072]{1,0:T(8,128)(2,1)S(1)}, u32[]{:S(2)}, u32[]{:S(2)}) %collective-permute-start.36) | collective-permute-done | bytes 1179680 | tf_op jit(solution)/shard_map/ppermute | solution.py:738
  212.7 3.2 %up_spread_0.1.refs_2_ = f32[768,3072]{1,0:T(8,128)} custom-call(s32[8]{0:T(128)S(1)} %stack.35.place, bf16[192,3072]{1,0:T(8,128)(2,1)S(1)} %constant_dynamic-update-slice_fusion.11.refs_0_, bf16[192,3072]{1,0:T(8,128)(2,1)S(1)} %collective-permute-done.36.refs_1_), custom_call_target="tpu_custom_call" | custom-call | flops 69000000 | bytes 1000 | tf_op jit(solution)/shard_map/up_spread_0/pallas_call | solution.py:694
  215.8 7.1 %collective-permute-done.38 = bf16[96,1664]{1,0:T(8,128)(2,1)S(1)} collective-permute-done((bf16[96,1664]{1,0:T(8,128)(2,1)S(1)}, bf16[96,1664]{1,0:T(8,128)(2,1)S(1)}, u32[]{:S(2)}, u32[]{:S(2)}) %collective-permute-start.38) | collective-permute-done | bytes 319520 | tf_op jit(solution)/shard_map/ppermute | solution.py:738
  223.0 2.3 collective-permute-done.42.refs_1_
  225.5 3.2 %up_spread_4.1 = f32[768,3072]{1,0:T(8,128)} custom-call(s32[8]{0:T(128)S(1)} %stack.35.place, bf16[192,3072]{1,0:T(8,128)(2,1)S(1)} %collective-permute-done.39.refs_0_, bf16[192,3072]{1,0:T(8,128)(2,1)S(1)} %collective-permute-done.40.refs_1_, f32[768,3072]{1,0:T(8,128)} %up_spread_0.1.refs_2_), custom_call_target="tpu_custom_call", output_to_operand_aliasing={{}: (3, {})} | custom-call | flops 69000000 | bytes 1000 | tf_op jit(solution)/shard_map/up_spread_4/pallas_call | solution.py:694
  229.0 4.4 %collective-permute-done.45.refs_1_ = bf16[192,1664]{1,0:T(8,128)(2,1)S(1)} collective-permute-done((bf16[192,1664]{1,0:T(8,128)(2,1)S(1)}, bf16[192,1664]{1,0:T(8,128)(2,1)S(1)}, u32[]{:S(2)}, u32[]{:S(2)}) %collective-permute-start.45) | collective-permute-done | bytes 639008 | tf_op jit(solution)/shard_map/ppermute | solution.py:738
  233.4 2.5 %value_spread_0.1 = (f32[768,768]{1,0:T(8,128)}, f32[768,768]{1,0:T(8,128)}) custom-call(s32[8]{0:T(128)S(1)} %stack.35.place, bf16[192,1536]{1,0:T(8,128)(2,1)S(1)} %constant_dynamic-update-slice_fusion.13.refs_0_, bf16[192,1536]{1,0:T(8,128)(2,1)S(1)} %collective-permute-done.42.refs_1_), custom_call_target="tpu_custom_call" | custom-call | flops 69000000 | bytes 1000 | tf_op jit(solution)/shard_map/value_spread_0/pallas_call | solution.py:694
  235.9 2.5 %value_spread_4.1 = (f32[768,768]{1,0:T(8,128)}, f32[768,768]{1,0:T(8,128)}) custom-call(s32[8]{0:T(128)S(1)} %stack.35.place, bf16[192,1536]{1,0:T(8,128)(2,1)S(1)} %collective-permute-done.41.refs_0_, bf16[192,1536]{1,0:T(8,128)(2,1)S(1)} %collective-permute-done.43.refs_1_, ...), custom_call_target="tpu_custom_call", output_to_operand_aliasing={{0}: (3, {}), {1}: (4, {})} | custom-call | flops 69000000 | bytes 1000 | tf_op jit(solution)/shard_map/value_spread_4/pallas_call | solution.py:694
  239.6 2.5 %query_spread_0.1 = (f32[768,768]{1,0:T(8,128)}, f32[768,768]{1,0:T(8,128)}, f32[24,128]{1,0:T(8,128)S(1)}, f32[6,128]{1,0:T(8,128)S(1)}, f32[6,128]{1,0:T(8,128...) custom-call(s32[8]{0:T(128)S(1)} %stack.35.place, ...), custom_call_target="tpu_custom_call" | custom-call | flops 69000000 | bytes 1000 | tf_op jit(solution)/shard_map/query_spread_0/pallas_call | solution.py:694
  242.1 2.6 %query_spread_4.1 = (f32[768,768]{1,0:T(8,128)}, f32[768,768]{1,0:T(8,128)}, f32[24,128]{1,0:T(8,128)}, f32[6,128]{1,0:T(8,128)}, f32[6,128]{1,0:T(8,128)}, /*in...) custom-call(s32[8]{0:T(128)S(1)} %stack.35.place, ...), custom_call_target="tpu_custom_call", output_to_operand_aliasing={{0}: (12, {}), {1}: (13, {})} | custom-call | flops 69000000 | bytes 1000 | tf_op jit(solution)/shard_map/query_spread_4/pallas_call | solution.py:694
  (140 shorter events, 19.9 us)
Async XLA Ops:
  1.3 14.3 %copy-start = (bf16[768,3072]{1,0:T(8,128)(2,1)S(1)}, bf16[768,3072]{1,0:T(8,128)(2,1)}, u32[]{:S(2)}) copy-start(bf16[768,3072]{1,0:T(8,128)(2,1)} %uw.7) | copy-start | bytes 14155780
  21.6 19.3 %collective-permute-start = (bf16[16,896]{1,0:T(8,128)(2,1)S(1)}, bf16[16,896]{1,0:T(8,128)(2,1)S(1)}, u32[]{:S(2)}, u32[]{:S(2)}) collective-permute-start(bf16[16,896]{1,0:T(8,128)(2,1)S(1)} %pad_maximum_fusion), channel_id=1, source_target_pairs={{0,1},{1,0},{2,3},{3,2},{4,5},{5,4},{6,7},{7,6},{8,9},{9,8},{10,11... | collective-permute-start | bytes 86024 | tf_op jit(solution)/shard_map/ppermute | solution.py:738
  24.6 16.3 %collective-permute-start.1 = (bf16[16,896]{1,0:T(8,128)(2,1)S(1)}, bf16[16,896]{1,0:T(8,128)(2,1)S(1)}, u32[]{:S(2)}, u32[]{:S(2)}) collective-permute-start(bf16[16,896]{1,0:T(8,128)(2,1)S(1)} %pad_maximum_fusion), channel_id=1, source_target_pairs={{0,2},{1,3},{2,0},{3,1},{4,6},{5,7},{6,4},{7,5},{8,10},{9,11},{10,... | collective-permute-start | bytes 86024 | tf_op jit(solution)/shard_map/ppermute | solution.py:738
  26.1 14.9 %collective-permute-start.2 = (bf16[16,896]{1,0:T(8,128)(2,1)S(1)}, bf16[16,896]{1,0:T(8,128)(2,1)S(1)}, u32[]{:S(2)}, u32[]{:S(2)}) collective-permute-start(bf16[16,896]{1,0:T(8,128)(2,1)S(1)} %pad_maximum_fusion), channel_id=1, source_target_pairs={{0,3},{1,2},{2,1},{3,0},{4,7},{5,6},{6,5},{7,4},{8,11},{9,10},{10,... | collective-permute-start | bytes 86024 | tf_op jit(solution)/shard_map/ppermute | solution.py:738
  41.0 19.5 %collective-permute-start.3 = (bf16[64,896]{1,0:T(8,128)(2,1)S(1)}, bf16[64,896]{1,0:T(8,128)(2,1)S(1)}, u32[]{:S(2)}, u32[]{:S(2)}) collective-permute-start(bf16[64,896]{1,0:T(8,128)(2,1)S(1)} %constant_dynamic-update-slice_fusion), channel_id=1, source_target_pairs={{0,4},{1,5},{2,6},{3,7},{4,0},{5,1},{6,2},{7,3},{8,12},{9,13},{10,... | collective-permute-start | bytes 344072 | tf_op jit(solution)/shard_map/ppermute | solution.py:738
  43.1 17.5 %collective-permute-start.4 = (bf16[64,896]{1,0:T(8,128)(2,1)S(1)}, bf16[64,896]{1,0:T(8,128)(2,1)S(1)}, u32[]{:S(2)}, u32[]{:S(2)}) collective-permute-start(bf16[64,896]{1,0:T(8,128)(2,1)S(1)} %constant_dynamic-update-slice_fusion), channel_id=1, source_target_pairs={{0,8},{1,9},{2,10},{3,11},{4,12},{5,13},{6,14},{7,15},{8,0},{9,1},... | collective-permute-start | bytes 344072 | tf_op jit(solution)/shard_map/ppermute | solution.py:738
  45.6 14.9 %collective-permute-start.5 = (bf16[64,896]{1,0:T(8,128)(2,1)S(1)}, bf16[64,896]{1,0:T(8,128)(2,1)S(1)}, u32[]{:S(2)}, u32[]{:S(2)}) collective-permute-start(bf16[64,896]{1,0:T(8,128)(2,1)S(1)} %constant_dynamic-update-slice_fusion), channel_id=1, source_target_pairs={{0,12},{1,13},{2,14},{3,15},{4,8},{5,9},{6,10},{7,11},{8,4},{9,5},... | collective-permute-start | bytes 344072 | tf_op jit(solution)/shard_map/ppermute | solution.py:738
  60.6 1.9 collective-permute-start.6
  71.0 6.1 %collective-permute-start.7 = (bf16[768,768]{1,0:T(8,128)(2,1)S(1)}, bf16[768,768]{1,0:T(8,128)(2,1)S(1)}, u32[]{:S(2)}, u32[]{:S(2)}) collective-permute-start(bf16[768,768]{1,0:T(8,128)(2,1)S(1)} %get-tuple-element.179), channel_id=1, source_target_pairs={{0,16},{1,17},{2,18},{3,19},{4,20},{5,21},{6,22},{7,23},{8,24},{9,... | collective-permute-start | bytes 3538952 | tf_op jit(solution)/shard_map/ppermute | solution.py:738
  71.1 9.0 %collective-permute-start.8 = (bf16[768,768]{1,0:T(8,128)(2,1)}, bf16[768,768]{1,0:T(8,128)(2,1)}, u32[]{:S(2)}, u32[]{:S(2)}) collective-permute-start(bf16[768,768]{1,0:T(8,128)(2,1)} %get-tuple-element.178), channel_id=1, source_target_pairs={{0,16},{1,17},{2,18},{3,19},{4,20},{5,21},{6,22},{7,23},{8,24},{9,... | collective-permute-start | bytes 3538952 | tf_op jit(solution)/shard_map/ppermute | solution.py:738
  78.4 18.7 %collective-permute-start.9 = (bf16[768,768]{1,0:T(8,128)(2,1)}, bf16[768,768]{1,0:T(8,128)(2,1)}, u32[]{:S(2)}, u32[]{:S(2)}) collective-permute-start(bf16[768,768]{1,0:T(8,128)(2,1)} %add_convert_fusion.3), channel_id=1, source_target_pairs={{0,1},{1,0},{2,3},{3,2},{4,5},{5,4},{6,7},{7,6},{8,9},{9,8},{10,11... | collective-permute-start | bytes 3538952 | tf_op jit(solution)/shard_map/ppermute | solution.py:738
  96.6 16.8 %collective-permute-start.12 = (bf16[192,3072]{1,0:T(8,128)(2,1)S(1)}, bf16[192,3072]{1,0:T(8,128)(2,1)S(1)}, u32[]{:S(2)}, u32[]{:S(2)}) collective-permute-start(bf16[192,3072]{1,0:T(8,128)(2,1)S(1)} %get-tuple-element.187), channel_id=1, source_target_pairs={{0,16},{1,17},{2,18},{3,19},{4,20},{5,21},{6,22},{7,23},{8,24},{9,... | collective-permute-start | bytes 3538952 | tf_op jit(solution)/shard_map/ppermute | solution.py:738
  96.6 15.7 %collective-permute-start.11 = (bf16[192,3072]{1,0:T(8,128)(2,1)S(1)}, bf16[192,3072]{1,0:T(8,128)(2,1)S(1)}, u32[]{:S(2)}, u32[]{:S(2)}) collective-permute-start(bf16[192,3072]{1,0:T(8,128)(2,1)S(1)} %get-tuple-element.188), channel_id=1, source_target_pairs={{0,16},{1,17},{2,18},{3,19},{4,20},{5,21},{6,22},{7,23},{8,24},{9,... | collective-permute-start | bytes 3538952 | tf_op jit(solution)/shard_map/ppermute | solution.py:738
  98.7 12.7 %collective-permute-start.10 = (bf16[384,768]{1,0:T(8,128)(2,1)S(1)}, bf16[384,768]{1,0:T(8,128)(2,1)S(1)}, u32[]{:S(2)}, u32[]{:S(2)}) collective-permute-start(bf16[384,768]{1,0:T(8,128)(2,1)S(1)} %get-tuple-element.289), channel_id=1, source_target_pairs={{0,2},{1,3},{2,0},{3,1},{4,6},{5,7},{6,4},{7,5},{8,10},{9,11},{10,... | collective-permute-start | bytes 1769480 | tf_op jit(solution)/shard_map/ppermute | solution.py:738
  111.6 16.7 %collective-permute-start.13 = (bf16[384,768]{1,0:T(8,128)(2,1)S(1)}, bf16[384,768]{1,0:T(8,128)(2,1)S(1)}, u32[]{:S(2)}, u32[]{:S(2)}) collective-permute-start(bf16[384,768]{1,0:T(8,128)(2,1)S(1)} %add_convert_fusion.15), channel_id=1, source_target_pairs={{0,4},{1,5},{2,6},{3,7},{4,0},{5,1},{6,2},{7,3},{8,12},{9,13},{10,... | collective-permute-start | bytes 1769480 | tf_op jit(solution)/shard_map/ppermute | solution.py:738
  112.8 19.2 %collective-permute-start.14 = (bf16[192,3072]{1,0:T(8,128)(2,1)S(1)}, bf16[192,3072]{1,0:T(8,128)(2,1)S(1)}, u32[]{:S(2)}, u32[]{:S(2)}) collective-permute-start(bf16[192,3072]{1,0:T(8,128)(2,1)S(1)} %add_convert_fusion.1), channel_id=1, source_target_pairs={{0,1},{1,0},{2,3},{3,2},{4,5},{5,4},{6,7},{7,6},{8,9},{9,8},{10,11... | collective-permute-start | bytes 3538952 | tf_op jit(solution)/shard_map/ppermute | solution.py:738
  127.6 11.7 %collective-permute-start.16 = (bf16[192,1536]{1,0:T(8,128)(2,1)S(1)}, bf16[192,1536]{1,0:T(8,128)(2,1)S(1)}, u32[]{:S(2)}, u32[]{:S(2)}) collective-permute-start(bf16[192,1536]{1,0:T(8,128)(2,1)S(1)} %get-tuple-element.202), channel_id=1, source_target_pairs={{0,16},{1,17},{2,18},{3,19},{4,20},{5,21},{6,22},{7,23},{8,24},{9,... | collective-permute-start | bytes 1769480 | tf_op jit(solution)/shard_map/ppermute | solution.py:738
  128.0 10.1 %collective-permute-start.15 = (bf16[192,1536]{1,0:T(8,128)(2,1)S(1)}, bf16[192,1536]{1,0:T(8,128)(2,1)S(1)}, u32[]{:S(2)}, u32[]{:S(2)}) collective-permute-start(bf16[192,1536]{1,0:T(8,128)(2,1)S(1)} %get-tuple-element.204), channel_id=1, source_target_pairs={{0,16},{1,17},{2,18},{3,19},{4,20},{5,21},{6,22},{7,23},{8,24},{9,... | collective-permute-start | bytes 1769480 | tf_op jit(solution)/shard_map/ppermute | solution.py:738
  128.4 17.4 %collective-permute-start.18 = (bf16[384,768]{1,0:T(8,128)(2,1)S(1)}, bf16[384,768]{1,0:T(8,128)(2,1)S(1)}, u32[]{:S(2)}, u32[]{:S(2)}) collective-permute-start(bf16[384,768]{1,0:T(8,128)(2,1)S(1)} %add_convert_fusion.14), channel_id=1, source_target_pairs={{0,8},{1,9},{2,10},{3,11},{4,12},{5,13},{6,14},{7,15},{8,0},{9,1},... | collective-permute-start | bytes 1769480 | tf_op jit(solution)/shard_map/ppermute | solution.py:738
  132.3 10.8 %collective-permute-start.17 = (bf16[96,3072]{1,0:T(8,128)(2,1)S(1)}, bf16[96,3072]{1,0:T(8,128)(2,1)S(1)}, u32[]{:S(2)}, u32[]{:S(2)}) collective-permute-start(bf16[96,3072]{1,0:T(8,128)(2,1)S(1)} %get-tuple-element.287), channel_id=1, source_target_pairs={{0,2},{1,3},{2,0},{3,1},{4,6},{5,7},{6,4},{7,5},{8,10},{9,11},{10,... | collective-permute-start | bytes 1769480 | tf_op jit(solution)/shard_map/ppermute | solution.py:738
  138.0 9.6 %collective-permute-start.20 = (bf16[192,1664]{1,0:T(8,128)(2,1)S(1)}, bf16[192,1664]{1,0:T(8,128)(2,1)S(1)}, u32[]{:S(2)}, u32[]{:S(2)}) collective-permute-start(bf16[192,1664]{1,0:T(8,128)(2,1)S(1)} %get-tuple-element.214), channel_id=1, source_target_pairs={{0,16},{1,17},{2,18},{3,19},{4,20},{5,21},{6,22},{7,23},{8,24},{9,... | collective-permute-start | bytes 1916936 | tf_op jit(solution)/shard_map/ppermute | solution.py:738
  138.3 10.7 %collective-permute-start.21 = (bf16[192,1536]{1,0:T(8,128)(2,1)S(1)}, bf16[192,1536]{1,0:T(8,128)(2,1)S(1)}, u32[]{:S(2)}, u32[]{:S(2)}) collective-permute-start(bf16[192,1536]{1,0:T(8,128)(2,1)S(1)} %add_convert_fusion.11), channel_id=1, source_target_pairs={{0,1},{1,0},{2,3},{3,2},{4,5},{5,4},{6,7},{7,6},{8,9},{9,8},{10,11... | collective-permute-start | bytes 1769480 | tf_op jit(solution)/shard_map/ppermute | solution.py:738
  139.4 7.1 %collective-permute-start.19 = (bf16[192,1664]{1,0:T(8,128)(2,1)S(1)}, bf16[192,1664]{1,0:T(8,128)(2,1)S(1)}, u32[]{:S(2)}, u32[]{:S(2)}) collective-permute-start(bf16[192,1664]{1,0:T(8,128)(2,1)S(1)} %get-tuple-element.218), channel_id=1, source_target_pairs={{0,16},{1,17},{2,18},{3,19},{4,20},{5,21},{6,22},{7,23},{8,24},{9,... | collective-permute-start | bytes 1916936 | tf_op jit(solution)/shard_map/ppermute | solution.py:738
  143.2 15.7 %collective-permute-start.22 = (bf16[96,3072]{1,0:T(8,128)(2,1)S(1)}, bf16[96,3072]{1,0:T(8,128)(2,1)S(1)}, u32[]{:S(2)}, u32[]{:S(2)}) collective-permute-start(bf16[96,3072]{1,0:T(8,128)(2,1)S(1)} %add_convert_fusion.9), channel_id=1, source_target_pairs={{0,4},{1,5},{2,6},{3,7},{4,0},{5,1},{6,2},{7,3},{8,12},{9,13},{10,... | collective-permute-start | bytes 1769480 | tf_op jit(solution)/shard_map/ppermute | solution.py:738
  146.0 15.8 %collective-permute-start.23 = (bf16[384,768]{1,0:T(8,128)(2,1)S(1)}, bf16[384,768]{1,0:T(8,128)(2,1)S(1)}, u32[]{:S(2)}, u32[]{:S(2)}) collective-permute-start(bf16[384,768]{1,0:T(8,128)(2,1)S(1)} %add_convert_fusion.8), channel_id=1, source_target_pairs={{0,2},{1,3},{2,0},{3,1},{4,6},{5,7},{6,4},{7,5},{8,10},{9,11},{10,... | collective-permute-start | bytes 1769480 | tf_op jit(solution)/shard_map/ppermute | solution.py:738
  146.7 24.1 %collective-permute-start.25 = (bf16[192,1664]{1,0:T(8,128)(2,1)S(1)}, bf16[192,1664]{1,0:T(8,128)(2,1)S(1)}, u32[]{:S(2)}, u32[]{:S(2)}) collective-permute-start(bf16[192,1664]{1,0:T(8,128)(2,1)S(1)} %add_convert_fusion.5), channel_id=1, source_target_pairs={{0,1},{1,0},{2,3},{3,2},{4,5},{5,4},{6,7},{7,6},{8,9},{9,8},{10,11... | collective-permute-start | bytes 1916936 | tf_op jit(solution)/shard_map/ppermute | solution.py:738
  149.1 21.3 %collective-permute-start.24 = (bf16[96,1536]{1,0:T(8,128)(2,1)S(1)}, bf16[96,1536]{1,0:T(8,128)(2,1)S(1)}, u32[]{:S(2)}, u32[]{:S(2)}) collective-permute-start(bf16[96,1536]{1,0:T(8,128)(2,1)S(1)} %get-tuple-element.293), channel_id=1, source_target_pairs={{0,2},{1,3},{2,0},{3,1},{4,6},{5,7},{6,4},{7,5},{8,10},{9,11},{10,... | collective-permute-start | bytes 884744 | tf_op jit(solution)/shard_map/ppermute | solution.py:738
  159.1 22.5 %collective-permute-start.26 = (bf16[96,3072]{1,0:T(8,128)(2,1)S(1)}, bf16[96,3072]{1,0:T(8,128)(2,1)S(1)}, u32[]{:S(2)}, u32[]{:S(2)}) collective-permute-start(bf16[96,3072]{1,0:T(8,128)(2,1)S(1)} %add_convert_fusion.7), channel_id=1, source_target_pairs={{0,8},{1,9},{2,10},{3,11},{4,12},{5,13},{6,14},{7,15},{8,0},{9,1},... | collective-permute-start | bytes 1769480 | tf_op jit(solution)/shard_map/ppermute | solution.py:738
  161.8 21.8 %collective-permute-start.27 = (bf16[768,768]{1,0:T(8,128)(2,1)S(1)}, bf16[768,768]{1,0:T(8,128)(2,1)S(1)}, u32[]{:S(2)}, u32[]{:S(2)}) collective-permute-start(bf16[768,768]{1,0:T(8,128)(2,1)S(1)} %constant_dynamic-update-slice_fusion.9.refs_0_), channel_id=1, source_target_pairs={{0,1},{1,0},{2,3},{3,2},{4,5},{5,4},{6,7},{7,6},{8,9},{9,8},{10,11... | collective-permute-start | bytes 3538952 | tf_op jit(solution)/shard_map/ppermute | solution.py:738
  170.5 13.2 %collective-permute-start.28 = (bf16[96,1536]{1,0:T(8,128)(2,1)S(1)}, bf16[96,1536]{1,0:T(8,128)(2,1)S(1)}, u32[]{:S(2)}, u32[]{:S(2)}) collective-permute-start(bf16[96,1536]{1,0:T(8,128)(2,1)S(1)} %add_convert_fusion.25), channel_id=1, source_target_pairs={{0,4},{1,5},{2,6},{3,7},{4,0},{5,1},{6,2},{7,3},{8,12},{9,13},{10,... | collective-permute-start | bytes 884744 | tf_op jit(solution)/shard_map/ppermute | solution.py:738
  171.0 12.7 %collective-permute-start.29 = (bf16[96,1664]{1,0:T(8,128)(2,1)S(1)}, bf16[96,1664]{1,0:T(8,128)(2,1)S(1)}, u32[]{:S(2)}, u32[]{:S(2)}) collective-permute-start(bf16[96,1664]{1,0:T(8,128)(2,1)S(1)} %get-tuple-element.291), channel_id=1, source_target_pairs={{0,2},{1,3},{2,0},{3,1},{4,6},{5,7},{6,4},{7,5},{8,10},{9,11},{10,... | collective-permute-start | bytes 958472 | tf_op jit(solution)/shard_map/ppermute | solution.py:738
  181.8 11.0 %collective-permute-start.30 = (bf16[96,3072]{1,0:T(8,128)(2,1)S(1)}, bf16[96,3072]{1,0:T(8,128)(2,1)S(1)}, u32[]{:S(2)}, u32[]{:S(2)}) collective-permute-start(bf16[96,3072]{1,0:T(8,128)(2,1)S(1)} %add_convert_fusion.6), channel_id=1, source_target_pairs={{0,2},{1,3},{2,0},{3,1},{4,6},{5,7},{6,4},{7,5},{8,10},{9,11},{10,... | collective-permute-start | bytes 1769480 | tf_op jit(solution)/shard_map/ppermute | solution.py:738
  181.9 22.1 %collective-permute-start.34 = (bf16[768,768]{1,0:T(8,128)(2,1)S(1)}, bf16[768,768]{1,0:T(8,128)(2,1)S(1)}, u32[]{:S(2)}, u32[]{:S(2)}) collective-permute-start(bf16[768,768]{1,0:T(8,128)(2,1)S(1)} %constant_dynamic-update-slice_fusion.9.refs_0_), channel_id=1, source_target_pairs={{0,16},{1,17},{2,18},{3,19},{4,20},{5,21},{6,22},{7,23},{8,24},{9,... | collective-permute-start | bytes 3538952 | tf_op jit(solution)/shard_map/ppermute | solution.py:738
  183.8 12.5 %collective-permute-start.31 = (bf16[96,1664]{1,0:T(8,128)(2,1)S(1)}, bf16[96,1664]{1,0:T(8,128)(2,1)S(1)}, u32[]{:S(2)}, u32[]{:S(2)}) collective-permute-start(bf16[96,1664]{1,0:T(8,128)(2,1)S(1)} %add_convert_fusion.20), channel_id=1, source_target_pairs={{0,4},{1,5},{2,6},{3,7},{4,0},{5,1},{6,2},{7,3},{8,12},{9,13},{10,... | collective-permute-start | bytes 958472 | tf_op jit(solution)/shard_map/ppermute | solution.py:738
  184.5 19.5 %collective-permute-start.35 = (bf16[768,768]{1,0:T(8,128)(2,1)S(1)}, bf16[768,768]{1,0:T(8,128)(2,1)S(1)}, u32[]{:S(2)}, u32[]{:S(2)}) collective-permute-start(bf16[768,768]{1,0:T(8,128)(2,1)S(1)} %collective-permute-done.27.refs_1_), channel_id=1, source_target_pairs={{0,16},{1,17},{2,18},{3,19},{4,20},{5,21},{6,22},{7,23},{8,24},{9,... | collective-permute-start | bytes 3538952 | tf_op jit(solution)/shard_map/ppermute | solution.py:738
  192.9 19.4 %collective-permute-start.36 = (bf16[192,3072]{1,0:T(8,128)(2,1)S(1)}, bf16[192,3072]{1,0:T(8,128)(2,1)S(1)}, u32[]{:S(2)}, u32[]{:S(2)}) collective-permute-start(bf16[192,3072]{1,0:T(8,128)(2,1)S(1)} %constant_dynamic-update-slice_fusion.11.refs_0_), channel_id=1, source_target_pairs={{0,1},{1,0},{2,3},{3,2},{4,5},{5,4},{6,7},{7,6},{8,9},{9,8},{10,11... | collective-permute-start | bytes 3538952 | tf_op jit(solution)/shard_map/ppermute | solution.py:738
  193.0 10.8 %collective-permute-start.32 = (bf16[96,1536]{1,0:T(8,128)(2,1)S(1)}, bf16[96,1536]{1,0:T(8,128)(2,1)S(1)}, u32[]{:S(2)}, u32[]{:S(2)}) collective-permute-start(bf16[96,1536]{1,0:T(8,128)(2,1)S(1)} %add_convert_fusion.24), channel_id=1, source_target_pairs={{0,8},{1,9},{2,10},{3,11},{4,12},{5,13},{6,14},{7,15},{8,0},{9,1},... | collective-permute-start | bytes 884744 | tf_op jit(solution)/shard_map/ppermute | solution.py:738
  196.4 15.9 %collective-permute-start.33 = (bf16[96,1664]{1,0:T(8,128)(2,1)S(1)}, bf16[96,1664]{1,0:T(8,128)(2,1)S(1)}, u32[]{:S(2)}, u32[]{:S(2)}) collective-permute-start(bf16[96,1664]{1,0:T(8,128)(2,1)S(1)} %add_convert_fusion.19), channel_id=1, source_target_pairs={{0,8},{1,9},{2,10},{3,11},{4,12},{5,13},{6,14},{7,15},{8,0},{9,1},... | collective-permute-start | bytes 958472 | tf_op jit(solution)/shard_map/ppermute | solution.py:738
  203.9 8.6 %collective-permute-start.37 = (bf16[96,1536]{1,0:T(8,128)(2,1)S(1)}, bf16[96,1536]{1,0:T(8,128)(2,1)S(1)}, u32[]{:S(2)}, u32[]{:S(2)}) collective-permute-start(bf16[96,1536]{1,0:T(8,128)(2,1)S(1)} %add_convert_fusion.23), channel_id=1, source_target_pairs={{0,2},{1,3},{2,0},{3,1},{4,6},{5,7},{6,4},{7,5},{8,10},{9,11},{10,... | collective-permute-start | bytes 884744 | tf_op jit(solution)/shard_map/ppermute | solution.py:738
  207.2 18.3 %collective-permute-start.39 = (bf16[192,3072]{1,0:T(8,128)(2,1)S(1)}, bf16[192,3072]{1,0:T(8,128)(2,1)S(1)}, u32[]{:S(2)}, u32[]{:S(2)}) collective-permute-start(bf16[192,3072]{1,0:T(8,128)(2,1)S(1)} %constant_dynamic-update-slice_fusion.11.refs_0_), channel_id=1, source_target_pairs={{0,16},{1,17},{2,18},{3,19},{4,20},{5,21},{6,22},{7,23},{8,24},{9,... | collective-permute-start | bytes 3538952 | tf_op jit(solution)/shard_map/ppermute | solution.py:738
  212.3 13.1 %collective-permute-start.40 = (bf16[192,3072]{1,0:T(8,128)(2,1)S(1)}, bf16[192,3072]{1,0:T(8,128)(2,1)S(1)}, u32[]{:S(2)}, u32[]{:S(2)}) collective-permute-start(bf16[192,3072]{1,0:T(8,128)(2,1)S(1)} %collective-permute-done.36.refs_1_), channel_id=1, source_target_pairs={{0,16},{1,17},{2,18},{3,19},{4,20},{5,21},{6,22},{7,23},{8,24},{9,... | collective-permute-start | bytes 3538952 | tf_op jit(solution)/shard_map/ppermute | solution.py:738
  212.4 10.5 %collective-permute-start.38 = (bf16[96,1664]{1,0:T(8,128)(2,1)S(1)}, bf16[96,1664]{1,0:T(8,128)(2,1)S(1)}, u32[]{:S(2)}, u32[]{:S(2)}) collective-permute-start(bf16[96,1664]{1,0:T(8,128)(2,1)S(1)} %add_convert_fusion.18), channel_id=1, source_target_pairs={{0,2},{1,3},{2,0},{3,1},{4,6},{5,7},{6,4},{7,5},{8,10},{9,11},{10,... | collective-permute-start | bytes 958472 | tf_op jit(solution)/shard_map/ppermute | solution.py:738
  212.6 12.8 %collective-permute-start.42 = (bf16[192,1536]{1,0:T(8,128)(2,1)S(1)}, bf16[192,1536]{1,0:T(8,128)(2,1)S(1)}, u32[]{:S(2)}, u32[]{:S(2)}) collective-permute-start(bf16[192,1536]{1,0:T(8,128)(2,1)S(1)} %constant_dynamic-update-slice_fusion.13.refs_0_), channel_id=1, source_target_pairs={{0,1},{1,0},{2,3},{3,2},{4,5},{5,4},{6,7},{7,6},{8,9},{9,8},{10,11... | collective-permute-start | bytes 1769480 | tf_op jit(solution)/shard_map/ppermute | solution.py:738
  222.9 10.5 %collective-permute-start.45 = (bf16[192,1664]{1,0:T(8,128)(2,1)S(1)}, bf16[192,1664]{1,0:T(8,128)(2,1)S(1)}, u32[]{:S(2)}, u32[]{:S(2)}) collective-permute-start(bf16[192,1664]{1,0:T(8,128)(2,1)S(1)} %constant_dynamic-update-slice_fusion.15.refs_0_), channel_id=1, source_target_pairs={{0,1},{1,0},{2,3},{3,2},{4,5},{5,4},{6,7},{7,6},{8,9},{9,8},{10,11... | collective-permute-start | bytes 1916936 | tf_op jit(solution)/shard_map/ppermute | solution.py:738
  225.3 10.6 %collective-permute-start.43 = (bf16[192,1536]{1,0:T(8,128)(2,1)S(1)}, bf16[192,1536]{1,0:T(8,128)(2,1)S(1)}, u32[]{:S(2)}, u32[]{:S(2)}) collective-permute-start(bf16[192,1536]{1,0:T(8,128)(2,1)S(1)} %collective-permute-done.42.refs_1_), channel_id=1, source_target_pairs={{0,16},{1,17},{2,18},{3,19},{4,20},{5,21},{6,22},{7,23},{8,24},{9,... | collective-permute-start | bytes 1769480 | tf_op jit(solution)/shard_map/ppermute | solution.py:738
  228.6 7.3 %collective-permute-start.41 = (bf16[192,1536]{1,0:T(8,128)(2,1)S(1)}, bf16[192,1536]{1,0:T(8,128)(2,1)S(1)}, u32[]{:S(2)}, u32[]{:S(2)}) collective-permute-start(bf16[192,1536]{1,0:T(8,128)(2,1)S(1)} %constant_dynamic-update-slice_fusion.13.refs_0_), channel_id=1, source_target_pairs={{0,16},{1,17},{2,18},{3,19},{4,20},{5,21},{6,22},{7,23},{8,24},{9,... | collective-permute-start | bytes 1769480 | tf_op jit(solution)/shard_map/ppermute | solution.py:738
  233.4 8.7 %collective-permute-start.46 = (bf16[192,1664]{1,0:T(8,128)(2,1)S(1)}, bf16[192,1664]{1,0:T(8,128)(2,1)S(1)}, u32[]{:S(2)}, u32[]{:S(2)}) collective-permute-start(bf16[192,1664]{1,0:T(8,128)(2,1)S(1)} %collective-permute-done.45.refs_1_), channel_id=1, source_target_pairs={{0,16},{1,17},{2,18},{3,19},{4,20},{5,21},{6,22},{7,23},{8,24},{9,... | collective-permute-start | bytes 1916936 | tf_op jit(solution)/shard_map/ppermute | solution.py:738
  238.4 3.7 %collective-permute-start.44 = (bf16[192,1664]{1,0:T(8,128)(2,1)S(1)}, bf16[192,1664]{1,0:T(8,128)(2,1)S(1)}, u32[]{:S(2)}, u32[]{:S(2)}) collective-permute-start(bf16[192,1664]{1,0:T(8,128)(2,1)S(1)} %constant_dynamic-update-slice_fusion.15.refs_0_), channel_id=1, source_target_pairs={{0,16},{1,17},{2,18},{3,19},{4,20},{5,21},{6,22},{7,23},{8,24},{9,... | collective-permute-start | bytes 1916936 | tf_op jit(solution)/shard_map/ppermute | solution.py:738
  (6 other events, 14.0 us)
